TPU v7x, 256 devices: a whole 4x4x8 slice. The times are simulated.
256 devices in a mesh: segment: 16 (over y, z_hi), band: 16 (over z_lo, x, core).
Axes of the slice: x: 4, y: 4, z: 8 (z_hi: 4, z_lo: 2; z = z_hi * 2 + z_lo), core: 2. Of those that a mesh axis runs over, the one named last changes fastest.
Arguments:
- forward_state: bfloat16 [16, 2, 128, 64, 256], P('segment', None, 'band'), may hold values from -6 to 6
- returning_state: bfloat16 [16, 2, 128, 64, 256], P('segment', None, 'band'), may hold values from -6 to 6
- returning_grad: bfloat16 [16, 2, 128, 64, 256], P('segment', None, 'band'), may hold values from -6 to 6
- weights: bfloat16 [16, 2, 2304, 256], P('segment'), may hold values from -0.125 to 0.125
- fresh_input: bfloat16 [2, 2, 128, 64, 256], P(None, None, 'band'), may hold values from -6 to 6
- loss_grad: bfloat16 [2, 2, 128, 64, 256], P(None, None, 'band'), may hold values from -6 to 6
Outputs:
- forward_out: bfloat16 [16, 2, 128, 64, 256], P('segment', None, 'band')
- returning_out: bfloat16 [16, 2, 128, 64, 256], P('segment', None, 'band')
- backward_out: bfloat16 [16, 2, 128, 64, 256], P('segment', None, 'band')
- weight_grad: float32 [16, 2, 2304, 256], P('segment', None, 'band')
All inputs are finite; a program needn't handle non-finite values.
Results may differ from a plain program's by a relative error of at most 0.02.
Values may be sent and summed in bfloat16 or wider, within the bound.
No kernel may reach another device: no remote copies, remote signals or barrier semaphores. Data moves between devices by JAX's collectives and lax.ppermute only.
A program may use at most 64 MiB of HBM per device.

v0:
```python
import jax
import jax.numpy as jnp
from jax import lax
from jax.sharding import PartitionSpec as P


def with_halo(value, sides, width):
    for axis, dim in sides:
        count, length = (lax.axis_size(axis), value.shape[dim])
        up = [(i, (i + 1) % count) for i in range(count - 1)]
        down = [(j, i) for i, j in up]
        last = lax.slice_in_dim(value, length - width, length, axis=dim)
        initial = lax.slice_in_dim(value, 0, width, axis=dim)
        before = lax.ppermute(last, axis, up)
        after = lax.ppermute(initial, axis, down)
        value = jnp.concatenate([before, value, after], axis=dim)
    return value


def from_behind(block, axis, distance):
    devices = range(lax.axis_size(axis))
    route = [(i - distance, i) for i in devices if i - distance in devices]
    return lax.ppermute(block, axis, route)


def activate(values):
    return jax.nn.silu(values.astype(jnp.float32)).astype(jnp.bfloat16)


def silu_slope(values):
    sigmoid = jax.nn.sigmoid(values)
    return sigmoid * (1.0 + values * (1.0 - sigmoid))


def gather_taps(rowpadded, flipped):
    height = rowpadded.shape[0] - 2
    across = rowpadded.shape[1]
    padded = jnp.pad(rowpadded, ((0, 0), (1, 1), (0, 0)))
    pieces = []
    for first in range(3):
        for second in range(3):
            if flipped:
                row_start, col_start = (2 - first, 2 - second)
            else:
                row_start, col_start = (first, second)
            pieces.append(padded[row_start : row_start + height, col_start : col_start + across, :])
    return jnp.concatenate(pieces, -1).reshape(height * across, -1)


def apply_taps(taps_matrix, weight):
    return jnp.dot(taps_matrix, weight, preferred_element_type=jnp.float32)


def flip_weight(weight, channels):
    return weight.reshape(9, channels, channels).transpose(0, 2, 1).reshape(9 * channels, channels)


def correlate(taps_matrix, grads):
    return lax.dot_general(
        taps_matrix, grads, (((0,), (0,)), ((), ())), preferred_element_type=jnp.float32
    )


def advance_exchange(state, weight_f, weight_g):
    first_in, second_in = (state[0], state[1])
    shape = first_in.shape
    rim_f = with_halo(activate(second_in), (("band", 0),), 1)
    first_out = (
        first_in.astype(jnp.float32)
        + apply_taps(gather_taps(rim_f, False), weight_f).reshape(shape)
    ).astype(jnp.bfloat16)
    rim_g = with_halo(activate(first_out), (("band", 0),), 1)
    second_out = (
        second_in.astype(jnp.float32)
        + apply_taps(gather_taps(rim_g, False), weight_g).reshape(shape)
    ).astype(jnp.bfloat16)
    return jnp.stack([first_out, second_out])


def invert_exchange(outputs, grads, weight_f, weight_g, flipped_f, flipped_g):
    first_out, second_out = (outputs[0], outputs[1])
    first_grad, second_grad = (grads[0], grads[1])
    shape = first_out.shape
    channels = shape[2]
    act_rim, grad_rim = (
        with_halo(activate(first_out), (("band", 0),), 1),
        with_halo(second_grad, (("band", 0),), 1),
    )
    taps_g = gather_taps(act_rim, False)
    second_in = (
        second_out.astype(jnp.float32) - apply_taps(taps_g, weight_g).reshape(shape)
    ).astype(jnp.bfloat16)
    back_g = apply_taps(gather_taps(grad_rim, True), flipped_g).reshape(shape)
    first_back = (
        first_grad.astype(jnp.float32) + silu_slope(first_out.astype(jnp.float32)) * back_g
    ).astype(jnp.bfloat16)
    act_rim_f, back_rim = (
        with_halo(activate(second_in), (("band", 0),), 1),
        with_halo(first_back, (("band", 0),), 1),
    )
    taps_f = gather_taps(act_rim_f, False)
    first_in = (first_out.astype(jnp.float32) - apply_taps(taps_f, weight_f).reshape(shape)).astype(
        jnp.bfloat16
    )
    back_f = apply_taps(gather_taps(back_rim, True), flipped_f).reshape(shape)
    second_back = (
        second_grad.astype(jnp.float32) + silu_slope(second_in.astype(jnp.float32)) * back_f
    ).astype(jnp.bfloat16)
    wgrad = jnp.stack(
        [
            correlate(taps_f, first_back.reshape(-1, channels)),
            correlate(taps_g, second_grad.reshape(-1, channels)),
        ]
    )
    return (jnp.stack([first_in, second_in]), jnp.stack([first_back, second_back]), wgrad)


def local(forward_state, returning_state, returning_grad, weights, fresh_input, loss_grad):
    segment_index = lax.axis_index("segment")
    last_segment = lax.axis_size("segment") - 1
    weight_f = weights[0, 0]
    weight_g = weights[0, 1]
    channels = weight_f.shape[1]
    flipped_f = flip_weight(weight_f, channels)
    flipped_g = flip_weight(weight_g, channels)
    state = forward_state[0]
    outputs = returning_state[0]
    grads = returning_grad[0]
    totals = jnp.zeros((2, 9 * channels // lax.axis_size("band"), channels), jnp.float32)
    for tick_index in range(fresh_input.shape[0]):
        advanced = advance_exchange(state, weight_f, weight_g)
        inverted, backed, wgrad = invert_exchange(
            outputs, grads, weight_f, weight_g, flipped_f, flipped_g
        )
        totals = totals + lax.psum_scatter(
            wgrad.astype(jnp.bfloat16), "band", scatter_dimension=1, tiled=True
        ).astype(jnp.float32)
        sent = from_behind(advanced, "segment", 1)
        state = jnp.where(segment_index == 0, fresh_input[tick_index], sent)
        came_state, came_grad = from_behind((inverted, backed), "segment", -1)
        at_end = segment_index == last_segment
        outputs = jnp.where(at_end, advanced, came_state)
        grads = jnp.where(at_end, loss_grad[tick_index], came_grad)
    return (state[None], outputs[None], grads[None], totals[None])


def solution(mesh):
    return jax.shard_map(
        local,
        mesh=mesh,
        in_specs=(
            P("segment", None, "band", None, None),
            P("segment", None, "band", None, None),
            P("segment", None, "band", None, None),
            P("segment", None, None, None),
            P(None, None, "band", None, None),
            P(None, None, "band", None, None),
        ),
        out_specs=(
            P("segment", None, "band", None, None),
            P("segment", None, "band", None, None),
            P("segment", None, "band", None, None),
            P("segment", None, "band", None),
        ),
        check_vma=False,
    )
```

profile of v0, /device:TPU:18, one launch (start us, length us, event | category | flops | bytes accessed | tf_op | source)
XLA Modules:
  0.0 276.8 jit_solution(6464817049620438630)
XLA Ops:
  9.9 3.6 %collective-permute-start.21 = (bf16[1,64,256]{2,1,0:T(8,128)(2,1)S(1)}, bf16[1,64,256]{2,1,0:T(8,128)(2,1)S(1)}, u32[]{:S(2)}, u32[]{:S(2)}) collective-permute-start(bf16[1,64,256]{2,1,0:T(8,128)(2,1)S(1)} %get-tuple-element.15), channel_id=1, source_target_pairs={{1,0},{2,1},{3,2},{4,3},{5,4},{6,5},{7,6},{8,7},{9,8},{10,9},{11,1... | collective-permute-start | bytes 98312 | tf_op jit(solution)/shard_map/ppermute | solution.py:15
  16.6 3.6 %collective-permute-start.1 = (bf16[1,64,256]{2,1,0:T(8,128)(2,1)S(1)}, bf16[1,64,256]{2,1,0:T(8,128)(2,1)S(1)}, u32[]{:S(2)}, u32[]{:S(2)}) collective-permute-start(bf16[1,64,256]{2,1,0:T(8,128)(2,1)S(1)} %get-tuple-element.39), channel_id=1, source_target_pairs={{1,0},{2,1},{3,2},{4,3},{5,4},{6,5},{7,6},{8,7},{9,8},{10,9},{11,1... | collective-permute-start | bytes 98312 | tf_op jit(solution)/shard_map/ppermute | solution.py:15
  29.7 3.6 %collective-permute-start.11 = (bf16[1,64,256]{2,1,0:T(8,128)(2,1)S(1)}, bf16[1,64,256]{2,1,0:T(8,128)(2,1)S(1)}, u32[]{:S(2)}, u32[]{:S(2)}) collective-permute-start(bf16[1,64,256]{2,1,0:T(8,128)(2,1)S(1)} %get-tuple-element.31), channel_id=1, source_target_pairs={{1,0},{2,1},{3,2},{4,3},{5,4},{6,5},{7,6},{8,7},{9,8},{10,9},{11,1... | collective-permute-start | bytes 98312 | tf_op jit(solution)/shard_map/ppermute | solution.py:15
  38.7 3.6 %collective-permute-start.3 = (bf16[1,64,256]{2,1,0:T(8,128)(2,1)S(1)}, bf16[1,64,256]{2,1,0:T(8,128)(2,1)S(1)}, u32[]{:S(2)}, u32[]{:S(2)}) collective-permute-start(bf16[1,64,256]{2,1,0:T(8,128)(2,1)S(1)} %get-tuple-element.37), channel_id=1, source_target_pairs={{1,0},{2,1},{3,2},{4,3},{5,4},{6,5},{7,6},{8,7},{9,8},{10,9},{11,1... | collective-permute-start | bytes 98312 | tf_op jit(solution)/shard_map/ppermute | solution.py:15
  45.8 3.6 %collective-permute-start.13 = (bf16[1,64,256]{2,1,0:T(8,128)(2,1)S(1)}, bf16[1,64,256]{2,1,0:T(8,128)(2,1)S(1)}, u32[]{:S(2)}, u32[]{:S(2)}) collective-permute-start(bf16[1,64,256]{2,1,0:T(8,128)(2,1)S(1)} %get-tuple-element.29), channel_id=1, source_target_pairs={{1,0},{2,1},{3,2},{4,3},{5,4},{6,5},{7,6},{8,7},{9,8},{10,9},{11,1... | collective-permute-start | bytes 98312 | tf_op jit(solution)/shard_map/ppermute | solution.py:15
  53.1 3.6 %collective-permute-start.23 = (bf16[1,64,256]{2,1,0:T(8,128)(2,1)S(1)}, bf16[1,64,256]{2,1,0:T(8,128)(2,1)S(1)}, u32[]{:S(2)}, u32[]{:S(2)}) collective-permute-start(bf16[1,64,256]{2,1,0:T(8,128)(2,1)S(1)} %get-tuple-element.23), channel_id=1, source_target_pairs={{1,0},{2,1},{3,2},{4,3},{5,4},{6,5},{7,6},{8,7},{9,8},{10,9},{11,1... | collective-permute-start | bytes 98312 | tf_op jit(solution)/shard_map/ppermute | solution.py:15
  61.1 8.1 %collective-permute-start.14 = (bf16[2,8,64,256]{3,2,1,0:T(8,128)(2,1)}, bf16[2,8,64,256]{3,2,1,0:T(8,128)(2,1)}, u32[]{:S(2)}, u32[]{:S(2)}) collective-permute-start(bf16[2,8,64,256]{3,2,1,0:T(8,128)(2,1)} %pad_maximum_fusion.4), channel_id=1, source_target_pairs={{16,0},{32,16},{48,32},{64,48},{80,64},{96,80},{112,96},{128,112},... | collective-permute-start | bytes 1572872 | tf_op jit(solution)/shard_map/ppermute | solution.py:23
  73.4 3.5 %collective-permute-start.24 = (bf16[2,8,64,256]{3,2,1,0:T(8,128)(2,1)S(1)}, bf16[2,8,64,256]{3,2,1,0:T(8,128)(2,1)S(1)}, u32[]{:S(2)}, u32[]{:S(2)}) collective-permute-start(bf16[2,8,64,256]{3,2,1,0:T(8,128)(2,1)S(1)} %pad_maximum_fusion.6), channel_id=1, source_target_pairs={{16,0},{32,16},{48,32},{64,48},{80,64},{96,80},{112,96},{128,112},... | collective-permute-start | bytes 1572872 | tf_op jit(solution)/shard_map/ppermute | solution.py:23
  77.9 4.1 %collective-permute-done.14 = bf16[2,8,64,256]{3,2,1,0:T(8,128)(2,1)} collective-permute-done((bf16[2,8,64,256]{3,2,1,0:T(8,128)(2,1)}, bf16[2,8,64,256]{3,2,1,0:T(8,128)(2,1)}, u32[]{:S(2)}, u32[]{:S(2)}) %collective-permute-start.14) | collective-permute-done | bytes 524320 | tf_op jit(solution)/shard_map/ppermute | solution.py:23
  86.0 3.6 %collective-permute-start.16 = (bf16[1,64,256]{2,1,0:T(8,128)(2,1)S(1)}, bf16[1,64,256]{2,1,0:T(8,128)(2,1)S(1)}, u32[]{:S(2)}, u32[]{:S(2)}) collective-permute-start(bf16[1,64,256]{2,1,0:T(8,128)(2,1)S(1)} %get-tuple-element.27), channel_id=1, source_target_pairs={{1,0},{2,1},{3,2},{4,3},{5,4},{6,5},{7,6},{8,7},{9,8},{10,9},{11,1... | collective-permute-start | bytes 98312 | tf_op jit(solution)/shard_map/ppermute | solution.py:15
  89.7 24.7 %collective-permute-done.24 = bf16[2,8,64,256]{3,2,1,0:T(8,128)(2,1)S(1)} collective-permute-done((bf16[2,8,64,256]{3,2,1,0:T(8,128)(2,1)S(1)}, bf16[2,8,64,256]{3,2,1,0:T(8,128)(2,1)S(1)}, u32[]{:S(2)}, u32[]{:S(2)}) %collective-permute-start.24) | collective-permute-done | bytes 524320 | tf_op jit(solution)/shard_map/ppermute | solution.py:23
  118.3 3.6 %collective-permute-start.26 = (bf16[1,64,256]{2,1,0:T(8,128)(2,1)S(1)}, bf16[1,64,256]{2,1,0:T(8,128)(2,1)S(1)}, u32[]{:S(2)}, u32[]{:S(2)}) collective-permute-start(bf16[1,64,256]{2,1,0:T(8,128)(2,1)S(1)} %get-tuple-element.13), channel_id=1, source_target_pairs={{1,0},{2,1},{3,2},{4,3},{5,4},{6,5},{7,6},{8,7},{9,8},{10,9},{11,1... | collective-permute-start | bytes 98312 | tf_op jit(solution)/shard_map/ppermute | solution.py:15
  123.5 4.4 %collective-permute-start.17 = (bf16[1,64,256]{2,1,0:T(8,128)(2,1)S(1)}, bf16[1,64,256]{2,1,0:T(8,128)(2,1)S(1)}, u32[]{:S(2)}, u32[]{:S(2)}) collective-permute-start(bf16[1,64,256]{2,1,0:T(8,128)(2,1)S(1)} %get-tuple-element.24), channel_id=1, source_target_pairs={{0,1},{1,2},{2,3},{3,4},{4,5},{5,6},{6,7},{7,8},{8,9},{9,10},{10,1... | collective-permute-start | bytes 98312 | tf_op jit(solution)/shard_map/ppermute | solution.py:14
  132.1 3.6 %collective-permute-start.27 = (bf16[1,64,256]{2,1,0:T(8,128)(2,1)S(1)}, bf16[1,64,256]{2,1,0:T(8,128)(2,1)S(1)}, u32[]{:S(2)}, u32[]{:S(2)}) collective-permute-start(bf16[1,64,256]{2,1,0:T(8,128)(2,1)S(1)} %get-tuple-element.20), channel_id=1, source_target_pairs={{0,1},{1,2},{2,3},{3,4},{4,5},{5,6},{6,7},{7,8},{8,9},{9,10},{10,1... | collective-permute-start | bytes 98312 | tf_op jit(solution)/shard_map/ppermute | solution.py:14
  140.8 6.6 %collective-permute-start.19 = (bf16[2,8,64,256]{3,2,1,0:T(8,128)(2,1)}, bf16[2,8,64,256]{3,2,1,0:T(8,128)(2,1)}, u32[]{:S(2)}, u32[]{:S(2)}) collective-permute-start(bf16[2,8,64,256]{3,2,1,0:T(8,128)(2,1)} %pad_maximum_fusion.5), channel_id=1, source_target_pairs={{16,0},{32,16},{48,32},{64,48},{80,64},{96,80},{112,96},{128,112},... | collective-permute-start | bytes 1572872 | tf_op jit(solution)/shard_map/ppermute | solution.py:23
  161.1 3.6 %collective-permute-start.6 = (bf16[1,64,256]{2,1,0:T(8,128)(2,1)S(1)}, bf16[1,64,256]{2,1,0:T(8,128)(2,1)S(1)}, u32[]{:S(2)}, u32[]{:S(2)}) collective-permute-start(bf16[1,64,256]{2,1,0:T(8,128)(2,1)S(1)} %get-tuple-element.35), channel_id=1, source_target_pairs={{1,0},{2,1},{3,2},{4,3},{5,4},{6,5},{7,6},{8,7},{9,8},{10,9},{11,1... | collective-permute-start | bytes 98312 | tf_op jit(solution)/shard_map/ppermute | solution.py:15
  164.7 3.6 %fusion.85 = bf16[1,8,64,256]{3,2,1,0:T(8,128)(2,1)} fusion(bf16[8,64,2304]{2,1,0:T(8,128)(2,1)} %slice_dynamic-update-slice_fusion, bf16[2304,256,1]{1,0,2:T(8,128)(2,1)} %bitcast.220, bf16[8,64,256]{2,1,0:T(8,128)(2,1)} %copy-done.11, bf16[2,8,64,256]{3,2,1,0:T(8,128)(2,1)S(1)} %bitcast_select_fusion), kind=kOutput, calls=%fused_computation.131 | convolution fusion | flops 605552640 | bytes 4325376 | tf_op jit(solution)/shard_map/dot_general | solution.py:51
  170.6 5.0 %collective-permute-start.7 = (bf16[1,64,256]{2,1,0:T(8,128)(2,1)S(1)}, bf16[1,64,256]{2,1,0:T(8,128)(2,1)S(1)}, u32[]{:S(2)}, u32[]{:S(2)}) collective-permute-start(bf16[1,64,256]{2,1,0:T(8,128)(2,1)S(1)} %get-tuple-element.32), channel_id=1, source_target_pairs={{0,1},{1,2},{2,3},{3,4},{4,5},{5,6},{6,7},{7,8},{8,9},{9,10},{10,1... | collective-permute-start | bytes 98312 | tf_op jit(solution)/shard_map/ppermute | solution.py:14
  177.6 3.5 %collective-permute-start.29 = (bf16[2,8,64,256]{3,2,1,0:T(8,128)(2,1)S(1)}, bf16[2,8,64,256]{3,2,1,0:T(8,128)(2,1)S(1)}, u32[]{:S(2)}, u32[]{:S(2)}) collective-permute-start(bf16[2,8,64,256]{3,2,1,0:T(8,128)(2,1)S(1)} %pad_maximum_fusion.7), channel_id=1, source_target_pairs={{16,0},{32,16},{48,32},{64,48},{80,64},{96,80},{112,96},{128,112},... | collective-permute-start | bytes 1572872 | tf_op jit(solution)/shard_map/ppermute | solution.py:23
  182.4 2.1 select_bitcast_fusion
  184.4 4.1 %collective-permute-start.9 = (bf16[2,8,64,256]{3,2,1,0:T(8,128)(2,1)S(1)}, bf16[2,8,64,256]{3,2,1,0:T(8,128)(2,1)S(1)}, u32[]{:S(2)}, u32[]{:S(2)}) collective-permute-start(bf16[2,8,64,256]{3,2,1,0:T(8,128)(2,1)S(1)} %get-tuple-element.17), channel_id=1, source_target_pairs={{0,16},{16,32},{32,48},{48,64},{64,80},{80,96},{96,112},{112,128},... | collective-permute-start | bytes 1572872 | tf_op jit(solution)/shard_map/ppermute | solution.py:23
  188.6 4.9 %collective-permute-done.29 = bf16[2,8,64,256]{3,2,1,0:T(8,128)(2,1)S(1)} collective-permute-done((bf16[2,8,64,256]{3,2,1,0:T(8,128)(2,1)S(1)}, bf16[2,8,64,256]{3,2,1,0:T(8,128)(2,1)S(1)}, u32[]{:S(2)}, u32[]{:S(2)}) %collective-permute-start.29) | collective-permute-done | bytes 524320 | tf_op jit(solution)/shard_map/ppermute | solution.py:23
  194.3 17.5 %collective-permute-done.9 = bf16[2,8,64,256]{3,2,1,0:T(8,128)(2,1)S(1)} collective-permute-done((bf16[2,8,64,256]{3,2,1,0:T(8,128)(2,1)S(1)}, bf16[2,8,64,256]{3,2,1,0:T(8,128)(2,1)S(1)}, u32[]{:S(2)}, u32[]{:S(2)}) %collective-permute-start.9) | collective-permute-done | bytes 524320 | tf_op jit(solution)/shard_map/ppermute | solution.py:23
  212.7 55.6 %reduce-scatter.5.cloned.1.call-done = bf16[2,144,256]{2,1,0:T(8,128)(2,1)} async-done(((bf16[2,2304,256]{2,1,0:T(8,128)(2,1)}), bf16[2,144,256]{2,1,0:T(8,128)(2,1)}) %reduce-scatter.5.cloned.1.call-update) | async-done | bytes 147472 | tf_op jit(solution)/shard_map/reduce_scatter | solution.py:135
  (262 shorter events, 77.1 us)
Async XLA Ops:
  7.2 205.5 %reduce-scatter.3.cloned.1.call-start = ((), (), s32[]{:S(2)}) async-start(), calls=%async_computation.2 | async-start | bytes 2506752 | tf_op jit(solution)/shard_map/reduce_scatter | solution.py:135
  8.0 21.7 %collective-permute-start.20 = (bf16[1,64,256]{2,1,0:T(8,128)(2,1)S(1)}, bf16[1,64,256]{2,1,0:T(8,128)(2,1)S(1)}, u32[]{:S(2)}, u32[]{:S(2)}) collective-permute-start(bf16[1,64,256]{2,1,0:T(8,128)(2,1)S(1)} %get-tuple-element.14), channel_id=1, source_target_pairs={{0,1},{1,2},{2,3},{3,4},{4,5},{5,6},{6,7},{7,8},{8,9},{9,10},{10,1... | collective-permute-start | bytes 98312 | tf_op jit(solution)/shard_map/ppermute | solution.py:14
  9.9 23.5 %collective-permute-start.21 = (bf16[1,64,256]{2,1,0:T(8,128)(2,1)S(1)}, bf16[1,64,256]{2,1,0:T(8,128)(2,1)S(1)}, u32[]{:S(2)}, u32[]{:S(2)}) collective-permute-start(bf16[1,64,256]{2,1,0:T(8,128)(2,1)S(1)} %get-tuple-element.15), channel_id=1, source_target_pairs={{1,0},{2,1},{3,2},{4,3},{5,4},{6,5},{7,6},{8,7},{9,8},{10,9},{11,1... | collective-permute-start | bytes 98312 | tf_op jit(solution)/shard_map/ppermute | solution.py:15
  14.7 19.2 %collective-permute-start = (bf16[1,64,256]{2,1,0:T(8,128)(2,1)S(1)}, bf16[1,64,256]{2,1,0:T(8,128)(2,1)S(1)}, u32[]{:S(2)}, u32[]{:S(2)}) collective-permute-start(bf16[1,64,256]{2,1,0:T(8,128)(2,1)S(1)} %get-tuple-element.38), channel_id=1, source_target_pairs={{0,1},{1,2},{2,3},{3,4},{4,5},{5,6},{6,7},{7,8},{8,9},{9,10},{10,1... | collective-permute-start | bytes 98312 | tf_op jit(solution)/shard_map/ppermute | solution.py:14
  16.6 17.3 %collective-permute-start.1 = (bf16[1,64,256]{2,1,0:T(8,128)(2,1)S(1)}, bf16[1,64,256]{2,1,0:T(8,128)(2,1)S(1)}, u32[]{:S(2)}, u32[]{:S(2)}) collective-permute-start(bf16[1,64,256]{2,1,0:T(8,128)(2,1)S(1)} %get-tuple-element.39), channel_id=1, source_target_pairs={{1,0},{2,1},{3,2},{4,3},{5,4},{6,5},{7,6},{8,7},{9,8},{10,9},{11,1... | collective-permute-start | bytes 98312 | tf_op jit(solution)/shard_map/ppermute | solution.py:15
  22.0 20.3 %collective-permute-start.10 = (bf16[1,64,256]{2,1,0:T(8,128)(2,1)}, bf16[1,64,256]{2,1,0:T(8,128)(2,1)S(1)}, u32[]{:S(2)}, u32[]{:S(2)}) collective-permute-start(bf16[1,64,256]{2,1,0:T(8,128)(2,1)} %get-tuple-element.30), channel_id=1, source_target_pairs={{0,1},{1,2},{2,3},{3,4},{4,5},{5,6},{6,7},{7,8},{8,9},{9,10},{10,1... | collective-permute-start | bytes 98312 | tf_op jit(solution)/shard_map/ppermute | solution.py:14
  29.7 12.6 %collective-permute-start.11 = (bf16[1,64,256]{2,1,0:T(8,128)(2,1)S(1)}, bf16[1,64,256]{2,1,0:T(8,128)(2,1)S(1)}, u32[]{:S(2)}, u32[]{:S(2)}) collective-permute-start(bf16[1,64,256]{2,1,0:T(8,128)(2,1)S(1)} %get-tuple-element.31), channel_id=1, source_target_pairs={{1,0},{2,1},{3,2},{4,3},{5,4},{6,5},{7,6},{8,7},{9,8},{10,9},{11,1... | collective-permute-start | bytes 98312 | tf_op jit(solution)/shard_map/ppermute | solution.py:15
  36.6 22.4 %collective-permute-start.2 = (bf16[1,64,256]{2,1,0:T(8,128)(2,1)S(1)}, bf16[1,64,256]{2,1,0:T(8,128)(2,1)S(1)}, u32[]{:S(2)}, u32[]{:S(2)}) collective-permute-start(bf16[1,64,256]{2,1,0:T(8,128)(2,1)S(1)} %get-tuple-element.36), channel_id=1, source_target_pairs={{0,1},{1,2},{2,3},{3,4},{4,5},{5,6},{6,7},{7,8},{8,9},{9,10},{10,1... | collective-permute-start | bytes 98312 | tf_op jit(solution)/shard_map/ppermute | solution.py:14
  38.7 20.4 %collective-permute-start.3 = (bf16[1,64,256]{2,1,0:T(8,128)(2,1)S(1)}, bf16[1,64,256]{2,1,0:T(8,128)(2,1)S(1)}, u32[]{:S(2)}, u32[]{:S(2)}) collective-permute-start(bf16[1,64,256]{2,1,0:T(8,128)(2,1)S(1)} %get-tuple-element.37), channel_id=1, source_target_pairs={{1,0},{2,1},{3,2},{4,3},{5,4},{6,5},{7,6},{8,7},{9,8},{10,9},{11,1... | collective-permute-start | bytes 98312 | tf_op jit(solution)/shard_map/ppermute | solution.py:15
  50.3 20.6 %collective-permute-start.22 = (bf16[1,64,256]{2,1,0:T(8,128)(2,1)S(1)}, bf16[1,64,256]{2,1,0:T(8,128)(2,1)S(1)}, u32[]{:S(2)}, u32[]{:S(2)}) collective-permute-start(bf16[1,64,256]{2,1,0:T(8,128)(2,1)S(1)} %get-tuple-element.22), channel_id=1, source_target_pairs={{0,1},{1,2},{2,3},{3,4},{4,5},{5,6},{6,7},{7,8},{8,9},{9,10},{10,1... | collective-permute-start | bytes 98312 | tf_op jit(solution)/shard_map/ppermute | solution.py:14
  53.1 17.8 %collective-permute-start.23 = (bf16[1,64,256]{2,1,0:T(8,128)(2,1)S(1)}, bf16[1,64,256]{2,1,0:T(8,128)(2,1)S(1)}, u32[]{:S(2)}, u32[]{:S(2)}) collective-permute-start(bf16[1,64,256]{2,1,0:T(8,128)(2,1)S(1)} %get-tuple-element.23), channel_id=1, source_target_pairs={{1,0},{2,1},{3,2},{4,3},{5,4},{6,5},{7,6},{8,7},{9,8},{10,9},{11,1... | collective-permute-start | bytes 98312 | tf_op jit(solution)/shard_map/ppermute | solution.py:15
  61.1 20.8 %collective-permute-start.14 = (bf16[2,8,64,256]{3,2,1,0:T(8,128)(2,1)}, bf16[2,8,64,256]{3,2,1,0:T(8,128)(2,1)}, u32[]{:S(2)}, u32[]{:S(2)}) collective-permute-start(bf16[2,8,64,256]{3,2,1,0:T(8,128)(2,1)} %pad_maximum_fusion.4), channel_id=1, source_target_pairs={{16,0},{32,16},{48,32},{64,48},{80,64},{96,80},{112,96},{128,112},... | collective-permute-start | bytes 1572872 | tf_op jit(solution)/shard_map/ppermute | solution.py:23
  70.8 197.4 %reduce-scatter.5.cloned.1.call-start = ((), (), s32[]{:S(2)}) async-start(), calls=%async_computation.3 | async-start | bytes 2506752 | tf_op jit(solution)/shard_map/reduce_scatter | solution.py:135
  73.4 40.9 %collective-permute-start.24 = (bf16[2,8,64,256]{3,2,1,0:T(8,128)(2,1)S(1)}, bf16[2,8,64,256]{3,2,1,0:T(8,128)(2,1)S(1)}, u32[]{:S(2)}, u32[]{:S(2)}) collective-permute-start(bf16[2,8,64,256]{3,2,1,0:T(8,128)(2,1)S(1)} %pad_maximum_fusion.6), channel_id=1, source_target_pairs={{16,0},{32,16},{48,32},{64,48},{80,64},{96,80},{112,96},{128,112},... | collective-permute-start | bytes 1572872 | tf_op jit(solution)/shard_map/ppermute | solution.py:23
  84.1 37.9 %collective-permute-start.15 = (bf16[1,64,256]{2,1,0:T(8,128)(2,1)S(1)}, bf16[1,64,256]{2,1,0:T(8,128)(2,1)S(1)}, u32[]{:S(2)}, u32[]{:S(2)}) collective-permute-start(bf16[1,64,256]{2,1,0:T(8,128)(2,1)S(1)} %get-tuple-element.26), channel_id=1, source_target_pairs={{0,1},{1,2},{2,3},{3,4},{4,5},{5,6},{6,7},{7,8},{8,9},{9,10},{10,1... | collective-permute-start | bytes 98312 | tf_op jit(solution)/shard_map/ppermute | solution.py:14
  86.0 36.0 %collective-permute-start.16 = (bf16[1,64,256]{2,1,0:T(8,128)(2,1)S(1)}, bf16[1,64,256]{2,1,0:T(8,128)(2,1)S(1)}, u32[]{:S(2)}, u32[]{:S(2)}) collective-permute-start(bf16[1,64,256]{2,1,0:T(8,128)(2,1)S(1)} %get-tuple-element.27), channel_id=1, source_target_pairs={{1,0},{2,1},{3,2},{4,3},{5,4},{6,5},{7,6},{8,7},{9,8},{10,9},{11,1... | collective-permute-start | bytes 98312 | tf_op jit(solution)/shard_map/ppermute | solution.py:15
  114.5 42.5 %collective-permute-start.4 = (bf16[2,8,64,256]{3,2,1,0:T(8,128)(2,1)}, bf16[2,8,64,256]{3,2,1,0:T(8,128)(2,1)}, u32[]{:S(2)}, u32[]{:S(2)}) collective-permute-start(bf16[2,8,64,256]{3,2,1,0:T(8,128)(2,1)} %get-tuple-element.19), channel_id=1, source_target_pairs={{0,16},{16,32},{32,48},{48,64},{64,80},{80,96},{96,112},{112,128},... | collective-permute-start | bytes 1572872 | tf_op jit(solution)/shard_map/ppermute | solution.py:23
  116.4 13.4 %collective-permute-start.25 = (bf16[1,64,256]{2,1,0:T(8,128)(2,1)S(1)}, bf16[1,64,256]{2,1,0:T(8,128)(2,1)S(1)}, u32[]{:S(2)}, u32[]{:S(2)}) collective-permute-start(bf16[1,64,256]{2,1,0:T(8,128)(2,1)S(1)} %get-tuple-element.12), channel_id=1, source_target_pairs={{0,1},{1,2},{2,3},{3,4},{4,5},{5,6},{6,7},{7,8},{8,9},{9,10},{10,1... | collective-permute-start | bytes 98312 | tf_op jit(solution)/shard_map/ppermute | solution.py:14
  123.5 15.0 %collective-permute-start.17 = (bf16[1,64,256]{2,1,0:T(8,128)(2,1)S(1)}, bf16[1,64,256]{2,1,0:T(8,128)(2,1)S(1)}, u32[]{:S(2)}, u32[]{:S(2)}) collective-permute-start(bf16[1,64,256]{2,1,0:T(8,128)(2,1)S(1)} %get-tuple-element.24), channel_id=1, source_target_pairs={{0,1},{1,2},{2,3},{3,4},{4,5},{5,6},{6,7},{7,8},{8,9},{9,10},{10,1... | collective-permute-start | bytes 98312 | tf_op jit(solution)/shard_map/ppermute | solution.py:14
  132.1 15.4 %collective-permute-start.27 = (bf16[1,64,256]{2,1,0:T(8,128)(2,1)S(1)}, bf16[1,64,256]{2,1,0:T(8,128)(2,1)S(1)}, u32[]{:S(2)}, u32[]{:S(2)}) collective-permute-start(bf16[1,64,256]{2,1,0:T(8,128)(2,1)S(1)} %get-tuple-element.20), channel_id=1, source_target_pairs={{0,1},{1,2},{2,3},{3,4},{4,5},{5,6},{6,7},{7,8},{8,9},{9,10},{10,1... | collective-permute-start | bytes 98312 | tf_op jit(solution)/shard_map/ppermute | solution.py:14
  135.7 11.7 %collective-permute-start.28 = (bf16[1,64,256]{2,1,0:T(8,128)(2,1)S(1)}, bf16[1,64,256]{2,1,0:T(8,128)(2,1)S(1)}, u32[]{:S(2)}, u32[]{:S(2)}) collective-permute-start(bf16[1,64,256]{2,1,0:T(8,128)(2,1)S(1)} %get-tuple-element.21), channel_id=1, source_target_pairs={{1,0},{2,1},{3,2},{4,3},{5,4},{6,5},{7,6},{8,7},{9,8},{10,9},{11,1... | collective-permute-start | bytes 98312 | tf_op jit(solution)/shard_map/ppermute | solution.py:15
  140.8 41.6 %collective-permute-start.19 = (bf16[2,8,64,256]{3,2,1,0:T(8,128)(2,1)}, bf16[2,8,64,256]{3,2,1,0:T(8,128)(2,1)}, u32[]{:S(2)}, u32[]{:S(2)}) collective-permute-start(bf16[2,8,64,256]{3,2,1,0:T(8,128)(2,1)} %pad_maximum_fusion.5), channel_id=1, source_target_pairs={{16,0},{32,16},{48,32},{64,48},{80,64},{96,80},{112,96},{128,112},... | collective-permute-start | bytes 1572872 | tf_op jit(solution)/shard_map/ppermute | solution.py:23
  177.6 15.9 %collective-permute-start.29 = (bf16[2,8,64,256]{3,2,1,0:T(8,128)(2,1)S(1)}, bf16[2,8,64,256]{3,2,1,0:T(8,128)(2,1)S(1)}, u32[]{:S(2)}, u32[]{:S(2)}) collective-permute-start(bf16[2,8,64,256]{3,2,1,0:T(8,128)(2,1)S(1)} %pad_maximum_fusion.7), channel_id=1, source_target_pairs={{16,0},{32,16},{48,32},{64,48},{80,64},{96,80},{112,96},{128,112},... | collective-permute-start | bytes 1572872 | tf_op jit(solution)/shard_map/ppermute | solution.py:23
  184.4 27.4 %collective-permute-start.9 = (bf16[2,8,64,256]{3,2,1,0:T(8,128)(2,1)S(1)}, bf16[2,8,64,256]{3,2,1,0:T(8,128)(2,1)S(1)}, u32[]{:S(2)}, u32[]{:S(2)}) collective-permute-start(bf16[2,8,64,256]{3,2,1,0:T(8,128)(2,1)S(1)} %get-tuple-element.17), channel_id=1, source_target_pairs={{0,16},{16,32},{32,48},{48,64},{64,80},{80,96},{96,112},{112,128},... | collective-permute-start | bytes 1572872 | tf_op jit(solution)/shard_map/ppermute | solution.py:23
  (33 other events, 270.8 us)
Sparse Core Ops, SparseCore 0:
  71.0 110.0 reduce-scatter.2
  183.6 84.6 reduce-scatter.4
where the time goes:
time: 282 us; the launch traced here: 277 us
  waiting for transfers between devices  107 us (38%)
  starting transfers between devices  96.9 us (34%)
  local copies, waits for them, and re-layouts  20.9 us (7%)
  other arithmetic  20.7 us (7%)
  between operations  15.8 us (6%)
  matrix products  15.7 us (6%)
    reduce_scatter x2, waiting for transfers between devices, local(): lax.psum_scatter(wgrad.astype(jnp.bfloat16), 'band', scatter_dimension=1,...  55.6 us
    ppermute x6, waiting for transfers between devices, from_behind(): return lax.ppermute(block, axis, route)  51.1 us
    ppermute x12, starting transfers between devices, with_halo(): after = lax.ppermute(initial, axis, down)  38.5 us
    ppermute x12, starting transfers between devices, with_halo(): before = lax.ppermute(last, axis, up)  30.6 us
    ppermute x6, starting transfers between devices, from_behind(): return lax.ppermute(block, axis, route)  27.8 us
    dot_general x12, matrix products, apply_taps(): return jnp.dot(taps_matrix, weight, preferred_element_type=jnp.float32)  12.4 us
    unnamed x115, local copies, waits for them, and re-layouts  12.4 us
  transfers between devices with their start and end apart: 32, of which 5 were waited for; matrix products, arithmetic and copies ran while one was open for 18% of the time, Pallas kernels for 0%

commit v1 on v0

v1 whole, which is shorter than its diff:
```python
import functools

import jax
import jax.numpy as jnp
from jax import lax
from jax.experimental import pallas as pl
from jax.experimental.pallas import tpu as pltpu
from jax.sharding import PartitionSpec as P

F32 = jnp.float32
BF16 = jnp.bfloat16
VMEM = pl.BlockSpec(memory_space=pltpu.VMEM)
SMEM = pl.BlockSpec(memory_space=pltpu.SMEM)


def sigmoid(v):
    return 1.0 / (1.0 + jnp.exp(-v))


def act(v):
    v = v.astype(F32)
    return (v * sigmoid(v)).astype(BF16).astype(F32)


def slope(v):
    v = v.astype(F32)
    s = sigmoid(v)
    return s * (1.0 + v * (1.0 - s))


def stencil(x_ref, v, cols):
    n, ch = v.shape
    col = lax.rem(lax.broadcasted_iota(jnp.int32, (n, ch), 0), cols)
    x_ref[:, :ch] = jnp.where(col == 0, 0.0, pltpu.roll(v, 1, 0)).astype(BF16)
    x_ref[:, ch : 2 * ch] = v.astype(BF16)
    x_ref[:, 2 * ch :] = jnp.where(col == cols - 1, 0.0, pltpu.roll(v, n - 1, 0)).astype(BF16)


def conv(x_ref, w_ref, cols, start, size):
    depth = x_ref.shape[1]
    total = None
    for a in range(3):
        term = jnp.dot(
            x_ref[start + a * cols : start + a * cols + size, :],
            w_ref[a * depth : (a + 1) * depth, :],
            preferred_element_type=F32,
        )
        total = term if total is None else total + term
    return total


def correlate(x_ref, d, cols):
    size = d.shape[0]
    return [
        lax.dot_general(
            x_ref[a * cols : a * cols + size, :], d, (((0,), (0,)), ((), ())), preferred_element_type=F32
        )
        for a in range(3)
    ]


def stacked(*pieces):
    return jnp.concatenate([p.astype(F32) for p in pieces], axis=0)


def params(mib):
    return pltpu.CompilerParams(vmem_limit_bytes=mib << 20)


def estimate(matmuls, pixels, channels, extra):
    flops = matmuls * 2 * pixels * 9 * channels * channels
    return pl.CostEstimate(flops=flops, bytes_accessed=extra, transcendentals=4 * pixels * channels)


def invert_second(cols, tick, *refs):
    if tick == 0:
        (y_ref, g_ref, up_ref, down_ref, w_ref, wt_ref, out_ref, top_ref, bottom_ref, x_ref) = refs
        y1, y2, g1, g2 = (y_ref[0], y_ref[1], g_ref[0], g_ref[1])
    else:
        (flag_ref, came_ref, tops_ref, mids_ref, bots_ref, adv_ref, loss_ref, state_ref, up_ref, down_ref,
         w_ref, wt_ref, out_ref, top_ref, bottom_ref, y1g2_ref, x_ref) = refs
        local = flag_ref[0] == 1
        y1 = jnp.where(local, adv_ref[0], jnp.concatenate([tops_ref[0], mids_ref[0], bots_ref[0]], 0))
        g2 = jnp.where(local, loss_ref[1], jnp.concatenate([tops_ref[1], mids_ref[1], bots_ref[1]], 0))
        y2 = jnp.where(local, adv_ref[1], came_ref[0])
        g1 = jnp.where(local, loss_ref[0], came_ref[1])
        y1g2_ref[0] = y1
        y1g2_ref[1] = g2
    size = y1.shape[0]
    stencil(x_ref, act(stacked(up_ref[0], y1, down_ref[0])), cols)
    q2 = (y2.astype(F32) - conv(x_ref, w_ref, cols, 0, size)).astype(BF16)
    out_ref[0] = q2
    stencil(x_ref, stacked(up_ref[1], g2, down_ref[1]), cols)
    h1 = (g1.astype(F32) + slope(y1) * conv(x_ref, wt_ref, cols, 0, size)).astype(BF16)
    out_ref[1] = h1
    top_ref[0] = q2[:cols]
    top_ref[1] = h1[:cols]
    bottom_ref[0] = q2[size - cols :]
    bottom_ref[1] = h1[size - cols :]
    if tick:
        top_ref[2] = state_ref[1, :cols]
        bottom_ref[2] = state_ref[1, size - cols :]


def invert_first(cols, tick, *refs):
    if tick == 0:
        y_ref, g_ref, qh_ref, up_ref, down_ref, w_ref, wt_ref, tops_ref, mids_ref, bots_ref, x_ref = refs
        y1, g2 = (y_ref[0], g_ref[1])
    else:
        flag_ref, yg_ref, loss_ref, qh_ref, up_ref, down_ref, w_ref, wt_ref, p_ref, h_ref, x_ref = refs
        y1, g2 = (yg_ref[0], yg_ref[1])
    q2, h1 = (qh_ref[0], qh_ref[1])
    size = y1.shape[0]
    stencil(x_ref, act(stacked(up_ref[0], q2, down_ref[0])), cols)
    p2 = (y1.astype(F32) - conv(x_ref, w_ref, cols, 0, size)).astype(BF16)
    stencil(x_ref, stacked(up_ref[1], h1, down_ref[1]), cols)
    h2 = (g2.astype(F32) + slope(q2) * conv(x_ref, wt_ref, cols, 0, size)).astype(BF16)
    if tick == 0:
        for k, v in enumerate((p2, h2)):
            tops_ref[k] = v[:cols]
            mids_ref[k] = v[cols : size - cols]
            bots_ref[k] = v[size - cols :]
    else:
        first = flag_ref[1] == 1
        p_ref[...] = p2
        h_ref[0] = jnp.where(first, loss_ref[0], h1)
        h_ref[1] = jnp.where(first, loss_ref[1], h2)


def advance_first(cols, index, state_ref, up_ref, down_ref, w_ref, out_ref, top_ref, bottom_ref, x_ref):
    size = out_ref.shape[0]
    stencil(x_ref, act(stacked(up_ref[index], state_ref[1], down_ref[index])), cols)
    out = (state_ref[0].astype(F32) + conv(x_ref, w_ref, cols, 0, size)).astype(BF16)
    out_ref[...] = out
    top_ref[...] = out[:cols]
    bottom_ref[...] = out[size - cols :]


def advance_second(cols, flag_ref, state_ref, fresh_ref, first_ref, up_ref, down_ref, w_ref, adv_ref, send_ref, x_ref):
    size = first_ref.shape[0]
    stencil(x_ref, act(stacked(up_ref[...], first_ref[...], down_ref[...])), cols)
    out = (state_ref[1].astype(F32) + conv(x_ref, w_ref, cols, 0, size)).astype(BF16)
    last = flag_ref[0] == 1
    adv_ref[0] = first_ref[...]
    adv_ref[1] = out
    send_ref[0] = jnp.where(last, fresh_ref[0], first_ref[...])
    send_ref[1] = jnp.where(last, fresh_ref[1], out)


def weight_terms(cols, y_ref, g_ref, up1_ref, down1_ref, qh_ref, up2_ref, down2_ref, out_ref, x_ref):
    depth = x_ref.shape[1]
    stencil(x_ref, act(stacked(up2_ref[0], qh_ref[0], down2_ref[0])), cols)
    for a, term in enumerate(correlate(x_ref, qh_ref[1], cols)):
        out_ref[0, a * depth : (a + 1) * depth] = term
    stencil(x_ref, act(stacked(up1_ref[0], y_ref[0], down1_ref[0])), cols)
    for a, term in enumerate(correlate(x_ref, g_ref[1], cols)):
        out_ref[1, a * depth : (a + 1) * depth] = term


def weight_sums(cols, flag_ref, yg_ref, up1_ref, down1_ref, qh_ref, up2_ref, down2_ref, before_ref,
                send_ref, keep_ref, x_ref, total_ref):
    depth = x_ref.shape[1]
    core = flag_ref[4]
    rows = send_ref.shape[2]
    for k, (up, v, down, d) in enumerate((
        (up2_ref[0], qh_ref[0], down2_ref[0], qh_ref[1]),
        (up1_ref[0], yg_ref[0], down1_ref[0], yg_ref[1]),
    )):
        stencil(x_ref, act(stacked(up, v, down)), cols)
        for a, term in enumerate(correlate(x_ref, d, cols)):
            part = slice(a * depth, (a + 1) * depth)
            total_ref[part] = term + before_ref[k, part]
        for j in range(send_ref.shape[1]):
            mine = pl.multiple_of((2 * j + core) * rows, rows)
            other = pl.multiple_of((2 * j + 1 - core) * rows, rows)
            keep_ref[k, j] = total_ref[pl.ds(mine, rows)]
            send_ref[k, j] = total_ref[pl.ds(other, rows)].astype(BF16)


def sum_cores(flag_ref, keep_ref, came_ref, own_ref, right_ref, far_ref, left_ref):
    x = flag_ref[3]
    for d, ref in enumerate((own_ref, right_ref, far_ref, left_ref)):
        to = lax.rem(x + d, 4)
        for k in range(2):
            for z in range(2):
                value = keep_ref[k, 4 * z + to] + came_ref[k, 4 * z + to].astype(F32)
                ref[k, z] = value.astype(ref.dtype)


def sum_chips(flag_ref, own_ref, a_ref, b_ref, c_ref, keep_ref, send_ref):
    z = flag_ref[2]
    for k in range(2):
        for ref, at in ((keep_ref, z), (send_ref, 1 - z)):
            value = own_ref[k, at] + a_ref[k, at].astype(F32) + b_ref[k, at].astype(F32) + c_ref[k, at].astype(F32)
            ref[k] = value.astype(ref.dtype)


def shape(*dims, dtype=BF16):
    return jax.ShapeDtypeStruct(dims, dtype)


def call(body, n_scalars, args, outs, scratch, cost, mib=40, name=None):
    return pl.pallas_call(
        body,
        out_shape=outs,
        in_specs=[SMEM] * n_scalars + [VMEM] * (len(args) - n_scalars),
        out_specs=jax.tree.map(lambda _: VMEM, outs),
        scratch_shapes=scratch,
        compiler_params=params(mib),
        cost_estimate=cost,
        name=name,
    )(*args)


def flip(weight, channels):
    return weight.reshape(9, channels, channels)[::-1].transpose(0, 2, 1).reshape(9 * channels, channels)


def local(forward_state, returning_state, returning_grad, weights, fresh_input, loss_grad):
    rows, cols, ch = forward_state.shape[3 - 1 :]
    size = rows * cols
    segments = lax.axis_size("segment")
    bands = lax.axis_size("band")
    seg = lax.axis_index("segment")
    band = lax.axis_index("band")
    flags = jnp.stack([
        (seg == segments - 1).astype(jnp.int32),
        (seg == 0).astype(jnp.int32),
        band // 8,
        (band // 2) % 4,
        band % 2,
    ]).astype(jnp.int32)

    def up_down(bottom, top):
        return (
            lax.ppermute(bottom, "band", [(i, i + 1) for i in range(bands - 1)]),
            lax.ppermute(top, "band", [(i + 1, i) for i in range(bands - 1)]),
        )

    back_route = [(i + 1, i) for i in range(segments - 1)]
    back_ring = [(i, (i - 1) % segments) for i in range(segments)]
    ahead_ring = [(i, (i + 1) % segments) for i in range(segments)]

    def along(block, route):
        return lax.ppermute(block, "segment", route)

    state = forward_state.reshape(2, size, ch)
    y = returning_state.reshape(2, size, ch)
    g = returning_grad.reshape(2, size, ch)
    fresh = fresh_input.reshape(2, 2, size, ch)
    loss = loss_grad.reshape(2, 2, size, ch)
    w_f, w_g = (weights[0, 0], weights[0, 1])
    t_f, t_g = (flip(w_f, ch), flip(w_g, ch))
    x_scratch = [pltpu.VMEM((size + 2 * cols, 3 * ch), BF16)]
    MB = size * ch * 2
    WB = 9 * ch * ch * 2
    cost1 = estimate(1, size, ch, 3 * MB + WB)
    cost2 = estimate(2, size, ch, 6 * MB + 2 * WB)
    last = size - cols
    pair = shape(2, size, ch)
    edge2 = shape(2, cols, ch)
    edge3 = shape(3, cols, ch)

    e1 = up_down(
        jnp.stack([y[0, last:], g[1, last:], state[1, last:]]),
        jnp.stack([y[0, :cols], g[1, :cols], state[1, :cols]]),
    )
    qh, top, bottom = call(
        functools.partial(invert_second, cols, 0), 0, (y, g, *e1, w_g, t_g), (pair, edge2, edge2), x_scratch, cost2,
        name="invert_second",
    )
    came_qh = along(qh, back_route)
    e2 = up_down(bottom, top)
    tops, mids, bots = call(
        functools.partial(invert_first, cols, 0), 0, (y, g, qh, *e2, w_f, t_f),
        (edge2, shape(2, size - 2 * cols, ch), edge2), x_scratch, cost2, name="invert_first",
    )
    came_tops = along(tops, back_route)
    came_bots = along(bots, back_route)
    came_mids = along(mids, back_route)
    first, top, bottom = call(
        functools.partial(advance_first, cols, 2), 0, (state, *e1, w_f),
        (shape(size, ch), shape(cols, ch), shape(cols, ch)), x_scratch, cost1, name="advance_first",
    )
    e3 = up_down(bottom, top)
    adv, send = call(
        functools.partial(advance_second, cols), 1, (flags, state, fresh[0], first, *e3, w_g),
        (pair, pair), x_scratch, cost1, name="advance_second",
    )
    state = along(send, ahead_ring)
    terms = call(
        functools.partial(weight_terms, cols), 0, (y, g, *e1, qh, *e2), shape(2, 9 * ch, ch, dtype=F32),
        x_scratch, cost2, name="weight_terms",
    )

    at_end = seg == segments - 1
    f1 = up_down(
        jnp.where(at_end, jnp.stack([adv[0, last:], loss[0, 1, last:]]), came_bots),
        jnp.where(at_end, jnp.stack([adv[0, :cols], loss[0, 1, :cols]]), came_tops),
    )
    qh, top, bottom, yg = call(
        functools.partial(invert_second, cols, 1), 1,
        (flags, came_qh, came_tops, came_mids, came_bots, adv, loss[0], state, *f1, w_g, t_g),
        (pair, edge3, edge3, pair), x_scratch, cost2, name="invert_second",
    )
    q_out = along(qh[0], back_route)
    f2 = up_down(bottom, top)
    p2, hh = call(
        functools.partial(invert_first, cols, 1), 1, (flags, yg, loss[1], qh, *f2, w_f, t_f),
        (shape(size, ch), pair), x_scratch, cost2, name="invert_first",
    )
    p_out = along(p2, back_route)
    backward_out = along(hh, back_ring)
    send, keep = call(
        functools.partial(weight_sums, cols), 1, (flags, yg, *f1, qh, *f2, terms),
        (shape(2, 8, 9 * ch // bands, ch), shape(2, 8, 9 * ch // bands, ch, dtype=F32)),
        x_scratch + [pltpu.VMEM((9 * ch, ch), F32)], cost2, name="weight_sums",
    )
    first, top, bottom = call(
        functools.partial(advance_first, cols, 2), 0, (state, *f2, w_f),
        (shape(size, ch), shape(cols, ch), shape(cols, ch)), x_scratch, cost1, name="advance_first",
    )
    f3 = up_down(bottom, top)
    adv, ahead = call(
        functools.partial(advance_second, cols), 1, (flags, state, fresh[1], first, *f3, w_g),
        (pair, pair), x_scratch, cost1, name="advance_second",
    )
    forward_out = along(ahead, ahead_ring)

    part = 9 * ch // bands
    came = lax.ppermute(send, "band", [(i, i ^ 1) for i in range(bands)])

    def on_x(block, step):
        return lax.ppermute(
            block, "band", [(i, (i & 8) | ((((i >> 1) & 3) + step) % 4) << 1 | (i & 1)) for i in range(bands)]
        )

    quarter = shape(2, 2, part, ch)
    own, right, far, left = call(
        sum_cores, 1, (flags, keep, came), (shape(2, 2, part, ch, dtype=F32), quarter, quarter, quarter), [],
        estimate(0, size, ch, 8 * MB), name="sum_cores",
    )
    far, right, left = (on_x(far, 2), on_x(right, 1), on_x(left, 3))
    keep, send = call(
        sum_chips, 1, (flags, own, far, right, left), (shape(2, part, ch, dtype=F32), shape(2, part, ch)), [],
        estimate(0, size, ch, 3 * MB), name="sum_chips",
    )
    weight_grad = keep + lax.ppermute(send, "band", [(i, i ^ 8) for i in range(bands)]).astype(F32)

    returning_out = jnp.where(at_end, adv, jnp.stack([p_out, q_out]))
    full = forward_state.shape
    return (forward_out.reshape(full), returning_out.reshape(full), backward_out.reshape(full), weight_grad[None])


def solution(mesh):
    return jax.shard_map(
        local,
        mesh=mesh,
        in_specs=(
            P("segment", None, "band", None, None),
            P("segment", None, "band", None, None),
            P("segment", None, "band", None, None),
            P("segment", None, None, None),
            P(None, None, "band", None, None),
            P(None, None, "band", None, None),
        ),
        out_specs=(
            P("segment", None, "band", None, None),
            P("segment", None, "band", None, None),
            P("segment", None, "band", None, None),
            P("segment", None, "band", None),
        ),
        check_vma=False,
    )
```

time: 282 us -> 178 us (0.63)
  waiting for transfers between devices: 107 us -> 50.9 us
  starting transfers between devices: 96.9 us -> 74.1 us
  Pallas kernels: 0 us -> 22.5 us
  other arithmetic: 20.7 us -> 2.93 us
  matrix products: 15.7 us -> 0 us
  between operations: 15.8 us -> 1.16 us
    reduce_scatter x2 -> x0, waiting for transfers between devices: 55.6 us -> none  [local(): lax.psum_scatter(wgrad.astype(jnp.bfloat16), 'band', scatter_dimension=1,...]
    ppermute x30 -> x26, starting transfers between devices: 96.9 us -> 74.1 us  [the longest x9 34.1 us: along(): return lax.ppermute(block, 'segment', route)]
    pallas_call x0 -> x12, Pallas kernels: none -> 22.5 us  [call(): pl.pallas_call(body, out_shape=outs, in_specs=[SMEM] * n_scalars + [VMEM]...]
    dot_general x16 -> x0, matrix products: 15.7 us -> none  [the longest x12 12.4 us: apply_taps(): return jnp.dot(taps_matrix, weight, preferred_element_type=jnp.float32)]
    broadcast_in_dim x4 -> x1, other arithmetic: 5.48 us -> 0.74 us  [local(): weight_grad[None]]
    another operation x0 -> x3, local copies, waits for them, and re-layouts: none -> 3.87 us  [the longest x1 2.39 us: flip(): weight.reshape(9, channels, channels)[::-1].transpose(0, 2, 1)]
    another operation x6 -> x2, other arithmetic: 5.04 us -> 1.31 us  [the longest x1 0.65 us: local(): jnp.stack([y[0, :cols], g[1, :cols], state[1, :cols]])]
    unnamed x31 -> x0, other arithmetic: 3.08 us -> none
  transfers between devices with their start and end apart: 32 -> 26, of which waited for: 5 -> 6; matrix products, arithmetic and copies ran while one was open for 18% -> 8% of each run, Pallas kernels for 0% -> 9%
where the time goes in v1:
time: 178 us; the launch traced here: 175 us
  starting transfers between devices  74.1 us (42%)
  waiting for transfers between devices  50.9 us (29%)
  local copies, waits for them, and re-layouts  23.5 us (13%)
  Pallas kernels  22.5 us (13%)
  other arithmetic  2.93 us (2%)
    ppermute x9, waiting for transfers between devices, along(): return lax.ppermute(block, 'segment', route)  43.6 us
    ppermute x9, starting transfers between devices, along(): return lax.ppermute(block, 'segment', route)  34.1 us
    pallas_call x12, Pallas kernels, call(): pl.pallas_call(body, out_shape=outs, in_specs=[SMEM] * n_scalars + [VMEM]...  22.5 us
    ppermute x6, starting transfers between devices, up_down(): lax.ppermute(top, 'band', [(i + 1, i) for i in range(bands - 1)])  20.8 us
    ppermute x6, starting transfers between devices, up_down(): lax.ppermute(bottom, 'band', [(i, i + 1) for i in range(bands - 1)])  11.7 us
    unnamed x42, local copies, waits for them, and re-layouts  9.84 us
    ppermute x3, starting transfers between devices, on_x(): lax.ppermute(block, 'band', [(i, i & 8 | ((i >> 1 & 3) + step) % 4 << 1 |...  6.5 us
    ppermute x1, waiting for transfers between devices, local(): lax.ppermute(send, 'band', [(i, i ^ 8) for i in range(bands)]).astype(F32)  3.86 us
  transfers between devices with their start and end apart: 26, of which 6 were waited for; matrix products, arithmetic and copies ran while one was open for 8% of the time, Pallas kernels for 9%

profile of v1, /device:TPU:18, one launch (start us, length us, event | category | flops | bytes accessed | tf_op | source)
XLA Modules:
  0.0 175.0 jit_solution(9325108478811808397)
XLA Ops:
  5.6 3.6 %collective-permute-start.1 = (bf16[3,64,256]{2,1,0:T(8,128)(2,1)}, bf16[3,64,256]{2,1,0:T(8,128)(2,1)}, u32[]{:S(2)}, u32[]{:S(2)}) collective-permute-start(bf16[3,64,256]{2,1,0:T(8,128)(2,1)} %pad_maximum_fusion.1), channel_id=1, source_target_pairs={{1,0},{2,1},{3,2},{4,3},{5,4},{6,5},{7,6},{8,7},{9,8},{10,9},{11,1... | collective-permute-start | bytes 294920 | tf_op jit(solution)/shard_map/ppermute | solution.py:237
  17.3 2.4 %advance_first.2 = (bf16[512,256]{1,0:T(8,128)(2,1)S(1)}, bf16[64,256]{1,0:T(8,128)(2,1)}, bf16[64,256]{1,0:T(8,128)(2,1)}) custom-call(bf16[2,512,256]{2,1,0:T(8,128)(2,1)S(1)} %bitcast.54, bf16[3,64,256]{2,1,0:T(8,128)(2,1)S(1)} %collective-permute-done.up_ref.refs_2_.up1_ref, bf16[3,64,256]{2,1,0:T(8,128)(2,1)} %collective-permute-done.1.down_ref.refs_3_.down1_ref, ...), custom_call_target="tpu_custom_call" | custom-call | flops 603979776 | bytes 1966080 | tf_op jit(solution)/shard_map/advance_first/pallas_call | solution.py:203
  21.6 3.6 %collective-permute-start.3 = (bf16[64,256]{1,0:T(8,128)(2,1)}, bf16[64,256]{1,0:T(8,128)(2,1)}, u32[]{:S(2)}, u32[]{:S(2)}) collective-permute-start(bf16[64,256]{1,0:T(8,128)(2,1)} %get-tuple-element.36), channel_id=1, source_target_pairs={{1,0},{2,1},{3,2},{4,3},{5,4},{6,5},{7,6},{8,7},{9,8},{10,9},{11,1... | collective-permute-start | bytes 98312 | tf_op jit(solution)/shard_map/ppermute | solution.py:237
  25.3 3.0 %invert_second.2 = (bf16[2,512,256]{2,1,0:T(8,128)(2,1)S(1)}, bf16[2,64,256]{2,1,0:T(8,128)(2,1)}, bf16[2,64,256]{2,1,0:T(8,128)(2,1)}) custom-call(bf16[2,512,256]{2,1,0:T(8,128)(2,1)S(1)} %bitcast.46, bf16[2,512,256]{2,1,0:T(8,128)(2,1)S(1)} %bitcast.50, bf16[3,64,256]{2,1,0:T(8,128)(2,1)S(1)} %collective-permute-done.up_ref.refs_2_.up1_ref, ...), custom_call_target="tpu_custom_call" | custom-call | flops 1207959552 | bytes 3932160 | tf_op jit(solution)/shard_map/invert_second/pallas_call | solution.py:203
  31.0 3.6 %collective-permute-start.7 = (bf16[2,64,256]{2,1,0:T(8,128)(2,1)}, bf16[2,64,256]{2,1,0:T(8,128)(2,1)}, u32[]{:S(2)}, u32[]{:S(2)}) collective-permute-start(bf16[2,64,256]{2,1,0:T(8,128)(2,1)} %get-tuple-element.40), channel_id=1, source_target_pairs={{1,0},{2,1},{3,2},{4,3},{5,4},{6,5},{7,6},{8,7},{9,8},{10,9},{11,1... | collective-permute-start | bytes 196616 | tf_op jit(solution)/shard_map/ppermute | solution.py:237
  36.1 2.4 %copy.11 = bf16[9,256,256]{1,2,0:T(8,128)(2,1)} copy(bf16[9,256,256]{2,1,0:T(8,128)(2,1)} %bitcast.57) | data formatting | bytes 2359296 | tf_op jit(solution)/shard_map/reshape;squeeze | solution.py:216
  40.9 8.1 %collective-permute-start.5 = (bf16[2,512,256]{2,1,0:T(8,128)(2,1)}, bf16[2,512,256]{2,1,0:T(8,128)(2,1)S(1)}, u32[]{:S(2)}, u32[]{:S(2)}) collective-permute-start(bf16[2,512,256]{2,1,0:T(8,128)(2,1)} %copy-done.11), channel_id=1, source_target_pairs={{16,0},{32,16},{48,32},{64,48},{80,64},{96,80},{112,96},{128,112},... | collective-permute-start | bytes 1572872 | tf_op jit(solution)/shard_map/ppermute | solution.py:245
  56.0 2.4 %invert_first.2 = (bf16[2,64,256]{2,1,0:T(8,128)(2,1)S(1)}, bf16[2,384,256]{2,1,0:T(8,128)(2,1)S(1)}, bf16[2,64,256]{2,1,0:T(8,128)(2,1)S(1)}) custom-call(bf16[2,512,256]{2,1,0:T(8,128)(2,1)S(1)} %bitcast.47, bf16[2,512,256]{2,1,0:T(8,128)(2,1)S(1)} %bitcast.51, bf16[2,512,256]{2,1,0:T(8,128)(2,1)S(1)} %copy-done.12, ...), custom_call_target="tpu_custom_call" | custom-call | flops 1207959552 | bytes 3932160 | tf_op jit(solution)/shard_map/invert_first/pallas_call | solution.py:203
  58.4 3.4 %collective-permute-start.8 = (bf16[2,64,256]{2,1,0:T(8,128)(2,1)S(1)}, bf16[2,64,256]{2,1,0:T(8,128)(2,1)S(1)}, u32[]{:S(2)}, u32[]{:S(2)}) collective-permute-start(bf16[2,64,256]{2,1,0:T(8,128)(2,1)S(1)} %get-tuple-element.41), channel_id=1, source_target_pairs={{16,0},{32,16},{48,32},{64,48},{80,64},{96,80},{112,96},{128,112},... | collective-permute-start | bytes 196616 | tf_op jit(solution)/shard_map/ppermute | solution.py:245
  63.4 5.5 %collective-permute-start.10 = (bf16[2,64,256]{2,1,0:T(8,128)(2,1)S(1)}, bf16[2,64,256]{2,1,0:T(8,128)(2,1)S(1)}, u32[]{:S(2)}, u32[]{:S(2)}) collective-permute-start(bf16[2,64,256]{2,1,0:T(8,128)(2,1)S(1)} %get-tuple-element.43), channel_id=1, source_target_pairs={{16,0},{32,16},{48,32},{64,48},{80,64},{96,80},{112,96},{128,112},... | collective-permute-start | bytes 196616 | tf_op jit(solution)/shard_map/ppermute | solution.py:245
  70.8 4.7 %collective-permute-done.8.refs_2_ = bf16[2,64,256]{2,1,0:T(8,128)(2,1)S(1)} collective-permute-done((bf16[2,64,256]{2,1,0:T(8,128)(2,1)S(1)}, bf16[2,64,256]{2,1,0:T(8,128)(2,1)S(1)}, u32[]{:S(2)}, u32[]{:S(2)}) %collective-permute-start.8) | collective-permute-done | bytes 65568 | tf_op jit(solution)/shard_map/ppermute | solution.py:245
  80.0 3.4 %collective-permute-done.11.refs_8_.up1_ref = bf16[2,64,256]{2,1,0:T(8,128)(2,1)S(1)} collective-permute-done((bf16[2,64,256]{2,1,0:T(8,128)(2,1)S(1)}, bf16[2,64,256]{2,1,0:T(8,128)(2,1)S(1)}, u32[]{:S(2)}, u32[]{:S(2)}) %collective-permute-start.11) | collective-permute-done | bytes 65568 | tf_op jit(solution)/shard_map/ppermute | solution.py:236
  83.4 10.7 %collective-permute-done.9.refs_3_ = bf16[2,384,256]{2,1,0:T(8,128)(2,1)S(1)} collective-permute-done((bf16[2,384,256]{2,1,0:T(8,128)(2,1)S(1)}, bf16[2,384,256]{2,1,0:T(8,128)(2,1)S(1)}, u32[]{:S(2)}, u32[]{:S(2)}) %collective-permute-start.9) | collective-permute-done | bytes 393248 | tf_op jit(solution)/shard_map/ppermute | solution.py:245
  98.2 3.9 %collective-permute-start.14 = (bf16[3,64,256]{2,1,0:T(8,128)(2,1)S(1)}, bf16[3,64,256]{2,1,0:T(8,128)(2,1)S(1)}, u32[]{:S(2)}, u32[]{:S(2)}) collective-permute-start(bf16[3,64,256]{2,1,0:T(8,128)(2,1)S(1)} %get-tuple-element.46), channel_id=1, source_target_pairs={{1,0},{2,1},{3,2},{4,3},{5,4},{6,5},{7,6},{8,7},{9,8},{10,9},{11,1... | collective-permute-start | bytes 294920 | tf_op jit(solution)/shard_map/ppermute | solution.py:237
  102.1 2.5 %weight_terms.1.before_ref = f32[2,2304,256]{2,1,0:T(8,128)S(1)} custom-call(bf16[2,512,256]{2,1,0:T(8,128)(2,1)S(1)} %bitcast.48, bf16[2,512,256]{2,1,0:T(8,128)(2,1)S(1)} %bitcast.52, bf16[3,64,256]{2,1,0:T(8,128)(2,1)S(1)} %collective-permute-done.up_ref.refs_2_.up1_ref, bf16[3,64,256]{2,1,0:T(8,128)(2,1)} %collective-permute-done.1.down_ref.refs_3_.down1_ref, ...), custom_call_target="tpu_custom_call" | custom-call | flops 1207959552 | bytes 3932160 | tf_op jit(solution)/shard_map/weight_terms/pallas_call | solution.py:203
  104.7 2.6 %weight_sums.1 = (bf16[2,8,144,256]{3,2,1,0:T(8,128)(2,1)S(1)}, f32[2,8,144,256]{3,2,1,0:T(8,128)S(1)}) custom-call(s32[5]{0:T(128)S(1)} %stack.52.flag_ref.refs_0_, bf16[2,512,256]{2,1,0:T(8,128)(2,1)S(1)} %get-tuple-element.52.refs_1_.yg_ref, bf16[2,64,256]{2,1,0:T(8,128)(2,1)S(1)} %collective-permute-done.11.refs_8_.up1_ref, ...), custom_call_target="tpu_custom_call" | custom-call | flops 1207959552 | bytes 3932160 | tf_op jit(solution)/shard_map/weight_sums/pallas_call | solution.py:203
  110.8 3.6 %collective-permute-start.16 = (bf16[64,256]{1,0:T(8,128)(2,1)S(1)}, bf16[64,256]{1,0:T(8,128)(2,1)S(1)}, u32[]{:S(2)}, u32[]{:S(2)}) collective-permute-start(bf16[64,256]{1,0:T(8,128)(2,1)S(1)} %get-tuple-element.49), channel_id=1, source_target_pairs={{1,0},{2,1},{3,2},{4,3},{5,4},{6,5},{7,6},{8,7},{9,8},{10,9},{11,1... | collective-permute-start | bytes 98312 | tf_op jit(solution)/shard_map/ppermute | solution.py:237
  115.3 4.4 %collective-permute-start.22 = (bf16[2,2,144,256]{3,2,1,0:T(8,128)(2,1)S(1)}, bf16[2,2,144,256]{3,2,1,0:T(8,128)(2,1)S(1)}, u32[]{:S(2)}, u32[]{:S(2)}) collective-permute-start(bf16[2,2,144,256]{3,2,1,0:T(8,128)(2,1)S(1)} %get-tuple-element.59), channel_id=1, source_target_pairs={{0,4},{1,5},{2,6},{3,7},{4,0},{5,1},{6,2},{7,3},{8,12},{9,13},{10,... | collective-permute-start | bytes 884744 | tf_op jit(solution)/shard_map/ppermute | solution.py:334
  121.7 3.3 %collective-permute-start.20 = (bf16[2,512,256]{2,1,0:T(8,128)(2,1)S(1)}, bf16[2,512,256]{2,1,0:T(8,128)(2,1)S(1)}, u32[]{:S(2)}, u32[]{:S(2)}) collective-permute-start(bf16[2,512,256]{2,1,0:T(8,128)(2,1)S(1)} %get-tuple-element.55), channel_id=1, source_target_pairs={{0,240},{16,0},{32,16},{48,32},{64,48},{80,64},{96,80},{112,96},{1... | collective-permute-start | bytes 1572872 | tf_op jit(solution)/shard_map/ppermute | solution.py:245
  128.7 6.9 %collective-permute-start.19 = (bf16[512,256]{1,0:T(8,128)(2,1)S(1)}, bf16[512,256]{1,0:T(8,128)(2,1)S(1)}, u32[]{:S(2)}, u32[]{:S(2)}) collective-permute-start(bf16[512,256]{1,0:T(8,128)(2,1)S(1)} %slice_bitcast_fusion), channel_id=1, source_target_pairs={{16,0},{32,16},{48,32},{64,48},{80,64},{96,80},{112,96},{128,112},... | collective-permute-start | bytes 786440 | tf_op jit(solution)/shard_map/ppermute | solution.py:245
  135.5 3.5 %collective-permute-start.18 = (bf16[512,256]{1,0:T(8,128)(2,1)S(1)}, bf16[512,256]{1,0:T(8,128)(2,1)S(1)}, u32[]{:S(2)}, u32[]{:S(2)}) collective-permute-start(bf16[512,256]{1,0:T(8,128)(2,1)S(1)} %get-tuple-element.54), channel_id=1, source_target_pairs={{16,0},{32,16},{48,32},{64,48},{80,64},{96,80},{112,96},{128,112},... | collective-permute-start | bytes 786440 | tf_op jit(solution)/shard_map/ppermute | solution.py:245
  139.9 22.6 %collective-permute-done.19 = bf16[512,256]{1,0:T(8,128)(2,1)S(1)} collective-permute-done((bf16[512,256]{1,0:T(8,128)(2,1)S(1)}, bf16[512,256]{1,0:T(8,128)(2,1)S(1)}, u32[]{:S(2)}, u32[]{:S(2)}) %collective-permute-start.19) | collective-permute-done | bytes 262176 | tf_op jit(solution)/shard_map/ppermute | solution.py:245
  162.5 5.5 %collective-permute-done.18 = bf16[512,256]{1,0:T(8,128)(2,1)S(1)} collective-permute-done((bf16[512,256]{1,0:T(8,128)(2,1)S(1)}, bf16[512,256]{1,0:T(8,128)(2,1)S(1)}, u32[]{:S(2)}, u32[]{:S(2)}) %collective-permute-start.18) | collective-permute-done | bytes 262176 | tf_op jit(solution)/shard_map/ppermute | solution.py:245
  168.9 3.9 %collective-permute-done.25 = bf16[2,144,256]{2,1,0:T(8,128)(2,1)S(1)} collective-permute-done((bf16[2,144,256]{2,1,0:T(8,128)(2,1)S(1)}, bf16[2,144,256]{2,1,0:T(8,128)(2,1)S(1)}, u32[]{:S(2)}, u32[]{:S(2)}) %collective-permute-start.25) | collective-permute-done | bytes 147488 | tf_op jit(solution)/shard_map/ppermute | solution.py:348
  (101 shorter events, 54.2 us)
Async XLA Ops:
  2.9 12.0 %collective-permute-start = (bf16[3,64,256]{2,1,0:T(8,128)(2,1)}, bf16[3,64,256]{2,1,0:T(8,128)(2,1)S(1)}, u32[]{:S(2)}, u32[]{:S(2)}) collective-permute-start(bf16[3,64,256]{2,1,0:T(8,128)(2,1)} %pad_maximum_fusion), channel_id=1, source_target_pairs={{0,1},{1,2},{2,3},{3,4},{4,5},{5,6},{6,7},{7,8},{8,9},{9,10},{10,1... | collective-permute-start | bytes 294920 | tf_op jit(solution)/shard_map/ppermute | solution.py:236
  5.6 9.4 %collective-permute-start.1 = (bf16[3,64,256]{2,1,0:T(8,128)(2,1)}, bf16[3,64,256]{2,1,0:T(8,128)(2,1)}, u32[]{:S(2)}, u32[]{:S(2)}) collective-permute-start(bf16[3,64,256]{2,1,0:T(8,128)(2,1)} %pad_maximum_fusion.1), channel_id=1, source_target_pairs={{1,0},{2,1},{3,2},{4,3},{5,4},{6,5},{7,6},{8,7},{9,8},{10,9},{11,1... | collective-permute-start | bytes 294920 | tf_op jit(solution)/shard_map/ppermute | solution.py:237
  19.7 29.3 %collective-permute-start.2 = (bf16[64,256]{1,0:T(8,128)(2,1)}, bf16[64,256]{1,0:T(8,128)(2,1)S(1)}, u32[]{:S(2)}, u32[]{:S(2)}) collective-permute-start(bf16[64,256]{1,0:T(8,128)(2,1)} %get-tuple-element.35), channel_id=1, source_target_pairs={{0,1},{1,2},{2,3},{3,4},{4,5},{5,6},{6,7},{7,8},{8,9},{9,10},{10,1... | collective-permute-start | bytes 98312 | tf_op jit(solution)/shard_map/ppermute | solution.py:236
  21.6 27.4 %collective-permute-start.3 = (bf16[64,256]{1,0:T(8,128)(2,1)}, bf16[64,256]{1,0:T(8,128)(2,1)}, u32[]{:S(2)}, u32[]{:S(2)}) collective-permute-start(bf16[64,256]{1,0:T(8,128)(2,1)} %get-tuple-element.36), channel_id=1, source_target_pairs={{1,0},{2,1},{3,2},{4,3},{5,4},{6,5},{7,6},{8,7},{9,8},{10,9},{11,1... | collective-permute-start | bytes 98312 | tf_op jit(solution)/shard_map/ppermute | solution.py:237
  29.1 23.7 %collective-permute-start.6 = (bf16[2,64,256]{2,1,0:T(8,128)(2,1)}, bf16[2,64,256]{2,1,0:T(8,128)(2,1)}, u32[]{:S(2)}, u32[]{:S(2)}) collective-permute-start(bf16[2,64,256]{2,1,0:T(8,128)(2,1)} %get-tuple-element.39), channel_id=1, source_target_pairs={{0,1},{1,2},{2,3},{3,4},{4,5},{5,6},{6,7},{7,8},{8,9},{9,10},{10,1... | collective-permute-start | bytes 196616 | tf_op jit(solution)/shard_map/ppermute | solution.py:236
  31.0 21.8 %collective-permute-start.7 = (bf16[2,64,256]{2,1,0:T(8,128)(2,1)}, bf16[2,64,256]{2,1,0:T(8,128)(2,1)}, u32[]{:S(2)}, u32[]{:S(2)}) collective-permute-start(bf16[2,64,256]{2,1,0:T(8,128)(2,1)} %get-tuple-element.40), channel_id=1, source_target_pairs={{1,0},{2,1},{3,2},{4,3},{5,4},{6,5},{7,6},{8,7},{9,8},{10,9},{11,1... | collective-permute-start | bytes 196616 | tf_op jit(solution)/shard_map/ppermute | solution.py:237
  40.9 53.2 %collective-permute-start.5 = (bf16[2,512,256]{2,1,0:T(8,128)(2,1)}, bf16[2,512,256]{2,1,0:T(8,128)(2,1)S(1)}, u32[]{:S(2)}, u32[]{:S(2)}) collective-permute-start(bf16[2,512,256]{2,1,0:T(8,128)(2,1)} %copy-done.11), channel_id=1, source_target_pairs={{16,0},{32,16},{48,32},{64,48},{80,64},{96,80},{112,96},{128,112},... | collective-permute-start | bytes 1572872 | tf_op jit(solution)/shard_map/ppermute | solution.py:245
  58.4 17.1 %collective-permute-start.8 = (bf16[2,64,256]{2,1,0:T(8,128)(2,1)S(1)}, bf16[2,64,256]{2,1,0:T(8,128)(2,1)S(1)}, u32[]{:S(2)}, u32[]{:S(2)}) collective-permute-start(bf16[2,64,256]{2,1,0:T(8,128)(2,1)S(1)} %get-tuple-element.41), channel_id=1, source_target_pairs={{16,0},{32,16},{48,32},{64,48},{80,64},{96,80},{112,96},{128,112},... | collective-permute-start | bytes 196616 | tf_op jit(solution)/shard_map/ppermute | solution.py:245
  61.8 32.3 %collective-permute-start.4 = (bf16[2,512,256]{2,1,0:T(8,128)(2,1)S(1)}, bf16[2,512,256]{2,1,0:T(8,128)(2,1)S(1)}, u32[]{:S(2)}, u32[]{:S(2)}) collective-permute-start(bf16[2,512,256]{2,1,0:T(8,128)(2,1)S(1)} %get-tuple-element.37), channel_id=1, source_target_pairs={{0,16},{16,32},{32,48},{48,64},{64,80},{80,96},{96,112},{112,128},... | collective-permute-start | bytes 1572872 | tf_op jit(solution)/shard_map/ppermute | solution.py:245
  63.4 14.4 %collective-permute-start.10 = (bf16[2,64,256]{2,1,0:T(8,128)(2,1)S(1)}, bf16[2,64,256]{2,1,0:T(8,128)(2,1)S(1)}, u32[]{:S(2)}, u32[]{:S(2)}) collective-permute-start(bf16[2,64,256]{2,1,0:T(8,128)(2,1)S(1)} %get-tuple-element.43), channel_id=1, source_target_pairs={{16,0},{32,16},{48,32},{64,48},{80,64},{96,80},{112,96},{128,112},... | collective-permute-start | bytes 196616 | tf_op jit(solution)/shard_map/ppermute | solution.py:245
  68.8 25.3 %collective-permute-start.9 = (bf16[2,384,256]{2,1,0:T(8,128)(2,1)S(1)}, bf16[2,384,256]{2,1,0:T(8,128)(2,1)S(1)}, u32[]{:S(2)}, u32[]{:S(2)}) collective-permute-start(bf16[2,384,256]{2,1,0:T(8,128)(2,1)S(1)} %get-tuple-element.42), channel_id=1, source_target_pairs={{16,0},{32,16},{48,32},{64,48},{80,64},{96,80},{112,96},{128,112},... | collective-permute-start | bytes 1179656 | tf_op jit(solution)/shard_map/ppermute | solution.py:245
  96.2 8.4 %collective-permute-start.13 = (bf16[3,64,256]{2,1,0:T(8,128)(2,1)S(1)}, bf16[3,64,256]{2,1,0:T(8,128)(2,1)S(1)}, u32[]{:S(2)}, u32[]{:S(2)}) collective-permute-start(bf16[3,64,256]{2,1,0:T(8,128)(2,1)S(1)} %get-tuple-element.45), channel_id=1, source_target_pairs={{0,1},{1,2},{2,3},{3,4},{4,5},{5,6},{6,7},{7,8},{8,9},{9,10},{10,1... | collective-permute-start | bytes 294920 | tf_op jit(solution)/shard_map/ppermute | solution.py:236
  98.2 6.5 %collective-permute-start.14 = (bf16[3,64,256]{2,1,0:T(8,128)(2,1)S(1)}, bf16[3,64,256]{2,1,0:T(8,128)(2,1)S(1)}, u32[]{:S(2)}, u32[]{:S(2)}) collective-permute-start(bf16[3,64,256]{2,1,0:T(8,128)(2,1)S(1)} %get-tuple-element.46), channel_id=1, source_target_pairs={{1,0},{2,1},{3,2},{4,3},{5,4},{6,5},{7,6},{8,7},{9,8},{10,9},{11,1... | collective-permute-start | bytes 294920 | tf_op jit(solution)/shard_map/ppermute | solution.py:237
  107.2 7.3 %collective-permute-start.21 = (bf16[2,8,144,256]{3,2,1,0:T(8,128)(2,1)S(1)}, bf16[2,8,144,256]{3,2,1,0:T(8,128)(2,1)S(1)}, u32[]{:S(2)}, u32[]{:S(2)}) collective-permute-start(bf16[2,8,144,256]{3,2,1,0:T(8,128)(2,1)S(1)} %get-tuple-element.57), channel_id=1, source_target_pairs={{0,1},{1,0},{2,3},{3,2},{4,5},{5,4},{6,7},{7,6},{8,9},{9,8},{10,11... | collective-permute-start | bytes 3538952 | tf_op jit(solution)/shard_map/ppermute | solution.py:331
  108.9 16.1 %collective-permute-start.15 = (bf16[64,256]{1,0:T(8,128)(2,1)S(1)}, bf16[64,256]{1,0:T(8,128)(2,1)S(1)}, u32[]{:S(2)}, u32[]{:S(2)}) collective-permute-start(bf16[64,256]{1,0:T(8,128)(2,1)S(1)} %get-tuple-element.48), channel_id=1, source_target_pairs={{0,1},{1,2},{2,3},{3,4},{4,5},{5,6},{6,7},{7,8},{8,9},{9,10},{10,1... | collective-permute-start | bytes 98312 | tf_op jit(solution)/shard_map/ppermute | solution.py:236
  110.8 14.2 %collective-permute-start.16 = (bf16[64,256]{1,0:T(8,128)(2,1)S(1)}, bf16[64,256]{1,0:T(8,128)(2,1)S(1)}, u32[]{:S(2)}, u32[]{:S(2)}) collective-permute-start(bf16[64,256]{1,0:T(8,128)(2,1)S(1)} %get-tuple-element.49), channel_id=1, source_target_pairs={{1,0},{2,1},{3,2},{4,3},{5,4},{6,5},{7,6},{8,7},{9,8},{10,9},{11,1... | collective-permute-start | bytes 98312 | tf_op jit(solution)/shard_map/ppermute | solution.py:237
  115.3 13.4 %collective-permute-start.22 = (bf16[2,2,144,256]{3,2,1,0:T(8,128)(2,1)S(1)}, bf16[2,2,144,256]{3,2,1,0:T(8,128)(2,1)S(1)}, u32[]{:S(2)}, u32[]{:S(2)}) collective-permute-start(bf16[2,2,144,256]{3,2,1,0:T(8,128)(2,1)S(1)} %get-tuple-element.59), channel_id=1, source_target_pairs={{0,4},{1,5},{2,6},{3,7},{4,0},{5,1},{6,2},{7,3},{8,12},{9,13},{10,... | collective-permute-start | bytes 884744 | tf_op jit(solution)/shard_map/ppermute | solution.py:334
  119.7 15.9 %collective-permute-start.23 = (bf16[2,2,144,256]{3,2,1,0:T(8,128)(2,1)S(1)}, bf16[2,2,144,256]{3,2,1,0:T(8,128)(2,1)S(1)}, u32[]{:S(2)}, u32[]{:S(2)}) collective-permute-start(bf16[2,2,144,256]{3,2,1,0:T(8,128)(2,1)S(1)} %get-tuple-element.60), channel_id=1, source_target_pairs={{0,2},{1,3},{2,4},{3,5},{4,6},{5,7},{6,0},{7,1},{8,10},{9,11},{10,... | collective-permute-start | bytes 884744 | tf_op jit(solution)/shard_map/ppermute | solution.py:334
  121.7 47.1 %collective-permute-start.20 = (bf16[2,512,256]{2,1,0:T(8,128)(2,1)S(1)}, bf16[2,512,256]{2,1,0:T(8,128)(2,1)S(1)}, u32[]{:S(2)}, u32[]{:S(2)}) collective-permute-start(bf16[2,512,256]{2,1,0:T(8,128)(2,1)S(1)} %get-tuple-element.55), channel_id=1, source_target_pairs={{0,240},{16,0},{32,16},{48,32},{64,48},{80,64},{96,80},{112,96},{1... | collective-permute-start | bytes 1572872 | tf_op jit(solution)/shard_map/ppermute | solution.py:245
  126.5 42.4 %collective-permute-start.17 = (bf16[2,512,256]{2,1,0:T(8,128)(2,1)S(1)}, bf16[2,512,256]{2,1,0:T(8,128)(2,1)S(1)}, u32[]{:S(2)}, u32[]{:S(2)}) collective-permute-start(bf16[2,512,256]{2,1,0:T(8,128)(2,1)S(1)} %get-tuple-element.50), channel_id=1, source_target_pairs={{0,16},{16,32},{32,48},{48,64},{64,80},{80,96},{96,112},{112,128},... | collective-permute-start | bytes 1572872 | tf_op jit(solution)/shard_map/ppermute | solution.py:245
  126.5 12.5 %collective-permute-start.24 = (bf16[2,2,144,256]{3,2,1,0:T(8,128)(2,1)S(1)}, bf16[2,2,144,256]{3,2,1,0:T(8,128)(2,1)S(1)}, u32[]{:S(2)}, u32[]{:S(2)}) collective-permute-start(bf16[2,2,144,256]{3,2,1,0:T(8,128)(2,1)S(1)} %get-tuple-element.61), channel_id=1, source_target_pairs={{0,6},{1,7},{2,0},{3,1},{4,2},{5,3},{6,4},{7,5},{8,14},{9,15},{10,... | collective-permute-start | bytes 884744 | tf_op jit(solution)/shard_map/ppermute | solution.py:334
  128.7 33.8 %collective-permute-start.19 = (bf16[512,256]{1,0:T(8,128)(2,1)S(1)}, bf16[512,256]{1,0:T(8,128)(2,1)S(1)}, u32[]{:S(2)}, u32[]{:S(2)}) collective-permute-start(bf16[512,256]{1,0:T(8,128)(2,1)S(1)} %slice_bitcast_fusion), channel_id=1, source_target_pairs={{16,0},{32,16},{48,32},{64,48},{80,64},{96,80},{112,96},{128,112},... | collective-permute-start | bytes 786440 | tf_op jit(solution)/shard_map/ppermute | solution.py:245
  135.5 32.4 %collective-permute-start.18 = (bf16[512,256]{1,0:T(8,128)(2,1)S(1)}, bf16[512,256]{1,0:T(8,128)(2,1)S(1)}, u32[]{:S(2)}, u32[]{:S(2)}) collective-permute-start(bf16[512,256]{1,0:T(8,128)(2,1)S(1)} %get-tuple-element.54), channel_id=1, source_target_pairs={{16,0},{32,16},{48,32},{64,48},{80,64},{96,80},{112,96},{128,112},... | collective-permute-start | bytes 786440 | tf_op jit(solution)/shard_map/ppermute | solution.py:245
  139.8 32.9 %collective-permute-start.25 = (bf16[2,144,256]{2,1,0:T(8,128)(2,1)S(1)}, bf16[2,144,256]{2,1,0:T(8,128)(2,1)S(1)}, u32[]{:S(2)}, u32[]{:S(2)}) collective-permute-start(bf16[2,144,256]{2,1,0:T(8,128)(2,1)S(1)} %get-tuple-element.63), channel_id=1, source_target_pairs={{0,8},{1,9},{2,10},{3,11},{4,12},{5,13},{6,14},{7,15},{8,0},{9,1},... | collective-permute-start | bytes 442376 | tf_op jit(solution)/shard_map/ppermute | solution.py:348
  (22 other events, 144.0 us)

commit v2 on v0

v2 whole, which is shorter than its diff:
```python
import functools

import jax
import jax.numpy as jnp
from jax import lax
from jax.experimental import pallas as pl
from jax.experimental.pallas import tpu as pltpu
from jax.sharding import PartitionSpec as P

F32 = jnp.float32
BF16 = jnp.bfloat16
ANY = pl.BlockSpec(memory_space=pl.ANY)
VMEM = pl.BlockSpec(memory_space=pltpu.VMEM)
SMEM = pl.BlockSpec(memory_space=pltpu.SMEM)
LITTLE = pl.CostEstimate(flops=1000, bytes_accessed=1000, transcendentals=0)


def shape(*dims, dtype=BF16):
    return jax.ShapeDtypeStruct(dims, dtype)


def last_section(at_ref):
    return at_ref[0] == at_ref[2] - 1


class View:
    def __init__(self, pieces, at_ref):
        self.pieces, self.at_ref = (pieces, at_ref)

    @property
    def ref(self):
        return self.pieces[0][0]

    def value(self):
        groups = []
        for ref, when in self.pieces:
            if when is None or not groups or groups[-1][0] is None:
                groups.append((None, [ref[...]]) if when is None else (0, ([], [])))
            if when is not None:
                groups[-1][1][int(when)].append(ref[...])
        parts = []
        for kind, group in groups:
            if kind is None:
                parts += group
            else:
                rest, last = (jnp.concatenate(g, 0) if len(g) > 1 else g[0] for g in group)
                parts.append(jnp.where(last_section(self.at_ref), last, rest))
        return parts[0] if len(parts) == 1 else jnp.concatenate(parts, 0)


def kernel(body, at, args, outs, scratch=(), after=(), mib=16):
    arrays = []

    def place(array):
        for i, a in enumerate(arrays):
            if a is array:
                return i
        arrays.append(array)
        return len(arrays) - 1

    plan = []
    for arg in args:
        if not isinstance(arg, list):
            arg = [(*(arg if isinstance(arg, tuple) else (arg, None)), None, None, None)]
        plan.append([(place(piece[0]), *piece[1:]) for piece in arg])
    after = [a for a in after if not any(a is b for b in arrays)]

    def run(*refs):
        at_ref, refs = (refs[len(after)], refs[len(after) + 1 :])
        views = []
        for pieces in plan:
            taken = []
            for i, index, start, size, when in pieces:
                ref = refs[i] if index is None else refs[i].at[index]
                taken.append((ref if start is None else ref.at[pl.ds(start, size)], when))
            views.append(View(taken, at_ref))
        refs = refs[len(arrays) :]
        body(at_ref, views, refs[: len(outs)], refs[len(outs) :])

    return pl.pallas_call(
        run,
        out_shape=outs,
        in_specs=[ANY] * len(after) + [SMEM] + [VMEM] * len(arrays),
        out_specs=[VMEM] * len(outs),
        scratch_shapes=list(scratch),
        compiler_params=pltpu.CompilerParams(vmem_limit_bytes=mib << 20),
        cost_estimate=LITTLE,
        name=getattr(body, "func", body).__name__,
    )(*after, at, *arrays)


def sigmoid(v):
    return 1.0 / (1.0 + jnp.exp(-v))


def act(v):
    v = v.astype(F32)
    return (v * sigmoid(v)).astype(BF16).astype(F32)


def slope(v):
    v = v.astype(F32)
    s = sigmoid(v)
    return s * (1.0 + v * (1.0 - s))


def stencil(x_ref, v, cols):
    n, ch = v.shape
    v = v.astype(F32)
    col = lax.rem(lax.broadcasted_iota(jnp.int32, (n, ch), 0), cols)
    x_ref[:n, :ch] = jnp.where(col == 0, 0.0, pltpu.roll(v, 1, 0)).astype(BF16)
    x_ref[:n, ch : 2 * ch] = v.astype(BF16)
    x_ref[:n, 2 * ch :] = jnp.where(col == cols - 1, 0.0, pltpu.roll(v, n - 1, 0)).astype(BF16)


def conv(x_ref, w_ref, cols, size):
    depth = x_ref.shape[1]
    total = None
    for a in range(3):
        term = jnp.dot(
            x_ref[a * cols : a * cols + size, :], w_ref[a * depth : (a + 1) * depth, :], preferred_element_type=F32
        )
        total = term if total is None else total + term
    return total


def correlate(x_ref, d, cols):
    size = d.shape[0]
    return [
        lax.dot_general(
            x_ref[a * cols : a * cols + size, :], d, (((0,), (0,)), ((), ())), preferred_element_type=F32
        )
        for a in range(3)
    ]


def inside_image(at_ref, values, margin):
    n = values.shape[0]
    pixel = lax.broadcasted_iota(jnp.int32, values.shape, 0)
    low = jnp.where(at_ref[1] == 0, margin, 0)
    high = jnp.where(at_ref[1] == at_ref[3] - 1, n - margin, n)
    return jnp.where((pixel >= low) & (pixel < high), values, jnp.zeros_like(values))


def flip(at_ref, args, outs, own):
    w_ref = args[0].ref
    ch = w_ref.shape[2]
    for k in (1, 0):
        for t in range(9):
            outs[0][k, (8 - t) * ch : (9 - t) * ch, :] = w_ref[k, t * ch : (t + 1) * ch, :].T


def pack(*refs):
    ins, outs = (refs[:-2], refs[-2:])
    half = len(ins) // 2
    for group, out in ((ins[:half], outs[0]), (ins[half:], outs[1])):
        end = 0
        for ref in group:
            size = ref.shape[-2]
            out[end : end + size] = ref[...].reshape(size, ref.shape[-1])
            end += size


def pick(at_ref, args, outs, own):
    for k, out in enumerate(outs):
        end = 0
        for arg in args[k * len(args) // len(outs) : (k + 1) * len(args) // len(outs)]:
            value = arg.value()
            out[end : end + value.shape[0]] = value
            end += value.shape[0]


def invert(cols, tick, at_ref, args, outs, own):
    y1, g2, y2, g1, w_f, w_g, t_f, t_g = args[:8]
    x_ref = own[0]
    y1, g2 = (y1.value(), g2.value())
    edge = 2 * cols
    wide = y1.shape[0] - edge
    size = wide - edge
    stencil(x_ref, act(y1), cols)
    q2 = (y2.value().astype(F32) - conv(x_ref, w_g.ref, cols, wide)).astype(BF16)
    q2 = inside_image(at_ref, q2, cols)
    outs[0][...] = q2
    stencil(x_ref, g2, cols)
    back = conv(x_ref, t_g.ref, cols, wide)
    h1 = (g1.value().astype(F32) + slope(y1[cols : cols + wide]) * back).astype(BF16)
    h1 = inside_image(at_ref, h1, cols)
    outs[1][...] = h1
    stencil(x_ref, act(q2), cols)
    p2 = (y1[edge : edge + size].astype(F32) - conv(x_ref, w_f.ref, cols, size)).astype(BF16)
    here = slice(cols, cols + size)
    stencil(x_ref, h1, cols)
    back = conv(x_ref, t_f.ref, cols, size)
    q2, h1 = (q2[here], h1[here])
    h2 = (g2[edge : edge + size].astype(F32) + slope(q2) * back).astype(BF16)
    if tick == 1:
        first = at_ref[0] == 0
        out, y_out, g_out = outs[2:]
        loss = args[8].ref
        out[0] = p2
        out[1] = q2
        out[2] = jnp.where(first, loss[0], h1)
        out[3] = jnp.where(first, loss[1], h2)
        y_out[...] = y1[cols : cols + wide]
        g_out[...] = g2[edge : edge + size]
    else:
        top, bottom = outs[2:4]
        inner = size - 2 * edge
        for k, (two, one) in enumerate(((p2, q2), (h2, h1))):
            at = k * edge
            top[at : at + edge] = two[:edge]
            bottom[at : at + edge] = two[size - edge :]
            at = 2 * edge + k * cols
            top[at : at + cols] = one[:cols]
            bottom[at : at + cols] = one[size - cols :]
            outs[4 + k][:inner] = two[edge : size - edge]
            outs[4 + k][inner:] = one[cols : size - cols]


def advance(cols, extra, at_ref, args, outs, own):
    q, p, w_f, w_g, new_q, new_p = args[:6]
    x_ref = own[0]
    q = q.value()
    edge = 2 * cols
    wide = q.shape[0] - edge
    size = wide - edge
    margin = extra * cols
    stencil(x_ref, act(q), cols)
    out1 = (p.value().astype(F32) + conv(x_ref, w_f.ref, cols, wide)).astype(BF16)
    out1 = inside_image(at_ref, out1, margin + cols)
    stencil(x_ref, act(out1), cols)
    out2 = (q[edge : edge + size].astype(F32) + conv(x_ref, w_g.ref, cols, size)).astype(BF16)
    adv, send = outs[:2]
    here = size - 2 * margin
    adv[0] = out1[cols + margin : cols + margin + here]
    adv[1] = out2[margin : margin + here]
    last = last_section(at_ref)
    if extra:
        out2 = inside_image(at_ref, out2, margin)
        send[:size] = jnp.where(last, new_q.value(), out2)
        rest = out1[margin : margin + here + edge]
        send[size:] = jnp.where(last, new_p.value(), rest)
        outs[2][...] = args[6].ref[...]
        outs[3][...] = args[7].ref[...]
    else:
        send[0] = jnp.where(last, new_p.value(), adv[0])
        send[1] = jnp.where(last, new_q.value(), out2)


def weight_terms(cols, at_ref, args, outs, own):
    x_ref = own[0]
    depth = x_ref.shape[1]
    for k, (v, d) in enumerate((args[2:4], args[0:2])):
        stencil(x_ref, act(v.value()), cols)
        for a, term in enumerate(correlate(x_ref, d.value(), cols)):
            outs[0][k, a * depth : (a + 1) * depth] = term


def weight_sums(cols, at_ref, args, outs, own):
    x_ref, total = own
    depth = x_ref.shape[1]
    even = lax.rem(at_ref[1], 2) == 0
    keep, send = outs
    rows = send.shape[2]
    before = args[4].ref
    for k, (v, d) in enumerate((args[2:4], args[0:2])):
        stencil(x_ref, act(v.value()), cols)
        for a, term in enumerate(correlate(x_ref, d.value(), cols)):
            part = slice(a * depth, (a + 1) * depth)
            total[part] = term + before[k, part]
        for j in range(send.shape[1]):
            one = total[2 * j * rows : (2 * j + 1) * rows]
            two = total[(2 * j + 1) * rows : (2 * j + 2) * rows]
            keep[k, j] = jnp.where(even, one, two)
            send[k, j] = jnp.where(even, two, one).astype(BF16)


def sum_cores(at_ref, args, outs, own):
    keep, came = (arg.ref for arg in args)
    x = lax.rem(at_ref[1] // 2, 4)
    for d, out in zip((0, 2, 1, 3), outs):
        to = lax.rem(x + d, 4)
        for k in range(2):
            for z in range(2):
                out[k, z] = (keep[k, 4 * z + to] + came[k, 4 * z + to].astype(F32)).astype(out.dtype)


def sum_chips(at_ref, args, outs, own):
    z = at_ref[1] // 8
    parts = [arg.ref for arg in args]
    for k in range(2):
        for out, at in ((outs[0], 1 - z), (outs[1], z)):
            value = parts[0][k, at]
            for part in parts[1:]:
                value = value + part[k, at].astype(F32)
            out[k] = value.astype(out.dtype)


def place_outputs(at_ref, ahead_ref, back_ref, adv_ref, forward_ref, returning_ref, backward_ref, sem):
    last = last_section(at_ref)
    ahead = pltpu.make_async_copy(ahead_ref, forward_ref, sem.at[0])
    back = pltpu.make_async_copy(back_ref.at[pl.ds(2, 2)], backward_ref, sem.at[1])
    came = pltpu.make_async_copy(back_ref.at[pl.ds(0, 2)], returning_ref, sem.at[2])
    own = pltpu.make_async_copy(adv_ref, returning_ref, sem.at[2])
    ahead.start()
    back.start()
    pl.when(last)(own.start)
    pl.when(jnp.logical_not(last))(came.start)
    ahead.wait()
    back.wait()
    came.wait()


def local(forward_state, returning_state, returning_grad, weights, fresh_input, loss_grad):
    full = forward_state.shape
    rows, cols, ch = full[2:]
    size = rows * cols
    edge = 2 * cols
    segments = lax.axis_size("segment")
    bands = lax.axis_size("band")
    seg = lax.axis_index("segment")
    at = jnp.stack([seg, lax.axis_index("band"), segments, bands]).astype(jnp.int32)

    def up_down(bottom, top):
        return (
            lax.ppermute(bottom, "band", [(i, i + 1) for i in range(bands - 1)]),
            lax.ppermute(top, "band", [(i + 1, i) for i in range(bands - 1)]),
        )

    back_route = [(i + 1, i) for i in range(segments - 1)]
    back_ring = [(i, (i - 1) % segments) for i in range(segments)]
    ahead_ring = [(i, (i + 1) % segments) for i in range(segments)]

    def along(block, route):
        return lax.ppermute(block, "segment", route)

    state = forward_state.reshape(2, size, ch)
    y = returning_state.reshape(2, size, ch)
    g = returning_grad.reshape(2, size, ch)
    fresh = fresh_input.reshape(4, size, ch)
    loss = loss_grad.reshape(2, 2, size, ch)
    w = weights[0]
    w_f, w_g = ((w, 0), (w, 1))

    def x_scratch(extra):
        return pltpu.VMEM((size + 2 * extra * cols, 3 * ch), BF16)

    pair = shape(2, size, ch)
    ext = shape(size + edge, ch)
    e6 = shape(6 * cols, ch)

    def pack_edges(parts):
        count = sum(n for _, _, n in parts) * cols

        def spec(index, n, last):
            start = (rows - n) * cols if last else 0
            return pl.BlockSpec((pl.Element(1), pl.Element(n * cols), pl.Element(ch)), lambda i: (index, start, 0))

        return pl.pallas_call(
            pack, grid=(1,), out_shape=[shape(count, ch)] * 2,
            in_specs=[spec(index, n, last) for last in (True, False) for _, index, n in parts],
            out_specs=[pl.BlockSpec((count, ch), lambda i: (0, 0))] * 2,
            compiler_params=pltpu.CompilerParams(vmem_limit_bytes=60 << 20), cost_estimate=LITTLE, name="pack_edges",
        )(*[array for array, _, _ in parts] * 2)

    up, down = up_down(*pack_edges([(y, 0, 2), (g, 1, 2), (y, 1, 1), (g, 0, 1), (fresh, 1, 2), (fresh, 0, 1)]))
    fwd_up, fwd_down = up_down(*pack_edges([(state, 1, 4), (state, 0, 3)]))
    (w_t,) = kernel(flip, at, (w,), (shape(2, 9 * ch, ch),))

    def extended(start, n, middle, up, down):
        start, n = (start * cols, n * cols)
        return [(up, None, start, n, None), *middle, (down, None, start, n, None)]

    def all_of(array, index):
        return [(array, index, 0, size, None)]

    mid = shape(2 * size - 6 * cols, ch)
    q2, h1, top, bottom, mid_y, mid_g = kernel(
        functools.partial(invert, cols, 0), at,
        (
            extended(0, 2, all_of(y, 0), up, down), extended(2, 2, all_of(g, 1), up, down),
            extended(4, 1, all_of(y, 1), up, down), extended(5, 1, all_of(g, 0), up, down),
            w_f, w_g, (w_t, 0), (w_t, 1),
        ),
        (ext, ext, e6, e6, mid, mid), [x_scratch(2)], (),
    )
    came_bottom = along(bottom, back_route)
    came_top = along(top, back_route)
    adv, ahead, mid_y, mid_g = kernel(
        functools.partial(advance, cols, 2), at,
        (
            extended(0, 4, all_of(state, 1), fwd_up, fwd_down), extended(4, 3, all_of(state, 0), fwd_up, fwd_down),
            w_f, w_g,
            extended(6, 2, all_of(fresh, 1), up, down), extended(8, 1, all_of(fresh, 0), up, down), mid_y, mid_g,
        ),
        (pair, shape(2 * size + 6 * cols, ch), mid, mid), [x_scratch(4)], (top,),
    )
    came_mids = (along(mid_y, back_route), along(mid_g, back_route))
    state = along(ahead, ahead_ring)
    (terms,) = kernel(
        functools.partial(weight_terms, cols), at,
        (
            [(up, None, cols, cols, None), (y, 0, 0, size, None), (down, None, 0, cols, None)], (g, 1),
            q2, [(h1, None, cols, size, None)],
        ),
        (shape(2, 9 * ch, ch, dtype=F32),), [x_scratch(1)], (adv,),
    )
    (w_t,) = kernel(flip, at, (w,), (shape(2, 9 * ch, ch),), after=(terms,))

    spans = ((0, 2, adv, 0), (2, 2, loss, (0, 1)), (4, 1, adv, 1), (5, 1, loss, (0, 0)))
    picks = [
        [
            (came, None, start * cols, n * cols, False),
            (own, index, size - n * cols if came is came_bottom else 0, n * cols, True),
        ]
        for came in (came_bottom, came_top)
        for start, n, own, index in spans
    ]
    bottom, top = kernel(pick, at, picks, (e6, e6))
    up, down = up_down(bottom, top)
    inner, outer = (size - 2 * edge, size - edge)

    def came_field(k):
        start, n, own, index = spans[k]
        mid = came_mids[k % 2]
        return extended(start, n, [
            (came_top, None, start * cols, n * cols, False),
            (mid, None, 0, inner, False) if k < 2 else (mid, None, inner, outer, False),
            (came_bottom, None, start * cols, n * cols, False), (own, index, 0, size, True),
        ], up, down)

    q2, h1, back, y1, g2 = kernel(
        functools.partial(invert, cols, 1), at,
        (
            *[came_field(k) for k in range(4)], w_f, w_g, (w_t, 0), (w_t, 1), (loss, 1),
        ),
        (ext, ext, shape(4, size, ch), ext, shape(size, ch)), [x_scratch(2)],
    )
    came_back = along(back, back_ring)
    part = 9 * ch // bands
    chunks = (2, 8, part, ch)
    keep, send = kernel(
        functools.partial(weight_sums, cols), at, (y1, g2, q2, [(h1, None, cols, size, None)], terms),
        (shape(*chunks, dtype=F32), shape(*chunks)), [x_scratch(1), pltpu.VMEM((9 * ch, ch), F32)], (back,),
    )
    adv, ahead = kernel(
        functools.partial(advance, cols, 0), at,
        (
            [(state, None, 0, size + 2 * edge, None)], [(state, None, size + 2 * edge, size + edge, None)], w_f, w_g,
            (fresh, 3), (fresh, 2),
        ),
        (pair, pair), [x_scratch(2)], (send,),
    )
    came_ahead = along(ahead, ahead_ring)

    def on_x(piece, step):
        return lax.ppermute(
            piece, "band", [(i, (i & 8) | ((((i >> 1) & 3) + step) % 4) << 1 | (i & 1)) for i in range(bands)]
        )

    def over_bands(send, keep, at):
        came = lax.ppermute(send, "band", [(i, i ^ 1) for i in range(bands)])
        quarter = shape(2, 2, part, ch)
        own, far, right, left = kernel(
            sum_cores, at, (keep, came), (shape(2, 2, part, ch, dtype=F32), quarter, quarter, quarter)
        )
        far, right, left = (on_x(far, 2), on_x(right, 1), on_x(left, 3))
        send, keep = kernel(
            sum_chips, at, (own, far, right, left), (shape(2, part, ch), shape(2, part, ch, dtype=F32))
        )
        return keep + lax.ppermute(send, "band", [(i, i ^ 8) for i in range(bands)]).astype(F32)

    send, keep, _ = lax.optimization_barrier((send, keep, adv))
    weight_grad = lax.cond(seg < segments, over_bands, lambda *_: jnp.zeros((2, part, ch), F32), send, keep, at)

    outputs = pl.pallas_call(
        place_outputs, out_shape=[pair] * 3, in_specs=[SMEM] + [VMEM] * 3, out_specs=[ANY] * 3,
        scratch_shapes=[pltpu.SemaphoreType.DMA((3,))], cost_estimate=LITTLE,
        compiler_params=pltpu.CompilerParams(vmem_limit_bytes=8 << 20), name="place_outputs",
    )(at, came_ahead, came_back, adv)
    return (*[out.reshape(full) for out in outputs], weight_grad[None])


def solution(mesh):
    return jax.shard_map(
        local,
        mesh=mesh,
        in_specs=(
            P("segment", None, "band", None, None),
            P("segment", None, "band", None, None),
            P("segment", None, "band", None, None),
            P("segment", None, None, None),
            P(None, None, "band", None, None),
            P(None, None, "band", None, None),
        ),
        out_specs=(
            P("segment", None, "band", None, None),
            P("segment", None, "band", None, None),
            P("segment", None, "band", None, None),
            P("segment", None, "band", None),
        ),
        check_vma=False,
    )
```

time: 282 us -> 135 us (0.48); the launches traced: 277 us -> 135 us
  waiting for transfers between devices: 107 us -> 38.2 us
  starting transfers between devices: 96.9 us -> 59.4 us
  Pallas kernels: 0 us -> 35.1 us
  other arithmetic: 20.7 us -> 0.11 us
  local copies, waits for them, and re-layouts: 20.9 us -> 0.84 us
  matrix products: 15.7 us -> 0 us
  between operations: 15.8 us -> 1.08 us
    reduce_scatter x2 -> x0, waiting for transfers between devices: 55.6 us -> none  [local(): lax.psum_scatter(wgrad.astype(jnp.bfloat16), 'band', scatter_dimension=1,...]
    ppermute x30 -> x18, starting transfers between devices: 96.9 us -> 59.4 us  [the longest x7 23.7 us: along(): return lax.ppermute(block, 'segment', route)]
    pallas_call x0 -> x14, Pallas kernels: none -> 35.1 us  [the longest x11 29.4 us: kernel(): pl.pallas_call(run, out_shape=outs, in_specs=[ANY] * len(after) + [SMEM]...]
    dot_general x16 -> x0, matrix products: 15.7 us -> none  [the longest x12 12.4 us: apply_taps(): return jnp.dot(taps_matrix, weight, preferred_element_type=jnp.float32)]
    ppermute x30 -> x18, waiting for transfers between devices: 51.2 us -> 38.2 us  [the longest x1 14.2 us: over_bands(): lax.ppermute(send, 'band', [(i, i ^ 8) for i in range(bands)]).astype(F32)]
    unnamed x115 -> x20, local copies, waits for them, and re-layouts: 12.4 us -> 0.84 us
    broadcast_in_dim x4 -> x1, other arithmetic: 5.48 us -> 0.03 us  [local(): return (*[out.reshape(full) for out in outputs], weight_grad[None])]
    another operation x6 -> x1, other arithmetic: 5.04 us -> 0.08 us  [local(): jnp.stack([seg, lax.axis_index('band'), segments, bands]).astype(jnp.int32)]
  transfers between devices with their start and end apart: 32 -> 18, of which waited for: 5 -> 7; matrix products, arithmetic and copies ran while one was open for 18% -> 0% of each run, Pallas kernels for 0% -> 23%
where the time goes in v2:
time: 135 us
  starting transfers between devices  59.4 us (44%)
  waiting for transfers between devices  38.2 us (28%)
  Pallas kernels  35.1 us (26%)
    pallas_call x11, Pallas kernels, kernel(): pl.pallas_call(run, out_shape=outs, in_specs=[ANY] * len(after) + [SMEM]...  29.4 us
    ppermute x7, starting transfers between devices, along(): return lax.ppermute(block, 'segment', route)  23.7 us
    ppermute x3, starting transfers between devices, up_down(): lax.ppermute(top, 'band', [(i + 1, i) for i in range(bands - 1)])  22.3 us
    ppermute x1, waiting for transfers between devices, over_bands(): lax.ppermute(send, 'band', [(i, i ^ 8) for i in range(bands)]).astype(F32)  14.2 us
    ppermute x3, waiting for transfers between devices, on_x(): lax.ppermute(piece, 'band', [(i, i & 8 | ((i >> 1 & 3) + step) % 4 << 1 |...  11.8 us
    ppermute x7, waiting for transfers between devices, along(): return lax.ppermute(block, 'segment', route)  9.07 us
    ppermute x3, starting transfers between devices, up_down(): lax.ppermute(bottom, 'band', [(i, i + 1) for i in range(bands - 1)])  5.74 us
    ppermute x3, starting transfers between devices, on_x(): lax.ppermute(piece, 'band', [(i, i & 8 | ((i >> 1 & 3) + step) % 4 << 1 |...  5.11 us
  transfers between devices with their start and end apart: 18, of which 7 were waited for; matrix products, arithmetic and copies ran while one was open for 0% of the time, Pallas kernels for 23%

profile of v2, /device:TPU:18, one launch (start us, length us, event | category | flops | bytes accessed | tf_op | source)
XLA Modules:
  0.0 134.7 jit_solution(16749704512526561965)
XLA Ops:
  0.6 2.1 %pack_edges.2 = (bf16[576,256]{1,0:T(8,128)(2,1)}, bf16[576,256]{1,0:T(8,128)(2,1)}) custom-call(bf16[2,512,256]{2,1,0:T(8,128)(2,1)} %bitcast.25, bf16[2,512,256]{2,1,0:T(8,128)(2,1)} %bitcast.31, bf16[2,512,256]{2,1,0:T(8,128)(2,1)} %bitcast.26, bf16[2,512,256]{2,1,0:T(8,128)(2,1)} %bitcast.32, bf16[4,512,256]{2,1,0:T(8,128)(2,1)} %bitcast.19, ...), custom_call_target="tpu_custom_call" | custom-call | flops 1000 | bytes 1000 | tf_op jit(solution)/shard_map/pack_edges/pallas_call | solution.py:359
  4.6 3.6 %collective-permute-start.6 = (bf16[576,256]{1,0:T(8,128)(2,1)}, bf16[576,256]{1,0:T(8,128)(2,1)S(1)}, u32[]{:S(2)}, u32[]{:S(2)}) collective-permute-start(bf16[576,256]{1,0:T(8,128)(2,1)} %get-tuple-element.54), channel_id=1, source_target_pairs={{1,0},{2,1},{3,2},{4,3},{5,4},{6,5},{7,6},{8,7},{9,8},{10,9},{11,1... | collective-permute-start | bytes 884744 | tf_op jit(solution)/shard_map/ppermute | solution.py:327
  12.0 3.6 %collective-permute-start.9 = (bf16[448,256]{1,0:T(8,128)(2,1)}, bf16[448,256]{1,0:T(8,128)(2,1)S(1)}, u32[]{:S(2)}, u32[]{:S(2)}) collective-permute-start(bf16[448,256]{1,0:T(8,128)(2,1)} %get-tuple-element.58), channel_id=1, source_target_pairs={{1,0},{2,1},{3,2},{4,3},{5,4},{6,5},{7,6},{8,7},{9,8},{10,9},{11,1... | collective-permute-start | bytes 688136 | tf_op jit(solution)/shard_map/ppermute | solution.py:327
  17.1 4.0 %invert.2 = (bf16[640,256]{1,0:T(8,128)(2,1)S(1)}, bf16[640,256]{1,0:T(8,128)(2,1)S(1)}, bf16[384,256]{1,0:T(8,128)(2,1)S(1)}, bf16[384,256]{1,0:T(8,128)(2,1)S(...) custom-call(s32[4]{0:T(128)S(1)} %pad_add_fusion.refs_0_.refs_1_.at_ref, ...), custom_call_target="tpu_custom_call" | custom-call | flops 1000 | bytes 1000 | tf_op jit(solution)/shard_map/invert/pallas_call | solution.py:80
  21.1 8.1 %collective-permute-start.7 = (bf16[384,256]{1,0:T(8,128)(2,1)S(1)}, bf16[384,256]{1,0:T(8,128)(2,1)S(1)}, u32[]{:S(2)}, u32[]{:S(2)}) collective-permute-start(bf16[384,256]{1,0:T(8,128)(2,1)S(1)} %get-tuple-element.55), channel_id=1, source_target_pairs={{16,0},{32,16},{48,32},{64,48},{80,64},{96,80},{112,96},{128,112},... | collective-permute-start | bytes 589832 | tf_op jit(solution)/shard_map/ppermute | solution.py:335
  29.2 3.4 %collective-permute-start.10 = (bf16[384,256]{1,0:T(8,128)(2,1)S(1)}, bf16[384,256]{1,0:T(8,128)(2,1)S(1)}, u32[]{:S(2)}, u32[]{:S(2)}) collective-permute-start(bf16[384,256]{1,0:T(8,128)(2,1)S(1)} %get-tuple-element.56.refs_0_), channel_id=1, source_target_pairs={{16,0},{32,16},{48,32},{64,48},{80,64},{96,80},{112,96},{128,112},... | collective-permute-start | bytes 589832 | tf_op jit(solution)/shard_map/ppermute | solution.py:335
  32.6 4.7 %advance.2 = (bf16[2,512,256]{2,1,0:T(8,128)(2,1)S(1)}, bf16[1408,256]{1,0:T(8,128)(2,1)S(1)}, bf16[640,256]{1,0:T(8,128)(2,1)S(1)}, bf16[640,256]{1,0:T(8,128)(2,1)S(1)}) custom-call(bf16[384,256]{1,0:T(8,128)(2,1)S(1)} %get-tuple-element.56.refs_0_, s32[4]{0:T(128)S(1)} %pad_add_fusion.refs_0_.refs_1_.at_ref, ...), custom_call_target="tpu_custom_call" | custom-call | flops 1000 | bytes 1000 | tf_op jit(solution)/shard_map/advance/pallas_call | solution.py:80
  41.2 3.0 %collective-permute-start.15 = (bf16[1408,256]{1,0:T(8,128)(2,1)S(1)}, bf16[1408,256]{1,0:T(8,128)(2,1)S(1)}, u32[]{:S(2)}, u32[]{:S(2)}) collective-permute-start(bf16[1408,256]{1,0:T(8,128)(2,1)S(1)} %get-tuple-element.74), channel_id=1, source_target_pairs={{0,16},{16,32},{32,48},{48,64},{64,80},{80,96},{96,112},{112,128},... | collective-permute-start | bytes 2162696 | tf_op jit(solution)/shard_map/ppermute | solution.py:335
  44.2 3.0 %collective-permute-done.10.refs_4_.refs_2_ = bf16[384,256]{1,0:T(8,128)(2,1)S(1)} collective-permute-done((bf16[384,256]{1,0:T(8,128)(2,1)S(1)}, bf16[384,256]{1,0:T(8,128)(2,1)S(1)}, u32[]{:S(2)}, u32[]{:S(2)}) %collective-permute-start.10) | collective-permute-done | bytes 196640 | tf_op jit(solution)/shard_map/ppermute | solution.py:335
  49.7 15.0 %collective-permute-start.13 = (bf16[384,256]{1,0:T(8,128)(2,1)S(1)}, bf16[384,256]{1,0:T(8,128)(2,1)S(1)}, u32[]{:S(2)}, u32[]{:S(2)}) collective-permute-start(bf16[384,256]{1,0:T(8,128)(2,1)S(1)} %get-tuple-element.64), channel_id=1, source_target_pairs={{1,0},{2,1},{3,2},{4,3},{5,4},{6,5},{7,6},{8,7},{9,8},{10,9},{11,1... | collective-permute-start | bytes 589832 | tf_op jit(solution)/shard_map/ppermute | solution.py:327
  64.8 2.1 %weight_terms.1.refs_0_.refs_6_ = f32[2,2304,256]{2,1,0:T(8,128)S(1)} custom-call(bf16[2,512,256]{2,1,0:T(8,128)(2,1)S(1)} %get-tuple-element.61.refs_2_.refs_0_.refs_5_, s32[4]{0:T(128)S(1)} %pad_add_fusion.refs_0_.refs_1_.at_ref, bf16[576,256]{1,0:T(8,128)(2,1)S(1)} %collective-permute-done.5.refs_1_.refs_6_.refs_2_, bf16[2,512,256]{2,1,0:T(8,128)(2,1)S(1)} %bitcast.30, ...), custom_call_target="tpu_custom_call" | custom-call | flops 1000 | bytes 1000 | tf_op jit(solution)/shard_map/weight_terms/pallas_call | solution.py:80
  68.1 6.0 %collective-permute-done.14.refs_7_ = bf16[640,256]{1,0:T(8,128)(2,1)S(1)} collective-permute-done((bf16[640,256]{1,0:T(8,128)(2,1)S(1)}, bf16[640,256]{1,0:T(8,128)(2,1)S(1)}, u32[]{:S(2)}, u32[]{:S(2)}) %collective-permute-start.14) | collective-permute-done | bytes 327712 | tf_op jit(solution)/shard_map/ppermute | solution.py:335
  74.1 5.1 %invert.3 = (bf16[640,256]{1,0:T(8,128)(2,1)S(1)}, bf16[640,256]{1,0:T(8,128)(2,1)S(1)}, bf16[4,512,256]{2,1,0:T(8,128)(2,1)}, bf16[640,256]{1,0:T(8,128)(2,1)S(1)}, bf16[512,256]{1,0:T(8,128)(2,1)S(1)}) custom-call(s32[4]{0:T(128)S(1)} %pad_add_fusion.refs_0_.refs_1_.at_ref, bf16[384,256]{1,0:T(8,128)(2,1)S(1)} %collective-permute-done.11.refs_1_, ...), custom_call_target="tpu_custom_call" | custom-call | flops 1000 | bytes 1000 | tf_op jit(solution)/shard_map/invert/pallas_call | solution.py:80
  79.2 5.5 %collective-permute-start.17 = (bf16[4,512,256]{2,1,0:T(8,128)(2,1)}, bf16[4,512,256]{2,1,0:T(8,128)(2,1)S(1)}, u32[]{:S(2)}, u32[]{:S(2)}) collective-permute-start(bf16[4,512,256]{2,1,0:T(8,128)(2,1)} %get-tuple-element.68.refs_0_), channel_id=1, source_target_pairs={{0,240},{16,0},{32,16},{48,32},{64,48},{80,64},{96,80},{112,96},{1... | collective-permute-start | bytes 3145736 | tf_op jit(solution)/shard_map/ppermute | solution.py:335
  84.6 3.6 %weight_sums.1 = (f32[2,8,144,256]{3,2,1,0:T(8,128)}, bf16[2,8,144,256]{3,2,1,0:T(8,128)(2,1)S(1)}) custom-call(bf16[4,512,256]{2,1,0:T(8,128)(2,1)} %get-tuple-element.68.refs_0_, s32[4]{0:T(128)S(1)} %pad_add_fusion.refs_0_.refs_1_.at_ref, bf16[640,256]{1,0:T(8,128)(2,1)S(1)} %get-tuple-element.69.refs_2_, bf16[512,256]{1,0:T(8,128)(2,1)S(1)} %get-tuple-element.70.refs_3_, ...), custom_call_target="tpu_custom_call" | custom-call | flops 1000 | bytes 1000 | tf_op jit(solution)/shard_map/weight_sums/pallas_call | solution.py:80
  88.2 4.4 %advance.3 = (bf16[2,512,256]{2,1,0:T(8,128)(2,1)S(1)}, bf16[2,512,256]{2,1,0:T(8,128)(2,1)}) custom-call(bf16[2,8,144,256]{3,2,1,0:T(8,128)(2,1)S(1)} %get-tuple-element.81.refs_0_, s32[4]{0:T(128)S(1)} %pad_add_fusion.refs_0_.refs_1_.at_ref, bf16[1408,256]{1,0:T(8,128)(2,1)S(1)} %collective-permute-done.15.refs_2_, bf16[2,2304,256]{2,1,0:T(8,128)(2,1)S(1)} %bitcast.18, ...), custom_call_target="tpu_custom_call" | custom-call | flops 1000 | bytes 1000 | tf_op jit(solution)/shard_map/advance/pallas_call | solution.py:80
  93.4 39.4 %conditional.1 = (f32[1,2,144,256]{3,2,1,0:T(8,128)S(1)}) conditional(s32[]{:T(128)} %convert_element_type.6, () %tuple.17, (bf16[2,8,144,256]{3,2,1,0:T(8,128)(2,1)}, s32[4]{0:T(128)S(1)}, f32[2,8,144,256]{3,2,1,0:T(8,128)}) %tuple.23), branch_computations={%region_0.0_spmd, %region_1.0_spmd} | conditional | flops 149456 | bytes 9586848 | solution.py:474
  93.4 3.1 %collective-permute-done.refs_2_ = bf16[2,8,144,256]{3,2,1,0:T(8,128)(2,1)S(1)} collective-permute-done((bf16[2,8,144,256]{3,2,1,0:T(8,128)(2,1)}, bf16[2,8,144,256]{3,2,1,0:T(8,128)(2,1)S(1)}, u32[]{:S(2)}, u32[]{:S(2)}) %collective-permute-start) | collective-permute-done | bytes 1179680 | tf_op jit(solution)/shard_map/cond/branch_1_fun/ppermute | solution.py:462
  98.4 3.1 %collective-permute-start.1 = (bf16[2,2,144,256]{3,2,1,0:T(8,128)(2,1)S(1)}, bf16[2,2,144,256]{3,2,1,0:T(8,128)(2,1)S(1)}, u32[]{:S(2)}, u32[]{:S(2)}) collective-permute-start(bf16[2,2,144,256]{3,2,1,0:T(8,128)(2,1)S(1)} %get-tuple-element.14), channel_id=1, source_target_pairs={{0,4},{1,5},{2,6},{3,7},{4,0},{5,1},{6,2},{7,3},{8,12},{9,13},{10,... | collective-permute-start | bytes 884744 | tf_op jit(solution)/shard_map/cond/branch_1_fun/ppermute | solution.py:457
  101.5 2.0 %collective-permute-start.3 = (bf16[2,2,144,256]{3,2,1,0:T(8,128)(2,1)S(1)}, bf16[2,2,144,256]{3,2,1,0:T(8,128)(2,1)S(1)}, u32[]{:S(2)}, u32[]{:S(2)}) collective-permute-start(bf16[2,2,144,256]{3,2,1,0:T(8,128)(2,1)S(1)} %get-tuple-element.16), channel_id=1, source_target_pairs={{0,6},{1,7},{2,0},{3,1},{4,2},{5,3},{6,4},{7,5},{8,14},{9,15},{10,... | collective-permute-start | bytes 884744 | tf_op jit(solution)/shard_map/cond/branch_1_fun/ppermute | solution.py:457
  103.5 6.4 %collective-permute-done.1.refs_2_ = bf16[2,2,144,256]{3,2,1,0:T(8,128)(2,1)S(1)} collective-permute-done((bf16[2,2,144,256]{3,2,1,0:T(8,128)(2,1)S(1)}, bf16[2,2,144,256]{3,2,1,0:T(8,128)(2,1)S(1)}, u32[]{:S(2)}, u32[]{:S(2)}) %collective-permute-start.1) | collective-permute-done | bytes 294944 | tf_op jit(solution)/shard_map/cond/branch_1_fun/ppermute | solution.py:457
  109.9 5.2 %collective-permute-done.2.refs_3_ = bf16[2,2,144,256]{3,2,1,0:T(8,128)(2,1)S(1)} collective-permute-done((bf16[2,2,144,256]{3,2,1,0:T(8,128)(2,1)S(1)}, bf16[2,2,144,256]{3,2,1,0:T(8,128)(2,1)S(1)}, u32[]{:S(2)}, u32[]{:S(2)}) %collective-permute-start.2) | collective-permute-done | bytes 294944 | tf_op jit(solution)/shard_map/cond/branch_1_fun/ppermute | solution.py:457
  116.0 2.5 %collective-permute-start.4 = (bf16[2,144,256]{2,1,0:T(8,128)(2,1)S(1)}, bf16[2,144,256]{2,1,0:T(8,128)(2,1)S(1)}, u32[]{:S(2)}, u32[]{:S(2)}) collective-permute-start(bf16[2,144,256]{2,1,0:T(8,128)(2,1)S(1)} %get-tuple-element.18), channel_id=1, source_target_pairs={{0,8},{1,9},{2,10},{3,11},{4,12},{5,13},{6,14},{7,15},{8,0},{9,1},... | collective-permute-start | bytes 442376 | tf_op jit(solution)/shard_map/cond/branch_1_fun/ppermute | solution.py:471
  118.5 14.2 %collective-permute-done.4 = bf16[2,144,256]{2,1,0:T(8,128)(2,1)S(1)} collective-permute-done((bf16[2,144,256]{2,1,0:T(8,128)(2,1)S(1)}, bf16[2,144,256]{2,1,0:T(8,128)(2,1)S(1)}, u32[]{:S(2)}, u32[]{:S(2)}) %collective-permute-start.4) | collective-permute-done | bytes 147488 | tf_op jit(solution)/shard_map/cond/branch_1_fun/ppermute | solution.py:471
  (50 shorter events, 19.9 us)
Async XLA Ops:
  0.6 15.2 %copy-start = (bf16[1,2,2304,256]{3,2,1,0:T(8,128)(2,1)S(1)}, bf16[1,2,2304,256]{3,2,1,0:T(8,128)(2,1)}, u32[]{:S(2)}) copy-start(bf16[1,2,2304,256]{3,2,1,0:T(8,128)(2,1)} %param.11) | copy-start | bytes 7077892
  2.7 14.3 %collective-permute-start.5 = (bf16[576,256]{1,0:T(8,128)(2,1)}, bf16[576,256]{1,0:T(8,128)(2,1)S(1)}, u32[]{:S(2)}, u32[]{:S(2)}) collective-permute-start(bf16[576,256]{1,0:T(8,128)(2,1)} %get-tuple-element.53), channel_id=1, source_target_pairs={{0,1},{1,2},{2,3},{3,4},{4,5},{5,6},{6,7},{7,8},{8,9},{9,10},{10,1... | collective-permute-start | bytes 884744 | tf_op jit(solution)/shard_map/ppermute | solution.py:326
  4.6 12.4 %collective-permute-start.6 = (bf16[576,256]{1,0:T(8,128)(2,1)}, bf16[576,256]{1,0:T(8,128)(2,1)S(1)}, u32[]{:S(2)}, u32[]{:S(2)}) collective-permute-start(bf16[576,256]{1,0:T(8,128)(2,1)} %get-tuple-element.54), channel_id=1, source_target_pairs={{1,0},{2,1},{3,2},{4,3},{5,4},{6,5},{7,6},{8,7},{9,8},{10,9},{11,1... | collective-permute-start | bytes 884744 | tf_op jit(solution)/shard_map/ppermute | solution.py:327
  10.1 22.4 %collective-permute-start.8 = (bf16[448,256]{1,0:T(8,128)(2,1)}, bf16[448,256]{1,0:T(8,128)(2,1)S(1)}, u32[]{:S(2)}, u32[]{:S(2)}) collective-permute-start(bf16[448,256]{1,0:T(8,128)(2,1)} %get-tuple-element.57), channel_id=1, source_target_pairs={{0,1},{1,2},{2,3},{3,4},{4,5},{5,6},{6,7},{7,8},{8,9},{9,10},{10,1... | collective-permute-start | bytes 688136 | tf_op jit(solution)/shard_map/ppermute | solution.py:326
  12.0 20.5 %collective-permute-start.9 = (bf16[448,256]{1,0:T(8,128)(2,1)}, bf16[448,256]{1,0:T(8,128)(2,1)S(1)}, u32[]{:S(2)}, u32[]{:S(2)}) collective-permute-start(bf16[448,256]{1,0:T(8,128)(2,1)} %get-tuple-element.58), channel_id=1, source_target_pairs={{1,0},{2,1},{3,2},{4,3},{5,4},{6,5},{7,6},{8,7},{9,8},{10,9},{11,1... | collective-permute-start | bytes 688136 | tf_op jit(solution)/shard_map/ppermute | solution.py:327
  17.0 15.6 %copy-start.1 = (bf16[2,2,8,64,256]{4,3,2,1,0:T(8,128)(2,1)S(1)}, bf16[2,2,8,64,256]{4,3,2,1,0:T(8,128)(2,1)}, u32[]{:S(2)}) copy-start(bf16[2,2,8,64,256]{4,3,2,1,0:T(8,128)(2,1)} %param.12) | copy-start | bytes 3145732
  17.0 15.6 %copy-start.4 = (bf16[1,2,8,64,256]{4,3,2,1,0:T(8,128)(2,1)S(1)}, bf16[1,2,8,64,256]{4,3,2,1,0:T(8,128)(2,1)}, u32[]{:S(2)}) copy-start(bf16[1,2,8,64,256]{4,3,2,1,0:T(8,128)(2,1)} %param.8) | copy-start | bytes 1572868
  21.1 23.1 %collective-permute-start.7 = (bf16[384,256]{1,0:T(8,128)(2,1)S(1)}, bf16[384,256]{1,0:T(8,128)(2,1)S(1)}, u32[]{:S(2)}, u32[]{:S(2)}) collective-permute-start(bf16[384,256]{1,0:T(8,128)(2,1)S(1)} %get-tuple-element.55), channel_id=1, source_target_pairs={{16,0},{32,16},{48,32},{64,48},{80,64},{96,80},{112,96},{128,112},... | collective-permute-start | bytes 589832 | tf_op jit(solution)/shard_map/ppermute | solution.py:335
  29.2 18.0 %collective-permute-start.10 = (bf16[384,256]{1,0:T(8,128)(2,1)S(1)}, bf16[384,256]{1,0:T(8,128)(2,1)S(1)}, u32[]{:S(2)}, u32[]{:S(2)}) collective-permute-start(bf16[384,256]{1,0:T(8,128)(2,1)S(1)} %get-tuple-element.56.refs_0_), channel_id=1, source_target_pairs={{16,0},{32,16},{48,32},{64,48},{80,64},{96,80},{112,96},{128,112},... | collective-permute-start | bytes 589832 | tf_op jit(solution)/shard_map/ppermute | solution.py:335
  32.6 14.6 %copy-start.5 = (bf16[2,2,8,64,256]{4,3,2,1,0:T(8,128)(2,1)S(1)}, bf16[2,2,8,64,256]{4,3,2,1,0:T(8,128)(2,1)}, u32[]{:S(2)}) copy-start(bf16[2,2,8,64,256]{4,3,2,1,0:T(8,128)(2,1)} %param.13) | copy-start | bytes 3145732
  37.4 30.7 %collective-permute-start.12 = (bf16[640,256]{1,0:T(8,128)(2,1)S(1)}, bf16[640,256]{1,0:T(8,128)(2,1)S(1)}, u32[]{:S(2)}, u32[]{:S(2)}) collective-permute-start(bf16[640,256]{1,0:T(8,128)(2,1)S(1)} %get-tuple-element.63), channel_id=1, source_target_pairs={{16,0},{32,16},{48,32},{64,48},{80,64},{96,80},{112,96},{128,112},... | collective-permute-start | bytes 983048 | tf_op jit(solution)/shard_map/ppermute | solution.py:335
  39.3 34.8 %collective-permute-start.14 = (bf16[640,256]{1,0:T(8,128)(2,1)S(1)}, bf16[640,256]{1,0:T(8,128)(2,1)S(1)}, u32[]{:S(2)}, u32[]{:S(2)}) collective-permute-start(bf16[640,256]{1,0:T(8,128)(2,1)S(1)} %get-tuple-element.65), channel_id=1, source_target_pairs={{16,0},{32,16},{48,32},{64,48},{80,64},{96,80},{112,96},{128,112},... | collective-permute-start | bytes 983048 | tf_op jit(solution)/shard_map/ppermute | solution.py:335
  41.2 47.0 %collective-permute-start.15 = (bf16[1408,256]{1,0:T(8,128)(2,1)S(1)}, bf16[1408,256]{1,0:T(8,128)(2,1)S(1)}, u32[]{:S(2)}, u32[]{:S(2)}) collective-permute-start(bf16[1408,256]{1,0:T(8,128)(2,1)S(1)} %get-tuple-element.74), channel_id=1, source_target_pairs={{0,16},{16,32},{32,48},{48,64},{64,80},{80,96},{96,112},{112,128},... | collective-permute-start | bytes 2162696 | tf_op jit(solution)/shard_map/ppermute | solution.py:335
  47.8 26.3 %collective-permute-start.11 = (bf16[384,256]{1,0:T(8,128)(2,1)S(1)}, bf16[384,256]{1,0:T(8,128)(2,1)S(1)}, u32[]{:S(2)}, u32[]{:S(2)}) collective-permute-start(bf16[384,256]{1,0:T(8,128)(2,1)S(1)} %get-tuple-element.62), channel_id=1, source_target_pairs={{0,1},{1,2},{2,3},{3,4},{4,5},{5,6},{6,7},{7,8},{8,9},{9,10},{10,1... | collective-permute-start | bytes 589832 | tf_op jit(solution)/shard_map/ppermute | solution.py:326
  49.7 24.4 %collective-permute-start.13 = (bf16[384,256]{1,0:T(8,128)(2,1)S(1)}, bf16[384,256]{1,0:T(8,128)(2,1)S(1)}, u32[]{:S(2)}, u32[]{:S(2)}) collective-permute-start(bf16[384,256]{1,0:T(8,128)(2,1)S(1)} %get-tuple-element.64), channel_id=1, source_target_pairs={{1,0},{2,1},{3,2},{4,3},{5,4},{6,5},{7,6},{8,7},{9,8},{10,9},{11,1... | collective-permute-start | bytes 589832 | tf_op jit(solution)/shard_map/ppermute | solution.py:327
  79.2 53.6 %collective-permute-start.17 = (bf16[4,512,256]{2,1,0:T(8,128)(2,1)}, bf16[4,512,256]{2,1,0:T(8,128)(2,1)S(1)}, u32[]{:S(2)}, u32[]{:S(2)}) collective-permute-start(bf16[4,512,256]{2,1,0:T(8,128)(2,1)} %get-tuple-element.68.refs_0_), channel_id=1, source_target_pairs={{0,240},{16,0},{32,16},{48,32},{64,48},{80,64},{96,80},{112,96},{1... | collective-permute-start | bytes 3145736 | tf_op jit(solution)/shard_map/ppermute | solution.py:335
  88.2 4.4 %copy-start.8 = (bf16[2,8,144,256]{3,2,1,0:T(8,128)(2,1)}, bf16[2,8,144,256]{3,2,1,0:T(8,128)(2,1)S(1)}, u32[]{:S(2)}) copy-start(bf16[2,8,144,256]{3,2,1,0:T(8,128)(2,1)S(1)} %get-tuple-element.81.refs_0_) | copy-start | bytes 3538948
  93.4 39.4 %collective-permute-start.16 = (bf16[2,512,256]{2,1,0:T(8,128)(2,1)}, bf16[2,512,256]{2,1,0:T(8,128)(2,1)S(1)}, u32[]{:S(2)}, u32[]{:S(2)}) collective-permute-start(bf16[2,512,256]{2,1,0:T(8,128)(2,1)} %get-tuple-element.75), channel_id=1, source_target_pairs={{0,16},{16,32},{32,48},{48,64},{64,80},{80,96},{96,112},{112,128},... | collective-permute-start | bytes 1572872 | tf_op jit(solution)/shard_map/ppermute | solution.py:335
  93.4 39.4 %copy-start.7 = (bf16[2,512,256]{2,1,0:T(8,128)(2,1)S(1)}, bf16[2,512,256]{2,1,0:T(8,128)(2,1)}, u32[]{:S(2)}) copy-start(bf16[2,512,256]{2,1,0:T(8,128)(2,1)} %copy-done.6) | copy-start | bytes 1572868
  93.4 3.1 %collective-permute-start = (bf16[2,8,144,256]{3,2,1,0:T(8,128)(2,1)}, bf16[2,8,144,256]{3,2,1,0:T(8,128)(2,1)S(1)}, u32[]{:S(2)}, u32[]{:S(2)}) collective-permute-start(bf16[2,8,144,256]{3,2,1,0:T(8,128)(2,1)} %get-tuple-element.12), channel_id=1, source_target_pairs={{0,1},{1,0},{2,3},{3,2},{4,5},{5,4},{6,7},{7,6},{8,9},{9,8},{10,11... | collective-permute-start | bytes 3538952 | tf_op jit(solution)/shard_map/cond/branch_1_fun/ppermute | solution.py:462
  98.4 11.5 %collective-permute-start.1 = (bf16[2,2,144,256]{3,2,1,0:T(8,128)(2,1)S(1)}, bf16[2,2,144,256]{3,2,1,0:T(8,128)(2,1)S(1)}, u32[]{:S(2)}, u32[]{:S(2)}) collective-permute-start(bf16[2,2,144,256]{3,2,1,0:T(8,128)(2,1)S(1)} %get-tuple-element.14), channel_id=1, source_target_pairs={{0,4},{1,5},{2,6},{3,7},{4,0},{5,1},{6,2},{7,3},{8,12},{9,13},{10,... | collective-permute-start | bytes 884744 | tf_op jit(solution)/shard_map/cond/branch_1_fun/ppermute | solution.py:457
  101.5 13.6 %collective-permute-start.2 = (bf16[2,2,144,256]{3,2,1,0:T(8,128)(2,1)S(1)}, bf16[2,2,144,256]{3,2,1,0:T(8,128)(2,1)S(1)}, u32[]{:S(2)}, u32[]{:S(2)}) collective-permute-start(bf16[2,2,144,256]{3,2,1,0:T(8,128)(2,1)S(1)} %get-tuple-element.15), channel_id=1, source_target_pairs={{0,2},{1,3},{2,4},{3,5},{4,6},{5,7},{6,0},{7,1},{8,10},{9,11},{10,... | collective-permute-start | bytes 884744 | tf_op jit(solution)/shard_map/cond/branch_1_fun/ppermute | solution.py:457
  101.5 13.9 %collective-permute-start.3 = (bf16[2,2,144,256]{3,2,1,0:T(8,128)(2,1)S(1)}, bf16[2,2,144,256]{3,2,1,0:T(8,128)(2,1)S(1)}, u32[]{:S(2)}, u32[]{:S(2)}) collective-permute-start(bf16[2,2,144,256]{3,2,1,0:T(8,128)(2,1)S(1)} %get-tuple-element.16), channel_id=1, source_target_pairs={{0,6},{1,7},{2,0},{3,1},{4,2},{5,3},{6,4},{7,5},{8,14},{9,15},{10,... | collective-permute-start | bytes 884744 | tf_op jit(solution)/shard_map/cond/branch_1_fun/ppermute | solution.py:457
  116.0 16.7 %collective-permute-start.4 = (bf16[2,144,256]{2,1,0:T(8,128)(2,1)S(1)}, bf16[2,144,256]{2,1,0:T(8,128)(2,1)S(1)}, u32[]{:S(2)}, u32[]{:S(2)}) collective-permute-start(bf16[2,144,256]{2,1,0:T(8,128)(2,1)S(1)} %get-tuple-element.18), channel_id=1, source_target_pairs={{0,8},{1,9},{2,10},{3,11},{4,12},{5,13},{6,14},{7,15},{8,0},{9,1},... | collective-permute-start | bytes 442376 | tf_op jit(solution)/shard_map/cond/branch_1_fun/ppermute | solution.py:471
  (4 other events, 5.1 us)

commit v3 on v2

v3 whole, which is shorter than its diff:
```python
import functools

import jax
import jax.numpy as jnp
from jax import lax
from jax.experimental import pallas as pl
from jax.experimental.pallas import tpu as pltpu
from jax.sharding import PartitionSpec as P

F32 = jnp.float32
BF16 = jnp.bfloat16
ANY = pl.BlockSpec(memory_space=pl.ANY)
VMEM = pl.BlockSpec(memory_space=pltpu.VMEM)
SMEM = pl.BlockSpec(memory_space=pltpu.SMEM)
LITTLE = pl.CostEstimate(flops=1000, bytes_accessed=1000, transcendentals=0)


def shape(*dims, dtype=BF16):
    return jax.ShapeDtypeStruct(dims, dtype)


def last_section(at_ref):
    return at_ref[0] == at_ref[2] - 1


def even_band(at_ref):
    return lax.rem(at_ref[1], 2) == 0


class View:
    def __init__(self, pieces, at_ref):
        self.pieces, self.at_ref = (pieces, at_ref)

    @property
    def ref(self):
        return self.pieces[0][0]

    def value(self):
        groups = []
        for ref, when in self.pieces:
            test, truth = when if when else (None, False)
            if not groups or groups[-1][0] is not test:
                groups.append((test, ([], [])))
            groups[-1][1][truth].append(ref[...])
        parts = []
        for test, group in groups:
            no, yes = (jnp.concatenate(g, 0) if len(g) > 1 else g[0] if g else None for g in group)
            parts.append(no if test is None else jnp.where(test(self.at_ref), yes, no))
        return parts[0] if len(parts) == 1 else jnp.concatenate(parts, 0)


def kernel(body, at, args, outs, scratch=(), after=(), token=False, mib=16):
    arrays = []
    outs = [*outs, shape(8, 128, dtype=F32)] if token else outs

    def place(array):
        for i, a in enumerate(arrays):
            if a is array:
                return i
        arrays.append(array)
        return len(arrays) - 1

    plan = []
    for arg in args:
        if not isinstance(arg, list):
            arg = [(*(arg if isinstance(arg, tuple) else (arg, None)), None, None, None)]
        plan.append([(place(piece[0]), *piece[1:]) for piece in arg])

    def run(*refs):
        at_ref, refs = (refs[len(after)], refs[len(after) + 1 :])
        views = []
        for pieces in plan:
            taken = []
            for i, index, start, size, when in pieces:
                ref = refs[i] if index is None else refs[i].at[index]
                taken.append((ref if start is None else ref.at[pl.ds(start, size)], when))
            views.append(View(taken, at_ref))
        refs = refs[len(arrays) :]
        body(at_ref, views, refs[: len(outs) - token], refs[len(outs) :])
        if token:
            refs[len(outs) - 1][...] = jnp.zeros((8, 128), F32)

    return pl.pallas_call(
        run,
        out_shape=outs,
        in_specs=[VMEM] * len(after) + [SMEM] + [VMEM] * len(arrays),
        out_specs=[VMEM] * len(outs),
        scratch_shapes=list(scratch),
        compiler_params=pltpu.CompilerParams(vmem_limit_bytes=mib << 20),
        cost_estimate=LITTLE,
        name=getattr(body, "func", body).__name__,
    )(*after, at, *arrays)


def sigmoid(v):
    return 1.0 / (1.0 + jnp.exp(-v))


def act(v):
    v = v.astype(F32)
    return (v * sigmoid(v)).astype(BF16).astype(F32)


def slope(v):
    v = v.astype(F32)
    s = sigmoid(v)
    return s * (1.0 + v * (1.0 - s))


def stencil(x_ref, v, cols):
    n, ch = v.shape
    v = v.astype(F32)
    col = lax.rem(lax.broadcasted_iota(jnp.int32, (n, ch), 0), cols)
    x_ref[:n, :ch] = jnp.where(col == 0, 0.0, pltpu.roll(v, 1, 0)).astype(BF16)
    x_ref[:n, ch : 2 * ch] = v.astype(BF16)
    x_ref[:n, 2 * ch :] = jnp.where(col == cols - 1, 0.0, pltpu.roll(v, n - 1, 0)).astype(BF16)


def conv(x_ref, w_ref, cols, size):
    depth = x_ref.shape[1]
    total = None
    for a in range(3):
        term = jnp.dot(
            x_ref[a * cols : a * cols + size, :], w_ref[a * depth : (a + 1) * depth, :], preferred_element_type=F32
        )
        total = term if total is None else total + term
    return total


def correlate(x_ref, d, cols):
    size = d.shape[0]
    return [
        lax.dot_general(
            x_ref[a * cols : a * cols + size, :], d, (((0,), (0,)), ((), ())), preferred_element_type=F32
        )
        for a in range(3)
    ]


def inside_image(at_ref, values, margin):
    n = values.shape[0]
    pixel = lax.broadcasted_iota(jnp.int32, values.shape, 0)
    low = jnp.where(at_ref[1] == 0, margin, 0)
    high = jnp.where(at_ref[1] == at_ref[3] - 1, n - margin, n)
    return jnp.where((pixel >= low) & (pixel < high), values, jnp.zeros_like(values))


def flip(at_ref, args, outs, own):
    w_ref = args[0].ref
    ch = w_ref.shape[2]
    for k in (1, 0):
        for t in range(9):
            outs[0][k, (8 - t) * ch : (9 - t) * ch, :] = w_ref[k, t * ch : (t + 1) * ch, :].T


def by_band(at_ref, bottom, top, inner_ref, outer_ref):
    even = even_band(at_ref)
    inner_ref[...] = jnp.where(even, bottom, top)
    outer_ref[...] = jnp.where(even, top, bottom)


def pack(counts, at_ref, *refs):
    refs, outs = (list(refs), refs[-2 * len(counts) :])
    for k, count in enumerate(counts):
        sides = []
        for _ in range(2):
            sides.append(jnp.concatenate([refs.pop(0)[0] for _ in range(count)], 0))
        by_band(at_ref, *sides, *outs[2 * k : 2 * k + 2])


def pick(at_ref, args, outs, own):
    half = len(args) // 2
    sides = [jnp.concatenate([arg.value() for arg in part], 0) for part in (args[:half], args[half:])]
    by_band(at_ref, *sides, *outs)


def invert_second(cols, x_ref, at_ref, y1, g2, y2, g1, w_g, t_g):
    wide = y1.shape[0] - 2 * cols
    stencil(x_ref, act(y1), cols)
    q2 = inside_image(at_ref, (y2.astype(F32) - conv(x_ref, w_g, cols, wide)).astype(BF16), cols)
    stencil(x_ref, g2, cols)
    back = conv(x_ref, t_g, cols, wide)
    h1 = (g1.astype(F32) + slope(y1[cols : cols + wide]) * back).astype(BF16)
    return q2, inside_image(at_ref, h1, cols)


def invert_first(cols, x_ref, y1, g2, q2, h1, w_f, t_f):
    size = y1.shape[0]
    stencil(x_ref, act(q2), cols)
    p2 = (y1.astype(F32) - conv(x_ref, w_f, cols, size)).astype(BF16)
    stencil(x_ref, h1, cols)
    back = conv(x_ref, t_f, cols, size)
    h2 = (g2.astype(F32) + slope(q2[cols : cols + size]) * back).astype(BF16)
    return p2, h2


def invert(cols, at_ref, args, outs, own):
    y1, g2, y2, g1 = (arg.value() for arg in args[:4])
    w_f, w_g, t_f, t_g = (arg.ref for arg in args[4:])
    edge = 2 * cols
    size = y1.shape[0] - 2 * edge
    q2, h1 = invert_second(cols, own[0], at_ref, y1, g2, y2, g1, w_g, t_g)
    outs[0][...] = q2
    outs[1][...] = h1
    there = slice(edge, edge + size)
    p2, h2 = invert_first(cols, own[0], y1[there], g2[there], q2, h1, w_f, t_f)
    here = slice(cols, cols + size)
    edges = outs[2]
    half = edges.shape[0] // 2
    inner = size - 2 * edge
    for k, (two, one) in enumerate(((p2, q2[here]), (h2, h1[here]))):
        at = k * edge
        edges[at : at + edge] = two[:edge]
        edges[half + at : half + at + edge] = two[size - edge :]
        at = 2 * edge + k * cols
        edges[at : at + cols] = one[:cols]
        edges[half + at : half + at + cols] = one[size - cols :]
        outs[3 + k][:inner] = two[edge : size - edge]
        outs[3 + k][inner:] = one[cols : size - cols]


def invert_last(cols, at_ref, args, outs, own):
    y1, g2, y2, g1 = (arg.value() for arg in args[:4])
    w_f, w_g, t_f, t_g, loss = (arg.ref for arg in args[4:])
    edge = 2 * cols
    size = y1.shape[0] - 2 * edge
    here = slice(cols, cols + size)
    there = slice(edge, edge + size)
    q2, h1 = invert_second(cols, own[0], at_ref, y1, g2, y2, g1, w_g, t_g)
    p2, h2 = invert_first(cols, own[0], y1[there], g2[there], q2, h1, w_f, t_f)
    send, fields = outs
    first = at_ref[0] == 0
    send[0] = p2
    send[1] = q2[here]
    send[2] = jnp.where(first, loss[0], h1[here])
    send[3] = jnp.where(first, loss[1], h2)
    inside = slice(cols, cols + size + edge)
    for k, field in enumerate((q2, h1, y1[inside], g2[inside])):
        fields[k] = field


def advance(cols, extra, at_ref, args, outs, own):
    q, p, w_f, w_g, new_q, new_p = args[:6]
    x_ref = own[0]
    q = q.value()
    edge = 2 * cols
    wide = q.shape[0] - edge
    size = wide - edge
    margin = extra * cols
    stencil(x_ref, act(q), cols)
    out1 = (p.value().astype(F32) + conv(x_ref, w_f.ref, cols, wide)).astype(BF16)
    out1 = inside_image(at_ref, out1, margin + cols)
    stencil(x_ref, act(out1), cols)
    out2 = (q[edge : edge + size].astype(F32) + conv(x_ref, w_g.ref, cols, size)).astype(BF16)
    adv, send = outs[:2]
    here = size - 2 * margin
    adv[0] = out1[cols + margin : cols + margin + here]
    adv[1] = out2[margin : margin + here]
    last = last_section(at_ref)
    if extra:
        out2 = inside_image(at_ref, out2, margin)
        send[...] = jnp.where(last, new_q.value(), out2)
        outs[2][...] = jnp.where(last, new_p.value(), out1[margin : margin + here + edge])
        outs[3][...] = args[6].ref[...]
        outs[4][...] = args[7].ref[...]
    else:
        send[0] = jnp.where(last, new_p.value(), adv[0])
        send[1] = jnp.where(last, new_q.value(), out2)


def weight_terms(cols, at_ref, args, outs, own):
    x_ref = own[0]
    depth = x_ref.shape[1]
    for k, (v, d) in enumerate((args[2:4], args[0:2])):
        stencil(x_ref, act(v.value()), cols)
        for a, term in enumerate(correlate(x_ref, d.value(), cols)):
            outs[0][k, a * depth : (a + 1) * depth] = term.astype(BF16)


def weight_sums(cols, at_ref, args, outs, own):
    x_ref, total = own
    depth = x_ref.shape[1]
    even = lax.rem(at_ref[1], 2) == 0
    keep, send = outs
    rows = send.shape[2]
    before = args[4].ref
    for k, (v, d) in enumerate((args[2:4], args[0:2])):
        stencil(x_ref, act(v.value()), cols)
        for a, term in enumerate(correlate(x_ref, d.value(), cols)):
            part = slice(a * depth, (a + 1) * depth)
            total[part] = term + before[k, part].astype(F32)
        for j in range(send.shape[1]):
            one = total[2 * j * rows : (2 * j + 1) * rows]
            two = total[(2 * j + 1) * rows : (2 * j + 2) * rows]
            keep[k, j] = jnp.where(even, one, two)
            send[k, j] = jnp.where(even, two, one).astype(BF16)


def sum_cores(at_ref, args, outs, own):
    keep, came = (arg.ref for arg in args)
    x = lax.rem(at_ref[1] // 2, 4)
    for d, out in zip((0, 2, 1, 3), outs):
        to = lax.rem(x + d, 4)
        for k in range(2):
            for z in range(2):
                out[k, z] = (keep[k, 4 * z + to] + came[k, 4 * z + to].astype(F32)).astype(out.dtype)


def sum_chips(at_ref, args, outs, own):
    z = at_ref[1] // 8
    parts = [arg.ref for arg in args]
    for k in range(2):
        for out, at in ((outs[0], 1 - z), (outs[1], z)):
            value = parts[0][k, at]
            for part in parts[1:]:
                value = value + part[k, at].astype(F32)
            out[k] = value.astype(out.dtype)


def place_outputs(at_ref, ahead_ref, back_ref, adv_ref, grad_ref,
                  forward_ref, returning_ref, backward_ref, weight_ref, held, sem):
    last = last_section(at_ref)
    copies = [
        pltpu.make_async_copy(ahead_ref, forward_ref, sem.at[0]),
        pltpu.make_async_copy(back_ref.at[pl.ds(2, 2)], backward_ref, sem.at[1]),
        pltpu.make_async_copy(grad_ref, weight_ref, sem.at[3]),
    ]
    came = pltpu.make_async_copy(back_ref.at[pl.ds(0, 2)], returning_ref, sem.at[2])
    for copy in copies:
        copy.start()
    pl.when(jnp.logical_not(last))(came.start)

    @pl.when(last)
    def own():
        fetch = pltpu.make_async_copy(adv_ref, held, sem.at[4])
        fetch.start()
        fetch.wait()
        pltpu.make_async_copy(held, returning_ref, sem.at[2]).start()

    for copy in copies:
        copy.wait()
    came.wait()


def local(forward_state, returning_state, returning_grad, weights, fresh_input, loss_grad):
    full = forward_state.shape
    rows, cols, ch = full[2:]
    size = rows * cols
    edge = 2 * cols
    segments = lax.axis_size("segment")
    bands = lax.axis_size("band")
    seg = lax.axis_index("segment")
    at = jnp.stack([seg, lax.axis_index("band"), segments, bands]).astype(jnp.int32)

    def swap(inner, outer):
        return (
            lax.ppermute(inner, "band", [(i, i ^ 1) for i in range(bands)]),
            lax.ppermute(outer, "band", [(i, i + 1 if i % 2 else i - 1) for i in range(1, bands - 1)]),
        )

    back_route = [(i + 1, i) for i in range(segments - 1)]
    back_ring = [(i, (i - 1) % segments) for i in range(segments)]
    ahead_ring = [(i, (i + 1) % segments) for i in range(segments)]

    def along(block, route):
        return lax.ppermute(block, "segment", route)

    state = forward_state.reshape(2, size, ch)
    y = returning_state.reshape(2, size, ch)
    g = returning_grad.reshape(2, size, ch)
    fresh = fresh_input.reshape(4, size, ch)
    loss = loss_grad.reshape(2, 2, size, ch)
    w = weights[0]
    w_f, w_g = ((w, 0), (w, 1))

    def x_scratch(extra):
        return pltpu.VMEM((size + 2 * extra * cols, 3 * ch), BF16)

    pair = shape(2, size, ch)
    ext = shape(size + edge, ch)
    e6 = shape(6 * cols, ch)

    def pack_edges(*groups):
        def spec(index, n, last):
            start = (rows - n) * cols if last else 0
            return pl.BlockSpec((pl.Element(1), pl.Element(n * cols), pl.Element(ch)), lambda i: (index, start, 0))

        parts = [(part, last) for group in groups for last in (True, False) for part in group]
        pixels = [sum(n for _, _, n in group) * cols for group in groups for _ in range(2)]
        return pl.pallas_call(
            functools.partial(pack, [len(group) for group in groups]), grid=(1,),
            out_shape=[shape(n, ch) for n in pixels],
            in_specs=[SMEM] + [spec(index, n, last) for (_, index, n), last in parts],
            out_specs=[pl.BlockSpec((n, ch), lambda i: (0, 0)) for n in pixels],
            compiler_params=pltpu.CompilerParams(vmem_limit_bytes=60 << 20), cost_estimate=LITTLE, name="pack_edges",
        )(at, *[array for (array, _, _), _ in parts])

    inner, outer, fwd_inner, fwd_outer = pack_edges(
        [(y, 0, 2), (g, 1, 2), (y, 1, 1), (g, 0, 1), (fresh, 1, 2), (fresh, 0, 1)], [(state, 1, 4), (state, 0, 3)]
    )
    edges0, fwd_edges = (swap(inner, outer), swap(fwd_inner, fwd_outer))
    (w_t,) = kernel(flip, at, (w,), (shape(2, 9 * ch, ch),))

    def extended(start, n, middle, edges, inset=0):
        (inner, outer), n = (edges, n * cols)
        above, below = ((start + inset) * cols, start * cols)
        yes, no = ((even_band, True), (even_band, False))
        return [
            (outer, None, above, n, yes), (inner, None, above, n, no), *middle,
            (inner, None, below, n, yes), (outer, None, below, n, no),
        ]

    def all_of(array, index):
        return [(array, index, 0, size, None)]

    mid = shape(2 * size - 6 * cols, ch)
    q2, h1, edges, mid_y, mid_g = kernel(
        functools.partial(invert, cols), at,
        (
            extended(0, 2, all_of(y, 0), edges0), extended(2, 2, all_of(g, 1), edges0),
            extended(4, 1, all_of(y, 1), edges0), extended(5, 1, all_of(g, 0), edges0),
            w_f, w_g, (w_t, 0), (w_t, 1),
        ),
        (ext, ext, shape(12 * cols, ch), mid, mid), [x_scratch(2)],
    )
    came_edges = along(edges, back_route)
    adv, ahead_q, ahead_p, mid_y, mid_g, token = kernel(
        functools.partial(advance, cols, 2), at,
        (
            extended(0, 4, all_of(state, 1), fwd_edges), extended(4, 3, all_of(state, 0), fwd_edges), w_f, w_g,
            extended(6, 2, all_of(fresh, 1), edges0), extended(8, 1, all_of(fresh, 0), edges0), mid_y, mid_g,
        ),
        (pair, shape(size + 4 * cols, ch), ext, mid, mid), [x_scratch(4)], token=True,
    )
    q, p = (along(ahead_q, ahead_ring), along(ahead_p, ahead_ring))
    came_mids = (along(mid_y, back_route), along(mid_g, back_route))
    terms, token = kernel(
        functools.partial(weight_terms, cols), at,
        (
            extended(0, 1, all_of(y, 0), edges0, 1), (g, 1),
            q2, [(h1, None, cols, size, None)],
        ),
        (shape(2, 9 * ch, ch),), [x_scratch(1)], (token,), True,
    )

    spans = ((0, 2, adv, 0), (2, 2, loss, (0, 1)), (4, 1, adv, 1), (5, 1, loss, (0, 0)))
    half = 6 * cols
    last, others = ((last_section, True), (last_section, False))
    picks = [
        [
            (came_edges, None, first + start * cols, n * cols, others),
            (own, index, size - n * cols if first else 0, n * cols, last),
        ]
        for first in (half, 0)
        for start, n, own, index in spans
    ]
    edges1 = swap(*kernel(pick, at, picks, (e6, e6)))
    inner, outer = (size - 2 * edge, size - edge)

    def came_field(k):
        start, n, own, index = spans[k]
        mid = came_mids[k % 2]
        return extended(start, n, [
            (came_edges, None, start * cols, n * cols, others),
            (mid, None, 0, inner, others) if k < 2 else (mid, None, inner, outer, others),
            (came_edges, None, half + start * cols, n * cols, others), (own, index, 0, size, last),
        ], edges1)

    last_adv, ahead, token = kernel(
        functools.partial(advance, cols, 0), at, (q, p, w_f, w_g, (fresh, 3), (fresh, 2)),
        (pair, pair), [x_scratch(2)], (token,), True,
    )
    (w_t,) = kernel(flip, at, (w,), (shape(2, 9 * ch, ch),), after=(token,))
    back, fields = kernel(
        functools.partial(invert_last, cols), at,
        (*[came_field(k) for k in range(4)], w_f, w_g, (w_t, 0), (w_t, 1), (loss, 1)),
        (shape(4, size, ch), shape(4, size + edge, ch)), [x_scratch(2)],
    )
    came_back = along(back, back_ring)
    part = 9 * ch // bands
    chunks = (2, 8, part, ch)
    keep, send = kernel(
        functools.partial(weight_sums, cols), at,
        ((fields, 2), [(fields, 3, cols, size, None)], (fields, 0), [(fields, 1, cols, size, None)], terms),
        (shape(*chunks, dtype=F32), shape(*chunks)), [x_scratch(1), pltpu.VMEM((9 * ch, ch), F32)],
    )

    def on_x(piece, step):
        return lax.ppermute(
            piece, "band", [(i, (i & 8) | ((((i >> 1) & 3) + step) % 4) << 1 | (i & 1)) for i in range(bands)]
        )

    def over_bands(send, keep, ahead, at):
        came_ahead = along(ahead, ahead_ring)
        came = lax.ppermute(send, "band", [(i, i ^ 1) for i in range(bands)])
        quarter = shape(2, 2, part, ch)
        own, far, right, left = kernel(
            sum_cores, at, (keep, came), (shape(2, 2, part, ch, dtype=F32), quarter, quarter, quarter)
        )
        far, right, left = (on_x(far, 2), on_x(right, 1), on_x(left, 3))
        send, keep = kernel(
            sum_chips, at, (own, far, right, left), (shape(2, part, ch), shape(2, part, ch, dtype=F32))
        )
        came = lax.ppermute(send, "band", [(i, i ^ 8) for i in range(bands)])
        return keep + came.astype(F32), came_ahead

    weight_grad, came_ahead = lax.cond(
        seg < segments, over_bands, lambda send, keep, ahead, at: (jnp.zeros((2, part, ch), F32), ahead),
        send, keep, ahead, at,
    )

    *outputs, weight_grad = pl.pallas_call(
        place_outputs, out_shape=[pair] * 3 + [shape(2, part, ch, dtype=F32)], in_specs=[SMEM] + [VMEM] * 2 + [ANY, VMEM],
        out_specs=[ANY] * 4,
        scratch_shapes=[pltpu.VMEM((2, size, ch), BF16), pltpu.SemaphoreType.DMA((5,))], cost_estimate=LITTLE,
        compiler_params=pltpu.CompilerParams(vmem_limit_bytes=8 << 20), name="place_outputs",
    )(at, came_ahead, came_back, last_adv, weight_grad)
    return (*[out.reshape(full) for out in outputs], weight_grad[None])


def solution(mesh):
    return jax.shard_map(
        local,
        mesh=mesh,
        in_specs=(
            P("segment", None, "band", None, None),
            P("segment", None, "band", None, None),
            P("segment", None, "band", None, None),
            P("segment", None, None, None),
            P(None, None, "band", None, None),
            P(None, None, "band", None, None),
        ),
        out_specs=(
            P("segment", None, "band", None, None),
            P("segment", None, "band", None, None),
            P("segment", None, "band", None, None),
            P("segment", None, "band", None),
        ),
        check_vma=False,
    )
```

time: 135 us -> 135 us (level)
  waiting for transfers between devices: 38.2 us -> 30.8 us
  starting transfers between devices: 59.4 us -> 66.5 us
  Pallas kernels: 35.1 us -> 32 us
  local copies, waits for them, and re-layouts: 0.84 us -> 3.92 us
    ppermute x7, waiting for transfers between devices: 14.3 us -> 3.36 us  [the longest x1 3.24 us: over_bands(): came = lax.ppermute(send, 'band', [(i, i ^ 8) for i in range(bands)])]
    ppermute x7, starting transfers between devices: 30.5 us -> 38.1 us  [the longest x1 23.1 us: over_bands(): came = lax.ppermute(send, 'band', [(i, i ^ 8) for i in range(bands)])]
    ppermute x7, waiting for transfers between devices: 9.07 us -> 12.2 us  [along(): return lax.ppermute(block, 'segment', route)]
    pallas_call x14 -> x13, Pallas kernels: 35.1 us -> 32 us  [the longest x11 27.2 us: kernel(): pl.pallas_call(run, out_shape=outs, in_specs=[VMEM] * len(after) + [SMEM]...]
    unnamed x20, local copies, waits for them, and re-layouts: 0.84 us -> 3.13 us
  transfers between devices with their start and end apart: 18 -> 18, of which waited for: 7 -> 6; matrix products, arithmetic and copies ran while one was open for 0% -> 1% of each run, Pallas kernels for 23% -> 16%
where the time goes in v3:
time: 135 us; the launch traced here: 134 us
  starting transfers between devices  66.5 us (49%)
  Pallas kernels  32 us (24%)
  waiting for transfers between devices  30.8 us (23%)
  local copies, waits for them, and re-layouts  3.92 us (3%)
    pallas_call x11, Pallas kernels, kernel(): pl.pallas_call(run, out_shape=outs, in_specs=[VMEM] * len(after) + [SMEM]...  27.2 us
    ppermute x1, starting transfers between devices, over_bands(): came = lax.ppermute(send, 'band', [(i, i ^ 8) for i in range(bands)])  23.1 us
    ppermute x7, starting transfers between devices, along(): return lax.ppermute(block, 'segment', route)  22.9 us
    ppermute x3, waiting for transfers between devices, on_x(): lax.ppermute(piece, 'band', [(i, i & 8 | ((i >> 1 & 3) + step) % 4 << 1 |...  12.7 us
    ppermute x7, waiting for transfers between devices, along(): return lax.ppermute(block, 'segment', route)  12.2 us
    ppermute x3, starting transfers between devices, swap(): lax.ppermute(inner, 'band', [(i, i ^ 1) for i in range(bands)])  9.19 us
    ppermute x3, starting transfers between devices, swap(): lax.ppermute(outer, 'band', [(i, i + 1 if i % 2 else i - 1) for i in rang...  5.89 us
    ppermute x3, starting transfers between devices, on_x(): lax.ppermute(piece, 'band', [(i, i & 8 | ((i >> 1 & 3) + step) % 4 << 1 |...  5.37 us
  transfers between devices with their start and end apart: 18, of which 6 were waited for; matrix products, arithmetic and copies ran while one was open for 1% of the time, Pallas kernels for 16%

profile of v3, /device:TPU:18, one launch (start us, length us, event | category | flops | bytes accessed | tf_op | source)
XLA Modules:
  0.0 134.5 jit_solution(16462338404104292123)
XLA Ops:
  0.7 2.5 %pack_edges.1 = (bf16[576,256]{1,0:T(8,128)(2,1)}, bf16[576,256]{1,0:T(8,128)(2,1)}, bf16[448,256]{1,0:T(8,128)(2,1)}, bf16[448,256]{1,0:T(8,128)(2,1)}) custom-call(s32[4]{0:T(128)S(1)} %pad_add_fusion.at_ref.refs_0_.refs_1_, bf16[2,512,256]{2,1,0:T(8,128)(2,1)} %bitcast.24, bf16[2,512,256]{2,1,0:T(8,128)(2,1)} %bitcast.30, bf16[2,512,256]{2,1,0:T(8,128)(2,1)} %bitcast.25, ...), custom_call_target="tpu_custom_call" | custom-call | flops 1000 | bytes 1000 | tf_op jit(solution)/shard_map/pack_edges/pallas_call | solution.py:390
  6.8 2.1 %collective-permute-start.6 = (bf16[448,256]{1,0:T(8,128)(2,1)}, bf16[448,256]{1,0:T(8,128)(2,1)S(1)}, u32[]{:S(2)}, u32[]{:S(2)}) collective-permute-start(bf16[448,256]{1,0:T(8,128)(2,1)} %get-tuple-element.55), channel_id=1, source_target_pairs={{1,2},{2,1},{3,4},{4,3},{5,6},{6,5},{7,8},{8,7},{9,10},{10,9},{11,... | collective-permute-start | bytes 688136 | tf_op jit(solution)/shard_map/ppermute | solution.py:358
  11.4 4.1 %invert.1 = (bf16[640,256]{1,0:T(8,128)(2,1)S(1)}, bf16[640,256]{1,0:T(8,128)(2,1)S(1)}, bf16[768,256]{1,0:T(8,128)(2,1)S(1)}, bf16[640,256]{1,0:T(8,128)(2,1)S(1)}, bf16[640,256]{1,0:T(8,128)(2,1)S(1)}) custom-call(s32[4]{0:T(128)S(1)} %pad_add_fusion.at_ref.refs_0_.refs_1_, bf16[576,256]{1,0:T(8,128)(2,1)S(1)} %collective-permute-done.8.refs_1_.refs_5_.refs_2_, ...), custom_call_target="tpu_custom_call" | custom-call | flops 1000 | bytes 1000 | tf_op jit(solution)/shard_map/invert/pallas_call | solution.py:83
  15.5 8.1 %collective-permute-start.12 = (bf16[768,256]{1,0:T(8,128)(2,1)S(1)}, bf16[768,256]{1,0:T(8,128)(2,1)S(1)}, u32[]{:S(2)}, u32[]{:S(2)}) collective-permute-start(bf16[768,256]{1,0:T(8,128)(2,1)S(1)} %get-tuple-element.68), channel_id=1, source_target_pairs={{16,0},{32,16},{48,32},{64,48},{80,64},{96,80},{112,96},{128,112},... | collective-permute-start | bytes 1179656 | tf_op jit(solution)/shard_map/ppermute | solution.py:366
  23.7 4.8 %advance.2 = (bf16[2,512,256]{2,1,0:T(8,128)(2,1)S(1)}, bf16[768,256]{1,0:T(8,128)(2,1)S(1)}, bf16[640,256]{1,0:T(8,128)(2,1)S(1)}, bf16[640,256]{1,0:T(8,128)(2...) custom-call(s32[4]{0:T(128)S(1)} %pad_add_fusion.at_ref.refs_0_.refs_1_, ...), custom_call_target="tpu_custom_call" | custom-call | flops 1000 | bytes 1000 | tf_op jit(solution)/shard_map/advance/pallas_call | solution.py:83
  30.1 5.4 %collective-permute-start.15 = (bf16[640,256]{1,0:T(8,128)(2,1)S(1)}, bf16[640,256]{1,0:T(8,128)(2,1)S(1)}, u32[]{:S(2)}, u32[]{:S(2)}) collective-permute-start(bf16[640,256]{1,0:T(8,128)(2,1)S(1)} %get-tuple-element.72), channel_id=1, source_target_pairs={{16,0},{32,16},{48,32},{64,48},{80,64},{96,80},{112,96},{128,112},... | collective-permute-start | bytes 983048 | tf_op jit(solution)/shard_map/ppermute | solution.py:366
  35.6 4.7 %collective-permute-start.16 = (bf16[640,256]{1,0:T(8,128)(2,1)S(1)}, bf16[640,256]{1,0:T(8,128)(2,1)S(1)}, u32[]{:S(2)}, u32[]{:S(2)}) collective-permute-start(bf16[640,256]{1,0:T(8,128)(2,1)S(1)} %get-tuple-element.73), channel_id=1, source_target_pairs={{16,0},{32,16},{48,32},{64,48},{80,64},{96,80},{112,96},{128,112},... | collective-permute-start | bytes 983048 | tf_op jit(solution)/shard_map/ppermute | solution.py:366
  40.9 1.9 %collective-permute-start.13 = (bf16[384,256]{1,0:T(8,128)(2,1)S(1)}, bf16[384,256]{1,0:T(8,128)(2,1)S(1)}, u32[]{:S(2)}, u32[]{:S(2)}) collective-permute-start(bf16[384,256]{1,0:T(8,128)(2,1)S(1)} %get-tuple-element.70), channel_id=1, source_target_pairs={{1,2},{2,1},{3,4},{4,3},{5,6},{6,5},{7,8},{8,7},{9,10},{10,9},{11,... | collective-permute-start | bytes 589832 | tf_op jit(solution)/shard_map/ppermute | solution.py:358
  42.9 6.3 %collective-permute-start.14 = (bf16[384,256]{1,0:T(8,128)(2,1)S(1)}, bf16[384,256]{1,0:T(8,128)(2,1)S(1)}, u32[]{:S(2)}, u32[]{:S(2)}) collective-permute-start(bf16[384,256]{1,0:T(8,128)(2,1)S(1)} %get-tuple-element.71), channel_id=1, source_target_pairs={{0,1},{1,0},{2,3},{3,2},{4,5},{5,4},{6,7},{7,6},{8,9},{9,8},{10,11... | collective-permute-start | bytes 589832 | tf_op jit(solution)/shard_map/ppermute | solution.py:357
  49.2 2.1 %weight_terms.1 = (bf16[2,2304,256]{2,1,0:T(8,128)(2,1)S(1)}, f32[8,128]{1,0:T(8,128)S(1)}) custom-call(f32[8,128]{1,0:T(8,128)S(1)} %get-tuple-element.61.refs_0_, s32[4]{0:T(128)S(1)} %pad_add_fusion.at_ref.refs_0_.refs_1_, bf16[576,256]{1,0:T(8,128)(2,1)S(1)} %collective-permute-done.8.refs_1_.refs_5_.refs_2_, ...), custom_call_target="tpu_custom_call" | custom-call | flops 1000 | bytes 1000 | tf_op jit(solution)/shard_map/weight_terms/pallas_call | solution.py:83
  52.7 12.2 %collective-permute-done.10.refs_2_ = bf16[768,256]{1,0:T(8,128)(2,1)S(1)} collective-permute-done((bf16[768,256]{1,0:T(8,128)(2,1)S(1)}, bf16[768,256]{1,0:T(8,128)(2,1)S(1)}, u32[]{:S(2)}, u32[]{:S(2)}) %collective-permute-start.10) | collective-permute-done | bytes 393248 | tf_op jit(solution)/shard_map/ppermute | solution.py:366
  64.9 4.4 %advance.3 = (bf16[2,512,256]{2,1,0:T(8,128)(2,1)S(1)}, bf16[2,512,256]{2,1,0:T(8,128)(2,1)}, f32[8,128]{1,0:T(8,128)S(1)}) custom-call(f32[8,128]{1,0:T(8,128)S(1)} %get-tuple-element.64.refs_0_, s32[4]{0:T(128)S(1)} %pad_add_fusion.at_ref.refs_0_.refs_1_, bf16[768,256]{1,0:T(8,128)(2,1)S(1)} %collective-permute-done.10.refs_2_, ...), custom_call_target="tpu_custom_call" | custom-call | flops 1000 | bytes 1000 | tf_op jit(solution)/shard_map/advance/pallas_call | solution.py:83
  70.5 5.1 %invert_last.1 = (bf16[4,512,256]{2,1,0:T(8,128)(2,1)}, bf16[4,640,256]{2,1,0:T(8,128)(2,1)S(1)}) custom-call(s32[4]{0:T(128)S(1)} %pad_add_fusion.at_ref.refs_0_.refs_1_, bf16[384,256]{1,0:T(8,128)(2,1)S(1)} %collective-permute-done.13.refs_1_, bf16[384,256]{1,0:T(8,128)(2,1)S(1)} %collective-permute-done.14.refs_2_, ...), custom_call_target="tpu_custom_call" | custom-call | flops 1000 | bytes 1000 | tf_op jit(solution)/shard_map/invert_last/pallas_call | solution.py:83
  75.7 2.7 %collective-permute-start.17 = (bf16[4,512,256]{2,1,0:T(8,128)(2,1)}, bf16[4,512,256]{2,1,0:T(8,128)(2,1)S(1)}, u32[]{:S(2)}, u32[]{:S(2)}) collective-permute-start(bf16[4,512,256]{2,1,0:T(8,128)(2,1)} %get-tuple-element.80), channel_id=1, source_target_pairs={{0,240},{16,0},{32,16},{48,32},{64,48},{80,64},{96,80},{112,96},{1... | collective-permute-start | bytes 3145736 | tf_op jit(solution)/shard_map/ppermute | solution.py:366
  80.0 2.3 %weight_sums.1 = (f32[2,8,144,256]{3,2,1,0:T(8,128)S(1)}, bf16[2,8,144,256]{3,2,1,0:T(8,128)(2,1)S(1)}) custom-call(s32[4]{0:T(128)S(1)} %pad_add_fusion.at_ref.refs_0_.refs_1_, bf16[4,640,256]{2,1,0:T(8,128)(2,1)S(1)} %get-tuple-element.75.refs_1_, bf16[2,2304,256]{2,1,0:T(8,128)(2,1)S(1)} %copy-done.7), custom_call_target="tpu_custom_call" | custom-call | flops 1000 | bytes 1000 | tf_op jit(solution)/shard_map/weight_sums/pallas_call | solution.py:83
  82.3 49.7 %conditional.1 = (f32[2,144,256]{2,1,0:T(8,128)S(1)}, bf16[2,512,256]{2,1,0:T(8,128)(2,1)}) conditional(s32[]{:T(128)} %convert_element_type.6, bf16[2,512,256]{2,1,0:T(8,128)(2,1)} %get-tuple-element.67, (bf16[2,8,144,256]{3,2,1,0:T(8,128)(2,1)S(1)}, s32[4]{0:T(128)S(1)}, f32[2,8,144,256]{3,2,1,0:T(8,128)S(1)}, bf16[2,512,256]{2,1,0:T(8,128)(2,1)}) %tuple.16), branch_computations={%region_0.0_spmd, %region_1.0_spmd} | conditional | flops 149456 | bytes 12732624 | solution.py:507
  82.7 2.5 %collective-permute-done.refs_2_ = bf16[2,8,144,256]{3,2,1,0:T(8,128)(2,1)S(1)} collective-permute-done((bf16[2,8,144,256]{3,2,1,0:T(8,128)(2,1)S(1)}, bf16[2,8,144,256]{3,2,1,0:T(8,128)(2,1)S(1)}, u32[]{:S(2)}, u32[]{:S(2)}) %collective-permute-start) | collective-permute-done | bytes 1179680 | tf_op jit(solution)/shard_map/cond/branch_1_fun/ppermute | solution.py:495
  86.0 3.3 %collective-permute-start.1 = (bf16[2,2,144,256]{3,2,1,0:T(8,128)(2,1)S(1)}, bf16[2,2,144,256]{3,2,1,0:T(8,128)(2,1)S(1)}, u32[]{:S(2)}, u32[]{:S(2)}) collective-permute-start(bf16[2,2,144,256]{3,2,1,0:T(8,128)(2,1)S(1)} %get-tuple-element.13), channel_id=1, source_target_pairs={{0,4},{1,5},{2,6},{3,7},{4,0},{5,1},{6,2},{7,3},{8,12},{9,13},{10,... | collective-permute-start | bytes 884744 | tf_op jit(solution)/shard_map/cond/branch_1_fun/ppermute | solution.py:489
  89.4 2.0 %collective-permute-start.3 = (bf16[2,2,144,256]{3,2,1,0:T(8,128)(2,1)S(1)}, bf16[2,2,144,256]{3,2,1,0:T(8,128)(2,1)S(1)}, u32[]{:S(2)}, u32[]{:S(2)}) collective-permute-start(bf16[2,2,144,256]{3,2,1,0:T(8,128)(2,1)S(1)} %get-tuple-element.15), channel_id=1, source_target_pairs={{0,6},{1,7},{2,0},{3,1},{4,2},{5,3},{6,4},{7,5},{8,14},{9,15},{10,... | collective-permute-start | bytes 884744 | tf_op jit(solution)/shard_map/cond/branch_1_fun/ppermute | solution.py:489
  91.4 6.1 %collective-permute-done.1.refs_2_ = bf16[2,2,144,256]{3,2,1,0:T(8,128)(2,1)S(1)} collective-permute-done((bf16[2,2,144,256]{3,2,1,0:T(8,128)(2,1)S(1)}, bf16[2,2,144,256]{3,2,1,0:T(8,128)(2,1)S(1)}, u32[]{:S(2)}, u32[]{:S(2)}) %collective-permute-start.1) | collective-permute-done | bytes 294944 | tf_op jit(solution)/shard_map/cond/branch_1_fun/ppermute | solution.py:489
  97.5 6.7 %collective-permute-done.2.refs_3_ = bf16[2,2,144,256]{3,2,1,0:T(8,128)(2,1)S(1)} collective-permute-done((bf16[2,2,144,256]{3,2,1,0:T(8,128)(2,1)S(1)}, bf16[2,2,144,256]{3,2,1,0:T(8,128)(2,1)S(1)}, u32[]{:S(2)}, u32[]{:S(2)}) %collective-permute-start.2) | collective-permute-done | bytes 294944 | tf_op jit(solution)/shard_map/cond/branch_1_fun/ppermute | solution.py:489
  104.8 23.1 %collective-permute-start.4 = (bf16[2,144,256]{2,1,0:T(8,128)(2,1)S(1)}, bf16[2,144,256]{2,1,0:T(8,128)(2,1)S(1)}, u32[]{:S(2)}, u32[]{:S(2)}) collective-permute-start(bf16[2,144,256]{2,1,0:T(8,128)(2,1)S(1)} %get-tuple-element.17), channel_id=1, source_target_pairs={{0,8},{1,9},{2,10},{3,11},{4,12},{5,13},{6,14},{7,15},{8,0},{9,1},... | collective-permute-start | bytes 442376 | tf_op jit(solution)/shard_map/cond/branch_1_fun/ppermute | solution.py:504
  128.7 3.2 %collective-permute-done.4 = bf16[2,144,256]{2,1,0:T(8,128)(2,1)S(1)} collective-permute-done((bf16[2,144,256]{2,1,0:T(8,128)(2,1)S(1)}, bf16[2,144,256]{2,1,0:T(8,128)(2,1)S(1)}, u32[]{:S(2)}, u32[]{:S(2)}) %collective-permute-start.4) | collective-permute-done | bytes 147488 | tf_op jit(solution)/shard_map/cond/branch_1_fun/ppermute | solution.py:504
  132.0 2.3 %place_outputs.1 = (bf16[2,512,256]{2,1,0:T(8,128)(2,1)}, bf16[2,512,256]{2,1,0:T(8,128)(2,1)}, bf16[2,512,256]{2,1,0:T(8,128)(2,1)}, f32[2,144,256]{2,1,0:T(8,128)}) custom-call(s32[4]{0:T(128)S(1)} %pad_add_fusion.at_ref.refs_0_.refs_1_, bf16[2,512,256]{2,1,0:T(8,128)(2,1)} %get-tuple-element.79.ahead_ref, ...), custom_call_target="tpu_custom_call" | custom-call | flops 1000 | bytes 1000 | tf_op jit(solution)/shard_map/place_outputs/pallas_call | solution.py:512
  (50 shorter events, 15.6 us)
Async XLA Ops:
  0.7 9.4 %copy-start = (bf16[1,2,2304,256]{3,2,1,0:T(8,128)(2,1)S(1)}, bf16[1,2,2304,256]{3,2,1,0:T(8,128)(2,1)}, u32[]{:S(2)}) copy-start(bf16[1,2,2304,256]{3,2,1,0:T(8,128)(2,1)} %param.11) | copy-start | bytes 7077892
  3.2 8.2 %collective-permute-start.8 = (bf16[576,256]{1,0:T(8,128)(2,1)}, bf16[576,256]{1,0:T(8,128)(2,1)S(1)}, u32[]{:S(2)}, u32[]{:S(2)}) collective-permute-start(bf16[576,256]{1,0:T(8,128)(2,1)} %get-tuple-element.57), channel_id=1, source_target_pairs={{1,2},{2,1},{3,4},{4,3},{5,6},{6,5},{7,8},{8,7},{9,10},{10,9},{11,... | collective-permute-start | bytes 884744 | tf_op jit(solution)/shard_map/ppermute | solution.py:358
  5.1 6.3 %collective-permute-start.9 = (bf16[576,256]{1,0:T(8,128)(2,1)}, bf16[576,256]{1,0:T(8,128)(2,1)S(1)}, u32[]{:S(2)}, u32[]{:S(2)}) collective-permute-start(bf16[576,256]{1,0:T(8,128)(2,1)} %get-tuple-element.58), channel_id=1, source_target_pairs={{0,1},{1,0},{2,3},{3,2},{4,5},{5,4},{6,7},{7,6},{8,9},{9,8},{10,11... | collective-permute-start | bytes 884744 | tf_op jit(solution)/shard_map/ppermute | solution.py:357
  6.8 16.8 %collective-permute-start.6 = (bf16[448,256]{1,0:T(8,128)(2,1)}, bf16[448,256]{1,0:T(8,128)(2,1)S(1)}, u32[]{:S(2)}, u32[]{:S(2)}) collective-permute-start(bf16[448,256]{1,0:T(8,128)(2,1)} %get-tuple-element.55), channel_id=1, source_target_pairs={{1,2},{2,1},{3,4},{4,3},{5,6},{6,5},{7,8},{8,7},{9,10},{10,9},{11,... | collective-permute-start | bytes 688136 | tf_op jit(solution)/shard_map/ppermute | solution.py:358
  8.8 14.8 %collective-permute-start.7 = (bf16[448,256]{1,0:T(8,128)(2,1)}, bf16[448,256]{1,0:T(8,128)(2,1)S(1)}, u32[]{:S(2)}, u32[]{:S(2)}) collective-permute-start(bf16[448,256]{1,0:T(8,128)(2,1)} %get-tuple-element.56), channel_id=1, source_target_pairs={{0,1},{1,0},{2,3},{3,2},{4,5},{5,4},{6,7},{7,6},{8,9},{9,8},{10,11... | collective-permute-start | bytes 688136 | tf_op jit(solution)/shard_map/ppermute | solution.py:357
  11.3 12.3 %copy-start.1 = (bf16[2,2,8,64,256]{4,3,2,1,0:T(8,128)(2,1)S(1)}, bf16[2,2,8,64,256]{4,3,2,1,0:T(8,128)(2,1)}, u32[]{:S(2)}) copy-start(bf16[2,2,8,64,256]{4,3,2,1,0:T(8,128)(2,1)} %param.12) | copy-start | bytes 3145732
  11.3 12.3 %copy-start.4 = (bf16[1,2,8,64,256]{4,3,2,1,0:T(8,128)(2,1)S(1)}, bf16[1,2,8,64,256]{4,3,2,1,0:T(8,128)(2,1)}, u32[]{:S(2)}) copy-start(bf16[1,2,8,64,256]{4,3,2,1,0:T(8,128)(2,1)} %param.8) | copy-start | bytes 1572868
  15.5 24.8 %collective-permute-start.12 = (bf16[768,256]{1,0:T(8,128)(2,1)S(1)}, bf16[768,256]{1,0:T(8,128)(2,1)S(1)}, u32[]{:S(2)}, u32[]{:S(2)}) collective-permute-start(bf16[768,256]{1,0:T(8,128)(2,1)S(1)} %get-tuple-element.68), channel_id=1, source_target_pairs={{16,0},{32,16},{48,32},{64,48},{80,64},{96,80},{112,96},{128,112},... | collective-permute-start | bytes 1179656 | tf_op jit(solution)/shard_map/ppermute | solution.py:366
  23.6 16.7 %copy-start.5 = (bf16[2,2,8,64,256]{4,3,2,1,0:T(8,128)(2,1)S(1)}, bf16[2,2,8,64,256]{4,3,2,1,0:T(8,128)(2,1)}, u32[]{:S(2)}) copy-start(bf16[2,2,8,64,256]{4,3,2,1,0:T(8,128)(2,1)} %param.13) | copy-start | bytes 3145732
  28.4 14.4 %collective-permute-start.11 = (bf16[640,256]{1,0:T(8,128)(2,1)S(1)}, bf16[640,256]{1,0:T(8,128)(2,1)S(1)}, u32[]{:S(2)}, u32[]{:S(2)}) collective-permute-start(bf16[640,256]{1,0:T(8,128)(2,1)S(1)} %get-tuple-element.66), channel_id=1, source_target_pairs={{0,16},{16,32},{32,48},{48,64},{64,80},{80,96},{96,112},{112,128},... | collective-permute-start | bytes 983048 | tf_op jit(solution)/shard_map/ppermute | solution.py:366
  28.5 36.3 %collective-permute-start.10 = (bf16[768,256]{1,0:T(8,128)(2,1)S(1)}, bf16[768,256]{1,0:T(8,128)(2,1)S(1)}, u32[]{:S(2)}, u32[]{:S(2)}) collective-permute-start(bf16[768,256]{1,0:T(8,128)(2,1)S(1)} %get-tuple-element.65), channel_id=1, source_target_pairs={{0,16},{16,32},{32,48},{48,64},{64,80},{80,96},{96,112},{112,128},... | collective-permute-start | bytes 1179656 | tf_op jit(solution)/shard_map/ppermute | solution.py:366
  30.1 40.3 %collective-permute-start.15 = (bf16[640,256]{1,0:T(8,128)(2,1)S(1)}, bf16[640,256]{1,0:T(8,128)(2,1)S(1)}, u32[]{:S(2)}, u32[]{:S(2)}) collective-permute-start(bf16[640,256]{1,0:T(8,128)(2,1)S(1)} %get-tuple-element.72), channel_id=1, source_target_pairs={{16,0},{32,16},{48,32},{64,48},{80,64},{96,80},{112,96},{128,112},... | collective-permute-start | bytes 983048 | tf_op jit(solution)/shard_map/ppermute | solution.py:366
  35.6 34.9 %collective-permute-start.16 = (bf16[640,256]{1,0:T(8,128)(2,1)S(1)}, bf16[640,256]{1,0:T(8,128)(2,1)S(1)}, u32[]{:S(2)}, u32[]{:S(2)}) collective-permute-start(bf16[640,256]{1,0:T(8,128)(2,1)S(1)} %get-tuple-element.73), channel_id=1, source_target_pairs={{16,0},{32,16},{48,32},{64,48},{80,64},{96,80},{112,96},{128,112},... | collective-permute-start | bytes 983048 | tf_op jit(solution)/shard_map/ppermute | solution.py:366
  40.9 29.5 %collective-permute-start.13 = (bf16[384,256]{1,0:T(8,128)(2,1)S(1)}, bf16[384,256]{1,0:T(8,128)(2,1)S(1)}, u32[]{:S(2)}, u32[]{:S(2)}) collective-permute-start(bf16[384,256]{1,0:T(8,128)(2,1)S(1)} %get-tuple-element.70), channel_id=1, source_target_pairs={{1,2},{2,1},{3,4},{4,3},{5,6},{6,5},{7,8},{8,7},{9,10},{10,9},{11,... | collective-permute-start | bytes 589832 | tf_op jit(solution)/shard_map/ppermute | solution.py:358
  42.9 27.6 %collective-permute-start.14 = (bf16[384,256]{1,0:T(8,128)(2,1)S(1)}, bf16[384,256]{1,0:T(8,128)(2,1)S(1)}, u32[]{:S(2)}, u32[]{:S(2)}) collective-permute-start(bf16[384,256]{1,0:T(8,128)(2,1)S(1)} %get-tuple-element.71), channel_id=1, source_target_pairs={{0,1},{1,0},{2,3},{3,2},{4,5},{5,4},{6,7},{7,6},{8,9},{9,8},{10,11... | collective-permute-start | bytes 589832 | tf_op jit(solution)/shard_map/ppermute | solution.py:357
  75.7 56.3 %collective-permute-start.17 = (bf16[4,512,256]{2,1,0:T(8,128)(2,1)}, bf16[4,512,256]{2,1,0:T(8,128)(2,1)S(1)}, u32[]{:S(2)}, u32[]{:S(2)}) collective-permute-start(bf16[4,512,256]{2,1,0:T(8,128)(2,1)} %get-tuple-element.80), channel_id=1, source_target_pairs={{0,240},{16,0},{32,16},{48,32},{64,48},{80,64},{96,80},{112,96},{1... | collective-permute-start | bytes 3145736 | tf_op jit(solution)/shard_map/ppermute | solution.py:366
  78.3 1.7 %copy-start.7 = (bf16[2,2304,256]{2,1,0:T(8,128)(2,1)S(1)}, bf16[2,2304,256]{2,1,0:T(8,128)(2,1)}, u32[]{:S(2)}) copy-start(bf16[2,2304,256]{2,1,0:T(8,128)(2,1)} %copy-done.6) | copy-start | bytes 7077892
  82.3 49.7 %copy-start.9 = (bf16[2,512,256]{2,1,0:T(8,128)(2,1)S(1)}, bf16[2,512,256]{2,1,0:T(8,128)(2,1)}, u32[]{:S(2)}) copy-start(bf16[2,512,256]{2,1,0:T(8,128)(2,1)} %copy-done.8) | copy-start | bytes 1572868
  82.3 2.9 %collective-permute-start = (bf16[2,8,144,256]{3,2,1,0:T(8,128)(2,1)S(1)}, bf16[2,8,144,256]{3,2,1,0:T(8,128)(2,1)S(1)}, u32[]{:S(2)}, u32[]{:S(2)}) collective-permute-start(bf16[2,8,144,256]{3,2,1,0:T(8,128)(2,1)S(1)} %get-tuple-element.11), channel_id=1, source_target_pairs={{0,1},{1,0},{2,3},{3,2},{4,5},{5,4},{6,7},{7,6},{8,9},{9,8},{10,11... | collective-permute-start | bytes 3538952 | tf_op jit(solution)/shard_map/cond/branch_1_fun/ppermute | solution.py:495
  82.4 45.5 %collective-permute-start.5 = (bf16[2,512,256]{2,1,0:T(8,128)(2,1)}, bf16[2,512,256]{2,1,0:T(8,128)(2,1)S(1)}, u32[]{:S(2)}, u32[]{:S(2)}) collective-permute-start(bf16[2,512,256]{2,1,0:T(8,128)(2,1)} %get-tuple-element.18), channel_id=1, source_target_pairs={{0,16},{16,32},{32,48},{48,64},{64,80},{80,96},{96,112},{112,128},... | collective-permute-start | bytes 1572872 | tf_op jit(solution)/shard_map/cond/branch_1_fun/ppermute | solution.py:366
  86.0 11.5 %collective-permute-start.1 = (bf16[2,2,144,256]{3,2,1,0:T(8,128)(2,1)S(1)}, bf16[2,2,144,256]{3,2,1,0:T(8,128)(2,1)S(1)}, u32[]{:S(2)}, u32[]{:S(2)}) collective-permute-start(bf16[2,2,144,256]{3,2,1,0:T(8,128)(2,1)S(1)} %get-tuple-element.13), channel_id=1, source_target_pairs={{0,4},{1,5},{2,6},{3,7},{4,0},{5,1},{6,2},{7,3},{8,12},{9,13},{10,... | collective-permute-start | bytes 884744 | tf_op jit(solution)/shard_map/cond/branch_1_fun/ppermute | solution.py:489
  89.4 14.8 %collective-permute-start.2 = (bf16[2,2,144,256]{3,2,1,0:T(8,128)(2,1)S(1)}, bf16[2,2,144,256]{3,2,1,0:T(8,128)(2,1)S(1)}, u32[]{:S(2)}, u32[]{:S(2)}) collective-permute-start(bf16[2,2,144,256]{3,2,1,0:T(8,128)(2,1)S(1)} %get-tuple-element.14), channel_id=1, source_target_pairs={{0,2},{1,3},{2,4},{3,5},{4,6},{5,7},{6,0},{7,1},{8,10},{9,11},{10,... | collective-permute-start | bytes 884744 | tf_op jit(solution)/shard_map/cond/branch_1_fun/ppermute | solution.py:489
  89.4 14.7 %collective-permute-start.3 = (bf16[2,2,144,256]{3,2,1,0:T(8,128)(2,1)S(1)}, bf16[2,2,144,256]{3,2,1,0:T(8,128)(2,1)S(1)}, u32[]{:S(2)}, u32[]{:S(2)}) collective-permute-start(bf16[2,2,144,256]{3,2,1,0:T(8,128)(2,1)S(1)} %get-tuple-element.15), channel_id=1, source_target_pairs={{0,6},{1,7},{2,0},{3,1},{4,2},{5,3},{6,4},{7,5},{8,14},{9,15},{10,... | collective-permute-start | bytes 884744 | tf_op jit(solution)/shard_map/cond/branch_1_fun/ppermute | solution.py:489
  104.8 27.1 %collective-permute-start.4 = (bf16[2,144,256]{2,1,0:T(8,128)(2,1)S(1)}, bf16[2,144,256]{2,1,0:T(8,128)(2,1)S(1)}, u32[]{:S(2)}, u32[]{:S(2)}) collective-permute-start(bf16[2,144,256]{2,1,0:T(8,128)(2,1)S(1)} %get-tuple-element.17), channel_id=1, source_target_pairs={{0,8},{1,9},{2,10},{3,11},{4,12},{5,13},{6,14},{7,15},{8,0},{9,1},... | collective-permute-start | bytes 442376 | tf_op jit(solution)/shard_map/cond/branch_1_fun/ppermute | solution.py:504
  (4 other events, 5.3 us)

commit v4 on v3

--- a/solution.py
+++ b/solution.py
@@ -23,10 +23,6 @@
     return at_ref[0] == at_ref[2] - 1
 
 
-def even_band(at_ref):
-    return lax.rem(at_ref[1], 2) == 0
-
-
 class View:
     def __init__(self, pieces, at_ref):
         self.pieces, self.at_ref = (pieces, at_ref)
@@ -38,14 +34,17 @@
     def value(self):
         groups = []
         for ref, when in self.pieces:
-            test, truth = when if when else (None, False)
-            if not groups or groups[-1][0] is not test:
-                groups.append((test, ([], [])))
-            groups[-1][1][truth].append(ref[...])
+            if when is None or not groups or groups[-1][0] is None:
+                groups.append((None, [ref[...]]) if when is None else (0, ([], [])))
+            if when is not None:
+                groups[-1][1][int(when)].append(ref[...])
         parts = []
-        for test, group in groups:
-            no, yes = (jnp.concatenate(g, 0) if len(g) > 1 else g[0] if g else None for g in group)
-            parts.append(no if test is None else jnp.where(test(self.at_ref), yes, no))
+        for kind, group in groups:
+            if kind is None:
+                parts += group
+            else:
+                rest, last = (jnp.concatenate(g, 0) if len(g) > 1 else g[0] for g in group)
+                parts.append(jnp.where(last_section(self.at_ref), last, rest))
         return parts[0] if len(parts) == 1 else jnp.concatenate(parts, 0)
 
 
@@ -153,25 +152,25 @@
             outs[0][k, (8 - t) * ch : (9 - t) * ch, :] = w_ref[k, t * ch : (t + 1) * ch, :].T
 
 
-def by_band(at_ref, bottom, top, inner_ref, outer_ref):
-    even = even_band(at_ref)
-    inner_ref[...] = jnp.where(even, bottom, top)
-    outer_ref[...] = jnp.where(even, top, bottom)
-
-
-def pack(counts, at_ref, *refs):
-    refs, outs = (list(refs), refs[-2 * len(counts) :])
-    for k, count in enumerate(counts):
-        sides = []
-        for _ in range(2):
-            sides.append(jnp.concatenate([refs.pop(0)[0] for _ in range(count)], 0))
-        by_band(at_ref, *sides, *outs[2 * k : 2 * k + 2])
+def pack(counts, *refs):
+    outs = refs[-len(counts) :]
+    refs = list(refs)
+    for count, out in zip(counts, outs):
+        end = 0
+        for _ in range(count):
+            ref = refs.pop(0)
+            size = ref.shape[-2]
+            out[end : end + size] = ref[...].reshape(size, ref.shape[-1])
+            end += size
 
 
 def pick(at_ref, args, outs, own):
-    half = len(args) // 2
-    sides = [jnp.concatenate([arg.value() for arg in part], 0) for part in (args[:half], args[half:])]
-    by_band(at_ref, *sides, *outs)
+    for k, out in enumerate(outs):
+        end = 0
+        for arg in args[k * len(args) // len(outs) : (k + 1) * len(args) // len(outs)]:
+            value = arg.value()
+            out[end : end + value.shape[0]] = value
+            end += value.shape[0]
 
 
 def invert_second(cols, x_ref, at_ref, y1, g2, y2, g1, w_g, t_g):
@@ -352,10 +351,10 @@
     seg = lax.axis_index("segment")
     at = jnp.stack([seg, lax.axis_index("band"), segments, bands]).astype(jnp.int32)
 
-    def swap(inner, outer):
+    def up_down(bottom, top):
         return (
-            lax.ppermute(inner, "band", [(i, i ^ 1) for i in range(bands)]),
-            lax.ppermute(outer, "band", [(i, i + 1 if i % 2 else i - 1) for i in range(1, bands - 1)]),
+            lax.ppermute(bottom, "band", [(i, i + 1) for i in range(bands - 1)]),
+            lax.ppermute(top, "band", [(i + 1, i) for i in range(bands - 1)]),
         )
 
     back_route = [(i + 1, i) for i in range(segments - 1)]
@@ -388,27 +387,23 @@
         parts = [(part, last) for group in groups for last in (True, False) for part in group]
         pixels = [sum(n for _, _, n in group) * cols for group in groups for _ in range(2)]
         return pl.pallas_call(
-            functools.partial(pack, [len(group) for group in groups]), grid=(1,),
+            functools.partial(pack, [len(group) for group in groups for _ in range(2)]), grid=(1,),
             out_shape=[shape(n, ch) for n in pixels],
-            in_specs=[SMEM] + [spec(index, n, last) for (_, index, n), last in parts],
+            in_specs=[spec(index, n, last) for (_, index, n), last in parts],
             out_specs=[pl.BlockSpec((n, ch), lambda i: (0, 0)) for n in pixels],
             compiler_params=pltpu.CompilerParams(vmem_limit_bytes=60 << 20), cost_estimate=LITTLE, name="pack_edges",
-        )(at, *[array for (array, _, _), _ in parts])
-
-    inner, outer, fwd_inner, fwd_outer = pack_edges(
+        )(*[array for (array, _, _), _ in parts])
+
+    bottom, top, fwd_bottom, fwd_top = pack_edges(
         [(y, 0, 2), (g, 1, 2), (y, 1, 1), (g, 0, 1), (fresh, 1, 2), (fresh, 0, 1)], [(state, 1, 4), (state, 0, 3)]
     )
-    edges0, fwd_edges = (swap(inner, outer), swap(fwd_inner, fwd_outer))
+    up, down = up_down(bottom, top)
+    fwd_up, fwd_down = up_down(fwd_bottom, fwd_top)
     (w_t,) = kernel(flip, at, (w,), (shape(2, 9 * ch, ch),))
 
-    def extended(start, n, middle, edges, inset=0):
-        (inner, outer), n = (edges, n * cols)
-        above, below = ((start + inset) * cols, start * cols)
-        yes, no = ((even_band, True), (even_band, False))
-        return [
-            (outer, None, above, n, yes), (inner, None, above, n, no), *middle,
-            (inner, None, below, n, yes), (outer, None, below, n, no),
-        ]
+    def extended(start, n, middle, up, down):
+        start, n = (start * cols, n * cols)
+        return [(up, None, start, n, None), *middle, (down, None, start, n, None)]
 
     def all_of(array, index):
         return [(array, index, 0, size, None)]
@@ -417,8 +412,8 @@
     q2, h1, edges, mid_y, mid_g = kernel(
         functools.partial(invert, cols), at,
         (
-            extended(0, 2, all_of(y, 0), edges0), extended(2, 2, all_of(g, 1), edges0),
-            extended(4, 1, all_of(y, 1), edges0), extended(5, 1, all_of(g, 0), edges0),
+            extended(0, 2, all_of(y, 0), up, down), extended(2, 2, all_of(g, 1), up, down),
+            extended(4, 1, all_of(y, 1), up, down), extended(5, 1, all_of(g, 0), up, down),
             w_f, w_g, (w_t, 0), (w_t, 1),
         ),
         (ext, ext, shape(12 * cols, ch), mid, mid), [x_scratch(2)],
@@ -427,8 +422,8 @@
     adv, ahead_q, ahead_p, mid_y, mid_g, token = kernel(
         functools.partial(advance, cols, 2), at,
         (
-            extended(0, 4, all_of(state, 1), fwd_edges), extended(4, 3, all_of(state, 0), fwd_edges), w_f, w_g,
-            extended(6, 2, all_of(fresh, 1), edges0), extended(8, 1, all_of(fresh, 0), edges0), mid_y, mid_g,
+            extended(0, 4, all_of(state, 1), fwd_up, fwd_down), extended(4, 3, all_of(state, 0), fwd_up, fwd_down), w_f, w_g,
+            extended(6, 2, all_of(fresh, 1), up, down), extended(8, 1, all_of(fresh, 0), up, down), mid_y, mid_g,
         ),
         (pair, shape(size + 4 * cols, ch), ext, mid, mid), [x_scratch(4)], token=True,
     )
@@ -437,7 +432,7 @@
     terms, token = kernel(
         functools.partial(weight_terms, cols), at,
         (
-            extended(0, 1, all_of(y, 0), edges0, 1), (g, 1),
+            [(up, None, cols, cols, None), (y, 0, 0, size, None), (down, None, 0, cols, None)], (g, 1),
             q2, [(h1, None, cols, size, None)],
         ),
         (shape(2, 9 * ch, ch),), [x_scratch(1)], (token,), True,
@@ -445,26 +440,26 @@
 
     spans = ((0, 2, adv, 0), (2, 2, loss, (0, 1)), (4, 1, adv, 1), (5, 1, loss, (0, 0)))
     half = 6 * cols
-    last, others = ((last_section, True), (last_section, False))
     picks = [
         [
-            (came_edges, None, first + start * cols, n * cols, others),
-            (own, index, size - n * cols if first else 0, n * cols, last),
+            (came_edges, None, first + start * cols, n * cols, False),
+            (own, index, size - n * cols if first else 0, n * cols, True),
         ]
         for first in (half, 0)
         for start, n, own, index in spans
     ]
-    edges1 = swap(*kernel(pick, at, picks, (e6, e6)))
+    bottom, top = kernel(pick, at, picks, (e6, e6))
+    up, down = up_down(bottom, top)
     inner, outer = (size - 2 * edge, size - edge)
 
     def came_field(k):
         start, n, own, index = spans[k]
         mid = came_mids[k % 2]
         return extended(start, n, [
-            (came_edges, None, start * cols, n * cols, others),
-            (mid, None, 0, inner, others) if k < 2 else (mid, None, inner, outer, others),
-            (came_edges, None, half + start * cols, n * cols, others), (own, index, 0, size, last),
-        ], edges1)
+            (came_edges, None, start * cols, n * cols, False),
+            (mid, None, 0, inner, False) if k < 2 else (mid, None, inner, outer, False),
+            (came_edges, None, half + start * cols, n * cols, False), (own, index, 0, size, True),
+        ], up, down)
 
     last_adv, ahead, token = kernel(
         functools.partial(advance, cols, 0), at, (q, p, w_f, w_g, (fresh, 3), (fresh, 2)),

time: 135 us -> 135 us (level)
  starting transfers between devices: 66.5 us -> 56.1 us
  waiting for transfers between devices: 30.8 us -> 40.4 us
  local copies, waits for them, and re-layouts: 3.92 us -> 5.53 us
  Pallas kernels: 32 us -> 30.5 us
    ppermute x1, starting transfers between devices: 23.1 us -> 1.93 us  [over_bands(): came = lax.ppermute(send, 'band', [(i, i ^ 8) for i in range(bands)])]
    ppermute x1, waiting for transfers between devices: 3.24 us -> 17.7 us  [over_bands(): came = lax.ppermute(send, 'band', [(i, i ^ 8) for i in range(bands)])]
    ppermute x6, starting transfers between devices: 15.1 us -> 25.5 us  [the longest x3 19.8 us: up_down(): lax.ppermute(top, 'band', [(i + 1, i) for i in range(bands - 1)])]
    ppermute x7, waiting for transfers between devices: 12.2 us -> 6.26 us  [along(): return lax.ppermute(block, 'segment', route)]
    unnamed x20, local copies, waits for them, and re-layouts: 3.13 us -> 5.49 us
    ppermute x7, starting transfers between devices: 22.9 us -> 25.2 us  [along(): return lax.ppermute(block, 'segment', route)]
    ppermute x3, starting transfers between devices: 5.37 us -> 3.34 us  [on_x(): lax.ppermute(piece, 'band', [(i, i & 8 | ((i >> 1 & 3) + step) % 4 << 1 |...]
  transfers between devices with their start and end apart: 18 -> 18, of which waited for: 6 -> 8; matrix products, arithmetic and copies ran while one was open for 1% -> 0% of each run, Pallas kernels for 16% -> 16%
where the time goes in v4:
time: 135 us; the launch traced here: 134 us
  starting transfers between devices  56.1 us (42%)
  waiting for transfers between devices  40.4 us (30%)
  Pallas kernels  30.5 us (23%)
  local copies, waits for them, and re-layouts  5.53 us (4%)
    pallas_call x11, Pallas kernels, kernel(): pl.pallas_call(run, out_shape=outs, in_specs=[VMEM] * len(after) + [SMEM]...  26.2 us
    ppermute x7, starting transfers between devices, along(): return lax.ppermute(block, 'segment', route)  25.2 us
    ppermute x3, starting transfers between devices, up_down(): lax.ppermute(top, 'band', [(i + 1, i) for i in range(bands - 1)])  19.8 us
    ppermute x1, waiting for transfers between devices, over_bands(): came = lax.ppermute(send, 'band', [(i, i ^ 8) for i in range(bands)])  17.7 us
    ppermute x3, waiting for transfers between devices, on_x(): lax.ppermute(piece, 'band', [(i, i & 8 | ((i >> 1 & 3) + step) % 4 << 1 |...  13.6 us
    ppermute x7, waiting for transfers between devices, along(): return lax.ppermute(block, 'segment', route)  6.26 us
    ppermute x3, starting transfers between devices, up_down(): lax.ppermute(bottom, 'band', [(i, i + 1) for i in range(bands - 1)])  5.75 us
    unnamed x20, local copies, waits for them, and re-layouts  5.49 us
  transfers between devices with their start and end apart: 18, of which 8 were waited for; matrix products, arithmetic and copies ran while one was open for 0% of the time, Pallas kernels for 16%

profile of v4, /device:TPU:18, one launch (start us, length us, event | category | flops | bytes accessed | tf_op | source)
XLA Modules:
  0.0 133.7 jit_solution(7693574877040418112)
XLA Ops:
  0.6 2.4 %pack_edges.1 = (bf16[576,256]{1,0:T(8,128)(2,1)}, bf16[576,256]{1,0:T(8,128)(2,1)}, bf16[448,256]{1,0:T(8,128)(2,1)}, bf16[448,256]{1,0:T(8,128)(2,1)}) custom-call(bf16[2,512,256]{2,1,0:T(8,128)(2,1)} %bitcast.24, bf16[2,512,256]{2,1,0:T(8,128)(2,1)} %bitcast.30, bf16[2,512,256]{2,1,0:T(8,128)(2,1)} %bitcast.25, bf16[2,512,256]{2,1,0:T(8,128)(2,1)} %bitcast.31, ...), custom_call_target="tpu_custom_call" | custom-call | flops 1000 | bytes 1000 | tf_op jit(solution)/shard_map/pack_edges/pallas_call | solution.py:389
  5.0 3.6 %collective-permute-start.9 = (bf16[576,256]{1,0:T(8,128)(2,1)}, bf16[576,256]{1,0:T(8,128)(2,1)S(1)}, u32[]{:S(2)}, u32[]{:S(2)}) collective-permute-start(bf16[576,256]{1,0:T(8,128)(2,1)} %get-tuple-element.58), channel_id=1, source_target_pairs={{1,0},{2,1},{3,2},{4,3},{5,4},{6,5},{7,6},{8,7},{9,8},{10,9},{11,1... | collective-permute-start | bytes 884744 | tf_op jit(solution)/shard_map/ppermute | solution.py:357
  8.6 1.9 %collective-permute-start.6 = (bf16[448,256]{1,0:T(8,128)(2,1)}, bf16[448,256]{1,0:T(8,128)(2,1)S(1)}, u32[]{:S(2)}, u32[]{:S(2)}) collective-permute-start(bf16[448,256]{1,0:T(8,128)(2,1)} %get-tuple-element.55), channel_id=1, source_target_pairs={{0,1},{1,2},{2,3},{3,4},{4,5},{5,6},{6,7},{7,8},{8,9},{9,10},{10,1... | collective-permute-start | bytes 688136 | tf_op jit(solution)/shard_map/ppermute | solution.py:356
  10.6 3.6 %collective-permute-start.7 = (bf16[448,256]{1,0:T(8,128)(2,1)}, bf16[448,256]{1,0:T(8,128)(2,1)S(1)}, u32[]{:S(2)}, u32[]{:S(2)}) collective-permute-start(bf16[448,256]{1,0:T(8,128)(2,1)} %get-tuple-element.56), channel_id=1, source_target_pairs={{1,0},{2,1},{3,2},{4,3},{5,4},{6,5},{7,6},{8,7},{9,8},{10,9},{11,1... | collective-permute-start | bytes 688136 | tf_op jit(solution)/shard_map/ppermute | solution.py:357
  15.6 4.0 %invert.1 = (bf16[640,256]{1,0:T(8,128)(2,1)S(1)}, bf16[640,256]{1,0:T(8,128)(2,1)S(1)}, bf16[768,256]{1,0:T(8,128)(2,1)S(1)}, bf16[640,256]{1,0:T(8,128)(2,1)S(1)}, bf16[640,256]{1,0:T(8,128)(2,1)S(1)}) custom-call(s32[4]{0:T(128)S(1)} %pad_add_fusion.refs_0_.refs_1_.at_ref, bf16[576,256]{1,0:T(8,128)(2,1)S(1)} %collective-permute-done.8.refs_1_.refs_5_.refs_2_, ...), custom_call_target="tpu_custom_call" | custom-call | flops 1000 | bytes 1000 | tf_op jit(solution)/shard_map/invert/pallas_call | solution.py:82
  19.6 8.1 %collective-permute-start.12 = (bf16[768,256]{1,0:T(8,128)(2,1)S(1)}, bf16[768,256]{1,0:T(8,128)(2,1)S(1)}, u32[]{:S(2)}, u32[]{:S(2)}) collective-permute-start(bf16[768,256]{1,0:T(8,128)(2,1)S(1)} %get-tuple-element.68), channel_id=1, source_target_pairs={{16,0},{32,16},{48,32},{64,48},{80,64},{96,80},{112,96},{128,112},... | collective-permute-start | bytes 1179656 | tf_op jit(solution)/shard_map/ppermute | solution.py:365
  27.7 4.8 %advance.2 = (bf16[2,512,256]{2,1,0:T(8,128)(2,1)S(1)}, bf16[768,256]{1,0:T(8,128)(2,1)S(1)}, bf16[640,256]{1,0:T(8,128)(2,1)S(1)}, bf16[640,256]{1,0:T(8,128)(2...) custom-call(s32[4]{0:T(128)S(1)} %pad_add_fusion.refs_0_.refs_1_.at_ref, ...), custom_call_target="tpu_custom_call" | custom-call | flops 1000 | bytes 1000 | tf_op jit(solution)/shard_map/advance/pallas_call | solution.py:82
  34.2 5.4 %collective-permute-start.14 = (bf16[640,256]{1,0:T(8,128)(2,1)S(1)}, bf16[640,256]{1,0:T(8,128)(2,1)S(1)}, u32[]{:S(2)}, u32[]{:S(2)}) collective-permute-start(bf16[640,256]{1,0:T(8,128)(2,1)S(1)} %get-tuple-element.71), channel_id=1, source_target_pairs={{16,0},{32,16},{48,32},{64,48},{80,64},{96,80},{112,96},{128,112},... | collective-permute-start | bytes 983048 | tf_op jit(solution)/shard_map/ppermute | solution.py:365
  39.6 4.7 %collective-permute-start.16 = (bf16[640,256]{1,0:T(8,128)(2,1)S(1)}, bf16[640,256]{1,0:T(8,128)(2,1)S(1)}, u32[]{:S(2)}, u32[]{:S(2)}) collective-permute-start(bf16[640,256]{1,0:T(8,128)(2,1)S(1)} %get-tuple-element.73), channel_id=1, source_target_pairs={{16,0},{32,16},{48,32},{64,48},{80,64},{96,80},{112,96},{128,112},... | collective-permute-start | bytes 983048 | tf_op jit(solution)/shard_map/ppermute | solution.py:365
  44.4 4.1 %collective-permute-done.12.refs_1_.refs_2_ = bf16[768,256]{1,0:T(8,128)(2,1)S(1)} collective-permute-done((bf16[768,256]{1,0:T(8,128)(2,1)S(1)}, bf16[768,256]{1,0:T(8,128)(2,1)S(1)}, u32[]{:S(2)}, u32[]{:S(2)}) %collective-permute-start.12) | collective-permute-done | bytes 393248 | tf_op jit(solution)/shard_map/ppermute | solution.py:365
  49.1 1.9 %collective-permute-start.13 = (bf16[384,256]{1,0:T(8,128)(2,1)S(1)}, bf16[384,256]{1,0:T(8,128)(2,1)S(1)}, u32[]{:S(2)}, u32[]{:S(2)}) collective-permute-start(bf16[384,256]{1,0:T(8,128)(2,1)S(1)} %get-tuple-element.70), channel_id=1, source_target_pairs={{0,1},{1,2},{2,3},{3,4},{4,5},{5,6},{6,7},{7,8},{8,9},{9,10},{10,1... | collective-permute-start | bytes 589832 | tf_op jit(solution)/shard_map/ppermute | solution.py:356
  51.0 12.5 %collective-permute-start.15 = (bf16[384,256]{1,0:T(8,128)(2,1)S(1)}, bf16[384,256]{1,0:T(8,128)(2,1)S(1)}, u32[]{:S(2)}, u32[]{:S(2)}) collective-permute-start(bf16[384,256]{1,0:T(8,128)(2,1)S(1)} %get-tuple-element.72), channel_id=1, source_target_pairs={{1,0},{2,1},{3,2},{4,3},{5,4},{6,5},{7,6},{8,7},{9,8},{10,9},{11,1... | collective-permute-start | bytes 589832 | tf_op jit(solution)/shard_map/ppermute | solution.py:357
  63.5 2.1 %weight_terms.1 = (bf16[2,2304,256]{2,1,0:T(8,128)(2,1)S(1)}, f32[8,128]{1,0:T(8,128)S(1)}) custom-call(f32[8,128]{1,0:T(8,128)S(1)} %get-tuple-element.61.refs_0_, s32[4]{0:T(128)S(1)} %pad_add_fusion.refs_0_.refs_1_.at_ref, bf16[576,256]{1,0:T(8,128)(2,1)S(1)} %collective-permute-done.8.refs_1_.refs_5_.refs_2_, bf16[2,512,256]{2,1,0:T(8,128)(2,1)S(1)} %bitcast.29, ...), custom_call_target="tpu_custom_call" | custom-call | flops 1000 | bytes 1000 | tf_op jit(solution)/shard_map/weight_terms/pallas_call | solution.py:82
  68.1 3.6 %advance.3 = (bf16[2,512,256]{2,1,0:T(8,128)(2,1)S(1)}, bf16[2,512,256]{2,1,0:T(8,128)(2,1)S(1)}, f32[8,128]{1,0:T(8,128)S(1)}) custom-call(f32[8,128]{1,0:T(8,128)S(1)} %get-tuple-element.64.refs_0_, s32[4]{0:T(128)S(1)} %pad_add_fusion.refs_0_.refs_1_.at_ref, bf16[768,256]{1,0:T(8,128)(2,1)S(1)} %collective-permute-done.10.refs_2_, ...), custom_call_target="tpu_custom_call" | custom-call | flops 1000 | bytes 1000 | tf_op jit(solution)/shard_map/advance/pallas_call | solution.py:82
  72.9 5.1 %invert_last.1 = (bf16[4,512,256]{2,1,0:T(8,128)(2,1)}, bf16[4,640,256]{2,1,0:T(8,128)(2,1)S(1)}) custom-call(s32[4]{0:T(128)S(1)} %pad_add_fusion.refs_0_.refs_1_.at_ref, bf16[384,256]{1,0:T(8,128)(2,1)S(1)} %collective-permute-done.13.refs_1_, bf16[768,256]{1,0:T(8,128)(2,1)S(1)} %collective-permute-done.12.refs_1_.refs_2_, ...), custom_call_target="tpu_custom_call" | custom-call | flops 1000 | bytes 1000 | tf_op jit(solution)/shard_map/invert_last/pallas_call | solution.py:82
  79.0 5.2 %collective-permute-start.17 = (bf16[4,512,256]{2,1,0:T(8,128)(2,1)}, bf16[4,512,256]{2,1,0:T(8,128)(2,1)S(1)}, u32[]{:S(2)}, u32[]{:S(2)}) collective-permute-start(bf16[4,512,256]{2,1,0:T(8,128)(2,1)} %get-tuple-element.80), channel_id=1, source_target_pairs={{0,240},{16,0},{32,16},{48,32},{64,48},{80,64},{96,80},{112,96},{1... | collective-permute-start | bytes 3145736 | tf_op jit(solution)/shard_map/ppermute | solution.py:365
  87.2 2.3 %weight_sums.1 = (f32[2,8,144,256]{3,2,1,0:T(8,128)S(1)}, bf16[2,8,144,256]{3,2,1,0:T(8,128)(2,1)S(1)}) custom-call(s32[4]{0:T(128)S(1)} %pad_add_fusion.refs_0_.refs_1_.at_ref, bf16[4,640,256]{2,1,0:T(8,128)(2,1)S(1)} %copy-done.9, bf16[2,2304,256]{2,1,0:T(8,128)(2,1)S(1)} %copy-done.7), custom_call_target="tpu_custom_call" | custom-call | flops 1000 | bytes 1000 | tf_op jit(solution)/shard_map/weight_sums/pallas_call | solution.py:82
  89.5 42.2 %conditional.1 = (f32[2,144,256]{2,1,0:T(8,128)S(1)}, bf16[2,512,256]{2,1,0:T(8,128)(2,1)S(1)}) conditional(s32[]{:T(128)} %convert_element_type.6, bf16[2,512,256]{2,1,0:T(8,128)(2,1)S(1)} %get-tuple-element.67, (bf16[2,8,144,256]{3,2,1,0:T(8,128)(2,1)S(1)}, s32[4]{0:T(128)S(1)}, f32[2,8,144,256]{3,2,1,0:T(8,128)S(1)}, ...), branch_computations={%region_0.0_spmd, %region_1.0_spmd} | conditional | flops 149456 | bytes 12732624 | solution.py:502
  89.7 2.7 %collective-permute-done.refs_2_ = bf16[2,8,144,256]{3,2,1,0:T(8,128)(2,1)S(1)} collective-permute-done((bf16[2,8,144,256]{3,2,1,0:T(8,128)(2,1)S(1)}, bf16[2,8,144,256]{3,2,1,0:T(8,128)(2,1)S(1)}, u32[]{:S(2)}, u32[]{:S(2)}) %collective-permute-start) | collective-permute-done | bytes 1179680 | tf_op jit(solution)/shard_map/cond/branch_1_fun/ppermute | solution.py:490
  94.6 2.0 %collective-permute-start.3 = (bf16[2,2,144,256]{3,2,1,0:T(8,128)(2,1)S(1)}, bf16[2,2,144,256]{3,2,1,0:T(8,128)(2,1)S(1)}, u32[]{:S(2)}, u32[]{:S(2)}) collective-permute-start(bf16[2,2,144,256]{3,2,1,0:T(8,128)(2,1)S(1)} %get-tuple-element.15), channel_id=1, source_target_pairs={{0,6},{1,7},{2,0},{3,1},{4,2},{5,3},{6,4},{7,5},{8,14},{9,15},{10,... | collective-permute-start | bytes 884744 | tf_op jit(solution)/shard_map/cond/branch_1_fun/ppermute | solution.py:484
  96.6 8.1 %collective-permute-done.1.refs_2_ = bf16[2,2,144,256]{3,2,1,0:T(8,128)(2,1)S(1)} collective-permute-done((bf16[2,2,144,256]{3,2,1,0:T(8,128)(2,1)S(1)}, bf16[2,2,144,256]{3,2,1,0:T(8,128)(2,1)S(1)}, u32[]{:S(2)}, u32[]{:S(2)}) %collective-permute-start.1) | collective-permute-done | bytes 294944 | tf_op jit(solution)/shard_map/cond/branch_1_fun/ppermute | solution.py:484
  104.7 5.2 %collective-permute-done.2.refs_3_ = bf16[2,2,144,256]{3,2,1,0:T(8,128)(2,1)S(1)} collective-permute-done((bf16[2,2,144,256]{3,2,1,0:T(8,128)(2,1)S(1)}, bf16[2,2,144,256]{3,2,1,0:T(8,128)(2,1)S(1)}, u32[]{:S(2)}, u32[]{:S(2)}) %collective-permute-start.2) | collective-permute-done | bytes 294944 | tf_op jit(solution)/shard_map/cond/branch_1_fun/ppermute | solution.py:484
  110.9 1.9 %collective-permute-start.4 = (bf16[2,144,256]{2,1,0:T(8,128)(2,1)S(1)}, bf16[2,144,256]{2,1,0:T(8,128)(2,1)S(1)}, u32[]{:S(2)}, u32[]{:S(2)}) collective-permute-start(bf16[2,144,256]{2,1,0:T(8,128)(2,1)S(1)} %get-tuple-element.17), channel_id=1, source_target_pairs={{0,8},{1,9},{2,10},{3,11},{4,12},{5,13},{6,14},{7,15},{8,0},{9,1},... | collective-permute-start | bytes 442376 | tf_op jit(solution)/shard_map/cond/branch_1_fun/ppermute | solution.py:499
  113.9 17.7 %collective-permute-done.4 = bf16[2,144,256]{2,1,0:T(8,128)(2,1)S(1)} collective-permute-done((bf16[2,144,256]{2,1,0:T(8,128)(2,1)S(1)}, bf16[2,144,256]{2,1,0:T(8,128)(2,1)S(1)}, u32[]{:S(2)}, u32[]{:S(2)}) %collective-permute-start.4) | collective-permute-done | bytes 147488 | tf_op jit(solution)/shard_map/cond/branch_1_fun/ppermute | solution.py:499
  (50 shorter events, 19.4 us)
Async XLA Ops:
  0.6 13.7 %copy-start = (bf16[1,2,2304,256]{3,2,1,0:T(8,128)(2,1)S(1)}, bf16[1,2,2304,256]{3,2,1,0:T(8,128)(2,1)}, u32[]{:S(2)}) copy-start(bf16[1,2,2304,256]{3,2,1,0:T(8,128)(2,1)} %param.11) | copy-start | bytes 7077892
  3.1 12.5 %collective-permute-start.8 = (bf16[576,256]{1,0:T(8,128)(2,1)}, bf16[576,256]{1,0:T(8,128)(2,1)S(1)}, u32[]{:S(2)}, u32[]{:S(2)}) collective-permute-start(bf16[576,256]{1,0:T(8,128)(2,1)} %get-tuple-element.57), channel_id=1, source_target_pairs={{0,1},{1,2},{2,3},{3,4},{4,5},{5,6},{6,7},{7,8},{8,9},{9,10},{10,1... | collective-permute-start | bytes 884744 | tf_op jit(solution)/shard_map/ppermute | solution.py:356
  5.0 10.6 %collective-permute-start.9 = (bf16[576,256]{1,0:T(8,128)(2,1)}, bf16[576,256]{1,0:T(8,128)(2,1)S(1)}, u32[]{:S(2)}, u32[]{:S(2)}) collective-permute-start(bf16[576,256]{1,0:T(8,128)(2,1)} %get-tuple-element.58), channel_id=1, source_target_pairs={{1,0},{2,1},{3,2},{4,3},{5,4},{6,5},{7,6},{8,7},{9,8},{10,9},{11,1... | collective-permute-start | bytes 884744 | tf_op jit(solution)/shard_map/ppermute | solution.py:357
  8.6 19.1 %collective-permute-start.6 = (bf16[448,256]{1,0:T(8,128)(2,1)}, bf16[448,256]{1,0:T(8,128)(2,1)S(1)}, u32[]{:S(2)}, u32[]{:S(2)}) collective-permute-start(bf16[448,256]{1,0:T(8,128)(2,1)} %get-tuple-element.55), channel_id=1, source_target_pairs={{0,1},{1,2},{2,3},{3,4},{4,5},{5,6},{6,7},{7,8},{8,9},{9,10},{10,1... | collective-permute-start | bytes 688136 | tf_op jit(solution)/shard_map/ppermute | solution.py:356
  10.6 17.1 %collective-permute-start.7 = (bf16[448,256]{1,0:T(8,128)(2,1)}, bf16[448,256]{1,0:T(8,128)(2,1)S(1)}, u32[]{:S(2)}, u32[]{:S(2)}) collective-permute-start(bf16[448,256]{1,0:T(8,128)(2,1)} %get-tuple-element.56), channel_id=1, source_target_pairs={{1,0},{2,1},{3,2},{4,3},{5,4},{6,5},{7,6},{8,7},{9,8},{10,9},{11,1... | collective-permute-start | bytes 688136 | tf_op jit(solution)/shard_map/ppermute | solution.py:357
  15.5 12.2 %copy-start.1 = (bf16[2,2,8,64,256]{4,3,2,1,0:T(8,128)(2,1)S(1)}, bf16[2,2,8,64,256]{4,3,2,1,0:T(8,128)(2,1)}, u32[]{:S(2)}) copy-start(bf16[2,2,8,64,256]{4,3,2,1,0:T(8,128)(2,1)} %param.12) | copy-start | bytes 3145732
  15.5 12.2 %copy-start.4 = (bf16[1,2,8,64,256]{4,3,2,1,0:T(8,128)(2,1)S(1)}, bf16[1,2,8,64,256]{4,3,2,1,0:T(8,128)(2,1)}, u32[]{:S(2)}) copy-start(bf16[1,2,8,64,256]{4,3,2,1,0:T(8,128)(2,1)} %param.8) | copy-start | bytes 1572868
  19.6 28.9 %collective-permute-start.12 = (bf16[768,256]{1,0:T(8,128)(2,1)S(1)}, bf16[768,256]{1,0:T(8,128)(2,1)S(1)}, u32[]{:S(2)}, u32[]{:S(2)}) collective-permute-start(bf16[768,256]{1,0:T(8,128)(2,1)S(1)} %get-tuple-element.68), channel_id=1, source_target_pairs={{16,0},{32,16},{48,32},{64,48},{80,64},{96,80},{112,96},{128,112},... | collective-permute-start | bytes 1179656 | tf_op jit(solution)/shard_map/ppermute | solution.py:365
  27.7 20.8 %copy-start.5 = (bf16[2,2,8,64,256]{4,3,2,1,0:T(8,128)(2,1)S(1)}, bf16[2,2,8,64,256]{4,3,2,1,0:T(8,128)(2,1)}, u32[]{:S(2)}) copy-start(bf16[2,2,8,64,256]{4,3,2,1,0:T(8,128)(2,1)} %param.13) | copy-start | bytes 3145732
  32.5 18.5 %collective-permute-start.11 = (bf16[640,256]{1,0:T(8,128)(2,1)S(1)}, bf16[640,256]{1,0:T(8,128)(2,1)S(1)}, u32[]{:S(2)}, u32[]{:S(2)}) collective-permute-start(bf16[640,256]{1,0:T(8,128)(2,1)S(1)} %get-tuple-element.66), channel_id=1, source_target_pairs={{0,16},{16,32},{32,48},{48,64},{64,80},{80,96},{96,112},{112,128},... | collective-permute-start | bytes 983048 | tf_op jit(solution)/shard_map/ppermute | solution.py:365
  32.6 35.5 %collective-permute-start.10 = (bf16[768,256]{1,0:T(8,128)(2,1)S(1)}, bf16[768,256]{1,0:T(8,128)(2,1)S(1)}, u32[]{:S(2)}, u32[]{:S(2)}) collective-permute-start(bf16[768,256]{1,0:T(8,128)(2,1)S(1)} %get-tuple-element.65), channel_id=1, source_target_pairs={{0,16},{16,32},{32,48},{48,64},{64,80},{80,96},{96,112},{112,128},... | collective-permute-start | bytes 1179656 | tf_op jit(solution)/shard_map/ppermute | solution.py:365
  34.2 38.7 %collective-permute-start.14 = (bf16[640,256]{1,0:T(8,128)(2,1)S(1)}, bf16[640,256]{1,0:T(8,128)(2,1)S(1)}, u32[]{:S(2)}, u32[]{:S(2)}) collective-permute-start(bf16[640,256]{1,0:T(8,128)(2,1)S(1)} %get-tuple-element.71), channel_id=1, source_target_pairs={{16,0},{32,16},{48,32},{64,48},{80,64},{96,80},{112,96},{128,112},... | collective-permute-start | bytes 983048 | tf_op jit(solution)/shard_map/ppermute | solution.py:365
  39.6 33.3 %collective-permute-start.16 = (bf16[640,256]{1,0:T(8,128)(2,1)S(1)}, bf16[640,256]{1,0:T(8,128)(2,1)S(1)}, u32[]{:S(2)}, u32[]{:S(2)}) collective-permute-start(bf16[640,256]{1,0:T(8,128)(2,1)S(1)} %get-tuple-element.73), channel_id=1, source_target_pairs={{16,0},{32,16},{48,32},{64,48},{80,64},{96,80},{112,96},{128,112},... | collective-permute-start | bytes 983048 | tf_op jit(solution)/shard_map/ppermute | solution.py:365
  49.1 23.8 %collective-permute-start.13 = (bf16[384,256]{1,0:T(8,128)(2,1)S(1)}, bf16[384,256]{1,0:T(8,128)(2,1)S(1)}, u32[]{:S(2)}, u32[]{:S(2)}) collective-permute-start(bf16[384,256]{1,0:T(8,128)(2,1)S(1)} %get-tuple-element.70), channel_id=1, source_target_pairs={{0,1},{1,2},{2,3},{3,4},{4,5},{5,6},{6,7},{7,8},{8,9},{9,10},{10,1... | collective-permute-start | bytes 589832 | tf_op jit(solution)/shard_map/ppermute | solution.py:356
  51.0 21.9 %collective-permute-start.15 = (bf16[384,256]{1,0:T(8,128)(2,1)S(1)}, bf16[384,256]{1,0:T(8,128)(2,1)S(1)}, u32[]{:S(2)}, u32[]{:S(2)}) collective-permute-start(bf16[384,256]{1,0:T(8,128)(2,1)S(1)} %get-tuple-element.72), channel_id=1, source_target_pairs={{1,0},{2,1},{3,2},{4,3},{5,4},{6,5},{7,6},{8,7},{9,8},{10,9},{11,1... | collective-permute-start | bytes 589832 | tf_op jit(solution)/shard_map/ppermute | solution.py:357
  65.6 1.4 %copy-start.6 = (bf16[2,2304,256]{2,1,0:T(8,128)(2,1)}, bf16[2,2304,256]{2,1,0:T(8,128)(2,1)S(1)}, u32[]{:S(2)}) copy-start(bf16[2,2304,256]{2,1,0:T(8,128)(2,1)S(1)} %get-tuple-element.76.refs_2_) | copy-start | bytes 7077892
  79.0 52.7 %collective-permute-start.17 = (bf16[4,512,256]{2,1,0:T(8,128)(2,1)}, bf16[4,512,256]{2,1,0:T(8,128)(2,1)S(1)}, u32[]{:S(2)}, u32[]{:S(2)}) collective-permute-start(bf16[4,512,256]{2,1,0:T(8,128)(2,1)} %get-tuple-element.80), channel_id=1, source_target_pairs={{0,240},{16,0},{32,16},{48,32},{64,48},{80,64},{96,80},{112,96},{1... | collective-permute-start | bytes 3145736 | tf_op jit(solution)/shard_map/ppermute | solution.py:365
  84.2 1.7 %copy-start.7 = (bf16[2,2304,256]{2,1,0:T(8,128)(2,1)S(1)}, bf16[2,2304,256]{2,1,0:T(8,128)(2,1)}, u32[]{:S(2)}) copy-start(bf16[2,2304,256]{2,1,0:T(8,128)(2,1)} %copy-done.6) | copy-start | bytes 7077892
  89.5 2.9 %collective-permute-start = (bf16[2,8,144,256]{3,2,1,0:T(8,128)(2,1)S(1)}, bf16[2,8,144,256]{3,2,1,0:T(8,128)(2,1)S(1)}, u32[]{:S(2)}, u32[]{:S(2)}) collective-permute-start(bf16[2,8,144,256]{3,2,1,0:T(8,128)(2,1)S(1)} %get-tuple-element.11), channel_id=1, source_target_pairs={{0,1},{1,0},{2,3},{3,2},{4,5},{5,4},{6,7},{7,6},{8,9},{9,8},{10,11... | collective-permute-start | bytes 3538952 | tf_op jit(solution)/shard_map/cond/branch_1_fun/ppermute | solution.py:490
  89.6 24.3 %collective-permute-start.5 = (bf16[2,512,256]{2,1,0:T(8,128)(2,1)S(1)}, bf16[2,512,256]{2,1,0:T(8,128)(2,1)S(1)}, u32[]{:S(2)}, u32[]{:S(2)}) collective-permute-start(bf16[2,512,256]{2,1,0:T(8,128)(2,1)S(1)} %get-tuple-element.18), channel_id=1, source_target_pairs={{0,16},{16,32},{32,48},{48,64},{64,80},{80,96},{96,112},{112,128},... | collective-permute-start | bytes 1572872 | tf_op jit(solution)/shard_map/cond/branch_1_fun/ppermute | solution.py:365
  93.2 11.5 %collective-permute-start.1 = (bf16[2,2,144,256]{3,2,1,0:T(8,128)(2,1)S(1)}, bf16[2,2,144,256]{3,2,1,0:T(8,128)(2,1)S(1)}, u32[]{:S(2)}, u32[]{:S(2)}) collective-permute-start(bf16[2,2,144,256]{3,2,1,0:T(8,128)(2,1)S(1)} %get-tuple-element.13), channel_id=1, source_target_pairs={{0,4},{1,5},{2,6},{3,7},{4,0},{5,1},{6,2},{7,3},{8,12},{9,13},{10,... | collective-permute-start | bytes 884744 | tf_op jit(solution)/shard_map/cond/branch_1_fun/ppermute | solution.py:484
  94.3 15.7 %collective-permute-start.2 = (bf16[2,2,144,256]{3,2,1,0:T(8,128)(2,1)S(1)}, bf16[2,2,144,256]{3,2,1,0:T(8,128)(2,1)S(1)}, u32[]{:S(2)}, u32[]{:S(2)}) collective-permute-start(bf16[2,2,144,256]{3,2,1,0:T(8,128)(2,1)S(1)} %get-tuple-element.14), channel_id=1, source_target_pairs={{0,2},{1,3},{2,4},{3,5},{4,6},{5,7},{6,0},{7,1},{8,10},{9,11},{10,... | collective-permute-start | bytes 884744 | tf_op jit(solution)/shard_map/cond/branch_1_fun/ppermute | solution.py:484
  94.6 15.6 %collective-permute-start.3 = (bf16[2,2,144,256]{3,2,1,0:T(8,128)(2,1)S(1)}, bf16[2,2,144,256]{3,2,1,0:T(8,128)(2,1)S(1)}, u32[]{:S(2)}, u32[]{:S(2)}) collective-permute-start(bf16[2,2,144,256]{3,2,1,0:T(8,128)(2,1)S(1)} %get-tuple-element.15), channel_id=1, source_target_pairs={{0,6},{1,7},{2,0},{3,1},{4,2},{5,3},{6,4},{7,5},{8,14},{9,15},{10,... | collective-permute-start | bytes 884744 | tf_op jit(solution)/shard_map/cond/branch_1_fun/ppermute | solution.py:484
  110.9 20.8 %collective-permute-start.4 = (bf16[2,144,256]{2,1,0:T(8,128)(2,1)S(1)}, bf16[2,144,256]{2,1,0:T(8,128)(2,1)S(1)}, u32[]{:S(2)}, u32[]{:S(2)}) collective-permute-start(bf16[2,144,256]{2,1,0:T(8,128)(2,1)S(1)} %get-tuple-element.17), channel_id=1, source_target_pairs={{0,8},{1,9},{2,10},{3,11},{4,12},{5,13},{6,14},{7,15},{8,0},{9,1},... | collective-permute-start | bytes 442376 | tf_op jit(solution)/shard_map/cond/branch_1_fun/ppermute | solution.py:499
  (4 other events, 4.9 us)

commit v5 on v3

--- a/solution.py
+++ b/solution.py
@@ -317,11 +317,15 @@
             out[k] = value.astype(out.dtype)
 
 
-def place_outputs(at_ref, ahead_ref, back_ref, adv_ref, grad_ref,
-                  forward_ref, returning_ref, backward_ref, weight_ref, held, sem):
+def place_forward(ahead_ref, forward_ref, sem):
+    copy = pltpu.make_async_copy(ahead_ref, forward_ref, sem)
+    copy.start()
+    copy.wait()
+
+
+def place_outputs(at_ref, back_ref, adv_ref, grad_ref, returning_ref, backward_ref, weight_ref, held, sem):
     last = last_section(at_ref)
     copies = [
-        pltpu.make_async_copy(ahead_ref, forward_ref, sem.at[0]),
         pltpu.make_async_copy(back_ref.at[pl.ds(2, 2)], backward_ref, sem.at[1]),
         pltpu.make_async_copy(grad_ref, weight_ref, sem.at[3]),
     ]
@@ -502,20 +506,24 @@
             sum_chips, at, (own, far, right, left), (shape(2, part, ch), shape(2, part, ch, dtype=F32))
         )
         came = lax.ppermute(send, "band", [(i, i ^ 8) for i in range(bands)])
-        return keep + came.astype(F32), came_ahead
-
-    weight_grad, came_ahead = lax.cond(
+        forward = pl.pallas_call(
+            place_forward, out_shape=pair, in_specs=[VMEM], out_specs=ANY, scratch_shapes=[pltpu.SemaphoreType.DMA],
+            cost_estimate=LITTLE, name="place_forward",
+        )(came_ahead)
+        return keep + came.astype(F32), forward
+
+    weight_grad, forward = lax.cond(
         seg < segments, over_bands, lambda send, keep, ahead, at: (jnp.zeros((2, part, ch), F32), ahead),
         send, keep, ahead, at,
     )
 
-    *outputs, weight_grad = pl.pallas_call(
-        place_outputs, out_shape=[pair] * 3 + [shape(2, part, ch, dtype=F32)], in_specs=[SMEM] + [VMEM] * 2 + [ANY, VMEM],
-        out_specs=[ANY] * 4,
+    returning, backward, weight_grad = pl.pallas_call(
+        place_outputs, out_shape=[pair] * 2 + [shape(2, part, ch, dtype=F32)], in_specs=[SMEM, VMEM, ANY, VMEM],
+        out_specs=[ANY] * 3,
         scratch_shapes=[pltpu.VMEM((2, size, ch), BF16), pltpu.SemaphoreType.DMA((5,))], cost_estimate=LITTLE,
         compiler_params=pltpu.CompilerParams(vmem_limit_bytes=8 << 20), name="place_outputs",
-    )(at, came_ahead, came_back, last_adv, weight_grad)
-    return (*[out.reshape(full) for out in outputs], weight_grad[None])
+    )(at, came_back, last_adv, weight_grad)
+    return (forward.reshape(full), returning.reshape(full), backward.reshape(full), weight_grad[None])
 
 
 def solution(mesh):

time: 135 us -> 134 us (level)
  waiting for transfers between devices: 30.8 us -> 29.2 us
  Pallas kernels: 32 us -> 33.4 us
    ppermute x1, waiting for transfers between devices: 3.24 us -> 1.38 us  [over_bands(): came = lax.ppermute(send, 'band', [(i, i ^ 8) for i in range(bands)])]
    pallas_call x1 -> x2, Pallas kernels: 2.33 us -> 3.49 us  [the longest x1 1.84 us: over_bands(): pl.pallas_call(place_forward, out_shape=pair, in_specs=[VMEM], out_specs=...]
  transfers between devices with their start and end apart: 18 -> 18, of which waited for: 6 -> 6; matrix products, arithmetic and copies ran while one was open for 1% -> 0% of each run, Pallas kernels for 16% -> 18%
where the time goes in v5:
time: 134 us
  starting transfers between devices  66.3 us (49%)
  Pallas kernels  33.4 us (25%)
  waiting for transfers between devices  29.2 us (22%)
  local copies, waits for them, and re-layouts  3.92 us (3%)
    pallas_call x11, Pallas kernels, kernel(): pl.pallas_call(run, out_shape=outs, in_specs=[VMEM] * len(after) + [SMEM]...  27.4 us
    ppermute x1, starting transfers between devices, over_bands(): came = lax.ppermute(send, 'band', [(i, i ^ 8) for i in range(bands)])  23.1 us
    ppermute x7, starting transfers between devices, along(): return lax.ppermute(block, 'segment', route)  22.9 us
    ppermute x3, waiting for transfers between devices, on_x(): lax.ppermute(piece, 'band', [(i, i & 8 | ((i >> 1 & 3) + step) % 4 << 1 |...  12.7 us
    ppermute x7, waiting for transfers between devices, along(): return lax.ppermute(block, 'segment', route)  12.4 us
    ppermute x3, starting transfers between devices, swap(): lax.ppermute(inner, 'band', [(i, i ^ 1) for i in range(bands)])  8.98 us
    ppermute x3, starting transfers between devices, swap(): lax.ppermute(outer, 'band', [(i, i + 1 if i % 2 else i - 1) for i in rang...  5.89 us
    ppermute x3, starting transfers between devices, on_x(): lax.ppermute(piece, 'band', [(i, i & 8 | ((i >> 1 & 3) + step) % 4 << 1 |...  5.31 us
  transfers between devices with their start and end apart: 18, of which 6 were waited for; matrix products, arithmetic and copies ran while one was open for 0% of the time, Pallas kernels for 18%

profile of v5, /device:TPU:18, one launch (start us, length us, event | category | flops | bytes accessed | tf_op | source)
XLA Modules:
  0.0 134.0 jit_solution(16805264776787458768)
XLA Ops:
  0.7 2.5 %pack_edges.1 = (bf16[576,256]{1,0:T(8,128)(2,1)}, bf16[576,256]{1,0:T(8,128)(2,1)}, bf16[448,256]{1,0:T(8,128)(2,1)}, bf16[448,256]{1,0:T(8,128)(2,1)}) custom-call(s32[4]{0:T(128)S(1)} %pad_add_fusion.at_ref.refs_0_.refs_1_, bf16[2,512,256]{2,1,0:T(8,128)(2,1)} %bitcast.24, bf16[2,512,256]{2,1,0:T(8,128)(2,1)} %bitcast.30, bf16[2,512,256]{2,1,0:T(8,128)(2,1)} %bitcast.25, ...), custom_call_target="tpu_custom_call" | custom-call | flops 1000 | bytes 1000 | tf_op jit(solution)/shard_map/pack_edges/pallas_call | solution.py:394
  3.2 1.9 %collective-permute-start.8 = (bf16[576,256]{1,0:T(8,128)(2,1)}, bf16[576,256]{1,0:T(8,128)(2,1)S(1)}, u32[]{:S(2)}, u32[]{:S(2)}) collective-permute-start(bf16[576,256]{1,0:T(8,128)(2,1)} %get-tuple-element.56), channel_id=1, source_target_pairs={{1,2},{2,1},{3,4},{4,3},{5,6},{6,5},{7,8},{8,7},{9,10},{10,9},{11,... | collective-permute-start | bytes 884744 | tf_op jit(solution)/shard_map/ppermute | solution.py:362
  6.8 2.1 %collective-permute-start.6 = (bf16[448,256]{1,0:T(8,128)(2,1)}, bf16[448,256]{1,0:T(8,128)(2,1)S(1)}, u32[]{:S(2)}, u32[]{:S(2)}) collective-permute-start(bf16[448,256]{1,0:T(8,128)(2,1)} %get-tuple-element.54), channel_id=1, source_target_pairs={{1,2},{2,1},{3,4},{4,3},{5,6},{6,5},{7,8},{8,7},{9,10},{10,9},{11,... | collective-permute-start | bytes 688136 | tf_op jit(solution)/shard_map/ppermute | solution.py:362
  11.4 4.1 %invert.1 = (bf16[640,256]{1,0:T(8,128)(2,1)S(1)}, bf16[640,256]{1,0:T(8,128)(2,1)S(1)}, bf16[768,256]{1,0:T(8,128)(2,1)S(1)}, bf16[640,256]{1,0:T(8,128)(2,1)S(1)}, bf16[640,256]{1,0:T(8,128)(2,1)S(1)}) custom-call(s32[4]{0:T(128)S(1)} %pad_add_fusion.at_ref.refs_0_.refs_1_, bf16[576,256]{1,0:T(8,128)(2,1)S(1)} %collective-permute-done.8.refs_1_.refs_5_.refs_2_, ...), custom_call_target="tpu_custom_call" | custom-call | flops 1000 | bytes 1000 | tf_op jit(solution)/shard_map/invert/pallas_call | solution.py:83
  15.6 8.1 %collective-permute-start.12 = (bf16[768,256]{1,0:T(8,128)(2,1)S(1)}, bf16[768,256]{1,0:T(8,128)(2,1)S(1)}, u32[]{:S(2)}, u32[]{:S(2)}) collective-permute-start(bf16[768,256]{1,0:T(8,128)(2,1)S(1)} %get-tuple-element.67), channel_id=1, source_target_pairs={{16,0},{32,16},{48,32},{64,48},{80,64},{96,80},{112,96},{128,112},... | collective-permute-start | bytes 1179656 | tf_op jit(solution)/shard_map/ppermute | solution.py:370
  23.7 4.8 %advance.2 = (bf16[2,512,256]{2,1,0:T(8,128)(2,1)S(1)}, bf16[768,256]{1,0:T(8,128)(2,1)S(1)}, bf16[640,256]{1,0:T(8,128)(2,1)S(1)}, bf16[640,256]{1,0:T(8,128)(2...) custom-call(s32[4]{0:T(128)S(1)} %pad_add_fusion.at_ref.refs_0_.refs_1_, ...), custom_call_target="tpu_custom_call" | custom-call | flops 1000 | bytes 1000 | tf_op jit(solution)/shard_map/advance/pallas_call | solution.py:83
  30.2 5.4 %collective-permute-start.15 = (bf16[640,256]{1,0:T(8,128)(2,1)S(1)}, bf16[640,256]{1,0:T(8,128)(2,1)S(1)}, u32[]{:S(2)}, u32[]{:S(2)}) collective-permute-start(bf16[640,256]{1,0:T(8,128)(2,1)S(1)} %get-tuple-element.71), channel_id=1, source_target_pairs={{16,0},{32,16},{48,32},{64,48},{80,64},{96,80},{112,96},{128,112},... | collective-permute-start | bytes 983048 | tf_op jit(solution)/shard_map/ppermute | solution.py:370
  35.6 4.7 %collective-permute-start.16 = (bf16[640,256]{1,0:T(8,128)(2,1)S(1)}, bf16[640,256]{1,0:T(8,128)(2,1)S(1)}, u32[]{:S(2)}, u32[]{:S(2)}) collective-permute-start(bf16[640,256]{1,0:T(8,128)(2,1)S(1)} %get-tuple-element.72), channel_id=1, source_target_pairs={{16,0},{32,16},{48,32},{64,48},{80,64},{96,80},{112,96},{128,112},... | collective-permute-start | bytes 983048 | tf_op jit(solution)/shard_map/ppermute | solution.py:370
  41.0 1.9 %collective-permute-start.13 = (bf16[384,256]{1,0:T(8,128)(2,1)S(1)}, bf16[384,256]{1,0:T(8,128)(2,1)S(1)}, u32[]{:S(2)}, u32[]{:S(2)}) collective-permute-start(bf16[384,256]{1,0:T(8,128)(2,1)S(1)} %get-tuple-element.69), channel_id=1, source_target_pairs={{1,2},{2,1},{3,4},{4,3},{5,6},{6,5},{7,8},{8,7},{9,10},{10,9},{11,... | collective-permute-start | bytes 589832 | tf_op jit(solution)/shard_map/ppermute | solution.py:362
  43.0 6.1 %collective-permute-start.14 = (bf16[384,256]{1,0:T(8,128)(2,1)S(1)}, bf16[384,256]{1,0:T(8,128)(2,1)S(1)}, u32[]{:S(2)}, u32[]{:S(2)}) collective-permute-start(bf16[384,256]{1,0:T(8,128)(2,1)S(1)} %get-tuple-element.70), channel_id=1, source_target_pairs={{0,1},{1,0},{2,3},{3,2},{4,5},{5,4},{6,7},{7,6},{8,9},{9,8},{10,11... | collective-permute-start | bytes 589832 | tf_op jit(solution)/shard_map/ppermute | solution.py:361
  49.0 2.1 %weight_terms.1 = (bf16[2,2304,256]{2,1,0:T(8,128)(2,1)S(1)}, f32[8,128]{1,0:T(8,128)S(1)}) custom-call(f32[8,128]{1,0:T(8,128)S(1)} %get-tuple-element.60.refs_0_, s32[4]{0:T(128)S(1)} %pad_add_fusion.at_ref.refs_0_.refs_1_, bf16[576,256]{1,0:T(8,128)(2,1)S(1)} %collective-permute-done.8.refs_1_.refs_5_.refs_2_, ...), custom_call_target="tpu_custom_call" | custom-call | flops 1000 | bytes 1000 | tf_op jit(solution)/shard_map/weight_terms/pallas_call | solution.py:83
  52.6 12.4 %collective-permute-done.10.refs_2_ = bf16[768,256]{1,0:T(8,128)(2,1)S(1)} collective-permute-done((bf16[768,256]{1,0:T(8,128)(2,1)S(1)}, bf16[768,256]{1,0:T(8,128)(2,1)S(1)}, u32[]{:S(2)}, u32[]{:S(2)}) %collective-permute-start.10) | collective-permute-done | bytes 393248 | tf_op jit(solution)/shard_map/ppermute | solution.py:370
  65.0 4.4 %advance.3 = (bf16[2,512,256]{2,1,0:T(8,128)(2,1)S(1)}, bf16[2,512,256]{2,1,0:T(8,128)(2,1)}, f32[8,128]{1,0:T(8,128)S(1)}) custom-call(f32[8,128]{1,0:T(8,128)S(1)} %get-tuple-element.63.refs_0_, s32[4]{0:T(128)S(1)} %pad_add_fusion.at_ref.refs_0_.refs_1_, bf16[768,256]{1,0:T(8,128)(2,1)S(1)} %collective-permute-done.10.refs_2_, ...), custom_call_target="tpu_custom_call" | custom-call | flops 1000 | bytes 1000 | tf_op jit(solution)/shard_map/advance/pallas_call | solution.py:83
  70.6 5.2 %invert_last.1 = (bf16[4,512,256]{2,1,0:T(8,128)(2,1)}, bf16[4,640,256]{2,1,0:T(8,128)(2,1)S(1)}) custom-call(s32[4]{0:T(128)S(1)} %pad_add_fusion.at_ref.refs_0_.refs_1_, bf16[384,256]{1,0:T(8,128)(2,1)S(1)} %collective-permute-done.13.refs_1_, bf16[384,256]{1,0:T(8,128)(2,1)S(1)} %collective-permute-done.14.refs_2_, ...), custom_call_target="tpu_custom_call" | custom-call | flops 1000 | bytes 1000 | tf_op jit(solution)/shard_map/invert_last/pallas_call | solution.py:83
  75.8 2.7 %collective-permute-start.17 = (bf16[4,512,256]{2,1,0:T(8,128)(2,1)}, bf16[4,512,256]{2,1,0:T(8,128)(2,1)S(1)}, u32[]{:S(2)}, u32[]{:S(2)}) collective-permute-start(bf16[4,512,256]{2,1,0:T(8,128)(2,1)} %get-tuple-element.79), channel_id=1, source_target_pairs={{0,240},{16,0},{32,16},{48,32},{64,48},{80,64},{96,80},{112,96},{1... | collective-permute-start | bytes 3145736 | tf_op jit(solution)/shard_map/ppermute | solution.py:370
  80.2 2.3 %weight_sums.1 = (f32[2,8,144,256]{3,2,1,0:T(8,128)S(1)}, bf16[2,8,144,256]{3,2,1,0:T(8,128)(2,1)S(1)}) custom-call(s32[4]{0:T(128)S(1)} %pad_add_fusion.at_ref.refs_0_.refs_1_, bf16[4,640,256]{2,1,0:T(8,128)(2,1)S(1)} %get-tuple-element.74.refs_1_, bf16[2,2304,256]{2,1,0:T(8,128)(2,1)S(1)} %copy-done.7), custom_call_target="tpu_custom_call" | custom-call | flops 1000 | bytes 1000 | tf_op jit(solution)/shard_map/weight_sums/pallas_call | solution.py:83
  82.5 49.6 %conditional.1 = (f32[2,144,256]{2,1,0:T(8,128)S(1)}, bf16[2,512,256]{2,1,0:T(8,128)(2,1)}) conditional(s32[]{:T(128)} %convert_element_type.6, bf16[2,512,256]{2,1,0:T(8,128)(2,1)} %get-tuple-element.66, (bf16[2,8,144,256]{3,2,1,0:T(8,128)(2,1)S(1)}, s32[4]{0:T(128)S(1)}, f32[2,8,144,256]{3,2,1,0:T(8,128)S(1)}, bf16[2,512,256]{2,1,0:T(8,128)(2,1)}) %tuple.16), branch_computations={%region_0.0_spmd, %region_1.0_spmd} | conditional | flops 150456 | bytes 13782228 | solution.py:515
  83.0 2.5 %collective-permute-done.refs_2_ = bf16[2,8,144,256]{3,2,1,0:T(8,128)(2,1)S(1)} collective-permute-done((bf16[2,8,144,256]{3,2,1,0:T(8,128)(2,1)S(1)}, bf16[2,8,144,256]{3,2,1,0:T(8,128)(2,1)S(1)}, u32[]{:S(2)}, u32[]{:S(2)}) %collective-permute-start) | collective-permute-done | bytes 1179680 | tf_op jit(solution)/shard_map/cond/branch_1_fun/ppermute | solution.py:499
  86.3 3.3 %collective-permute-start.1 = (bf16[2,2,144,256]{3,2,1,0:T(8,128)(2,1)S(1)}, bf16[2,2,144,256]{3,2,1,0:T(8,128)(2,1)S(1)}, u32[]{:S(2)}, u32[]{:S(2)}) collective-permute-start(bf16[2,2,144,256]{3,2,1,0:T(8,128)(2,1)S(1)} %get-tuple-element.13), channel_id=1, source_target_pairs={{0,4},{1,5},{2,6},{3,7},{4,0},{5,1},{6,2},{7,3},{8,12},{9,13},{10,... | collective-permute-start | bytes 884744 | tf_op jit(solution)/shard_map/cond/branch_1_fun/ppermute | solution.py:493
  89.6 2.0 %collective-permute-start.3 = (bf16[2,2,144,256]{3,2,1,0:T(8,128)(2,1)S(1)}, bf16[2,2,144,256]{3,2,1,0:T(8,128)(2,1)S(1)}, u32[]{:S(2)}, u32[]{:S(2)}) collective-permute-start(bf16[2,2,144,256]{3,2,1,0:T(8,128)(2,1)S(1)} %get-tuple-element.15), channel_id=1, source_target_pairs={{0,6},{1,7},{2,0},{3,1},{4,2},{5,3},{6,4},{7,5},{8,14},{9,15},{10,... | collective-permute-start | bytes 884744 | tf_op jit(solution)/shard_map/cond/branch_1_fun/ppermute | solution.py:493
  91.6 6.2 %collective-permute-done.1.refs_2_ = bf16[2,2,144,256]{3,2,1,0:T(8,128)(2,1)S(1)} collective-permute-done((bf16[2,2,144,256]{3,2,1,0:T(8,128)(2,1)S(1)}, bf16[2,2,144,256]{3,2,1,0:T(8,128)(2,1)S(1)}, u32[]{:S(2)}, u32[]{:S(2)}) %collective-permute-start.1) | collective-permute-done | bytes 294944 | tf_op jit(solution)/shard_map/cond/branch_1_fun/ppermute | solution.py:493
  97.7 6.6 %collective-permute-done.2.refs_3_ = bf16[2,2,144,256]{3,2,1,0:T(8,128)(2,1)S(1)} collective-permute-done((bf16[2,2,144,256]{3,2,1,0:T(8,128)(2,1)S(1)}, bf16[2,2,144,256]{3,2,1,0:T(8,128)(2,1)S(1)}, u32[]{:S(2)}, u32[]{:S(2)}) %collective-permute-start.2) | collective-permute-done | bytes 294944 | tf_op jit(solution)/shard_map/cond/branch_1_fun/ppermute | solution.py:493
  105.0 23.1 %collective-permute-start.4 = (bf16[2,144,256]{2,1,0:T(8,128)(2,1)S(1)}, bf16[2,144,256]{2,1,0:T(8,128)(2,1)S(1)}, u32[]{:S(2)}, u32[]{:S(2)}) collective-permute-start(bf16[2,144,256]{2,1,0:T(8,128)(2,1)S(1)} %get-tuple-element.17), channel_id=1, source_target_pairs={{0,8},{1,9},{2,10},{3,11},{4,12},{5,13},{6,14},{7,15},{8,0},{9,1},... | collective-permute-start | bytes 442376 | tf_op jit(solution)/shard_map/cond/branch_1_fun/ppermute | solution.py:508
  128.9 1.8 %place_forward.1 = bf16[2,512,256]{2,1,0:T(8,128)(2,1)} custom-call(bf16[2,512,256]{2,1,0:T(8,128)(2,1)} %copy-done.10), custom_call_target="tpu_custom_call" | custom-call | flops 1000 | bytes 1000 | tf_op jit(solution)/shard_map/cond/branch_1_fun/place_forward/pallas_call | solution.py:509
  (52 shorter events, 16.7 us)
Async XLA Ops:
  0.7 9.4 %copy-start = (bf16[1,2,2304,256]{3,2,1,0:T(8,128)(2,1)S(1)}, bf16[1,2,2304,256]{3,2,1,0:T(8,128)(2,1)}, u32[]{:S(2)}) copy-start(bf16[1,2,2304,256]{3,2,1,0:T(8,128)(2,1)} %param.11) | copy-start | bytes 7077892
  3.2 8.2 %collective-permute-start.8 = (bf16[576,256]{1,0:T(8,128)(2,1)}, bf16[576,256]{1,0:T(8,128)(2,1)S(1)}, u32[]{:S(2)}, u32[]{:S(2)}) collective-permute-start(bf16[576,256]{1,0:T(8,128)(2,1)} %get-tuple-element.56), channel_id=1, source_target_pairs={{1,2},{2,1},{3,4},{4,3},{5,6},{6,5},{7,8},{8,7},{9,10},{10,9},{11,... | collective-permute-start | bytes 884744 | tf_op jit(solution)/shard_map/ppermute | solution.py:362
  5.1 6.3 %collective-permute-start.9 = (bf16[576,256]{1,0:T(8,128)(2,1)}, bf16[576,256]{1,0:T(8,128)(2,1)S(1)}, u32[]{:S(2)}, u32[]{:S(2)}) collective-permute-start(bf16[576,256]{1,0:T(8,128)(2,1)} %get-tuple-element.57), channel_id=1, source_target_pairs={{0,1},{1,0},{2,3},{3,2},{4,5},{5,4},{6,7},{7,6},{8,9},{9,8},{10,11... | collective-permute-start | bytes 884744 | tf_op jit(solution)/shard_map/ppermute | solution.py:361
  6.8 16.9 %collective-permute-start.6 = (bf16[448,256]{1,0:T(8,128)(2,1)}, bf16[448,256]{1,0:T(8,128)(2,1)S(1)}, u32[]{:S(2)}, u32[]{:S(2)}) collective-permute-start(bf16[448,256]{1,0:T(8,128)(2,1)} %get-tuple-element.54), channel_id=1, source_target_pairs={{1,2},{2,1},{3,4},{4,3},{5,6},{6,5},{7,8},{8,7},{9,10},{10,9},{11,... | collective-permute-start | bytes 688136 | tf_op jit(solution)/shard_map/ppermute | solution.py:362
  8.8 14.8 %collective-permute-start.7 = (bf16[448,256]{1,0:T(8,128)(2,1)}, bf16[448,256]{1,0:T(8,128)(2,1)S(1)}, u32[]{:S(2)}, u32[]{:S(2)}) collective-permute-start(bf16[448,256]{1,0:T(8,128)(2,1)} %get-tuple-element.55), channel_id=1, source_target_pairs={{0,1},{1,0},{2,3},{3,2},{4,5},{5,4},{6,7},{7,6},{8,9},{9,8},{10,11... | collective-permute-start | bytes 688136 | tf_op jit(solution)/shard_map/ppermute | solution.py:361
  11.3 12.4 %copy-start.1 = (bf16[2,2,8,64,256]{4,3,2,1,0:T(8,128)(2,1)S(1)}, bf16[2,2,8,64,256]{4,3,2,1,0:T(8,128)(2,1)}, u32[]{:S(2)}) copy-start(bf16[2,2,8,64,256]{4,3,2,1,0:T(8,128)(2,1)} %param.12) | copy-start | bytes 3145732
  11.3 12.4 %copy-start.4 = (bf16[1,2,8,64,256]{4,3,2,1,0:T(8,128)(2,1)S(1)}, bf16[1,2,8,64,256]{4,3,2,1,0:T(8,128)(2,1)}, u32[]{:S(2)}) copy-start(bf16[1,2,8,64,256]{4,3,2,1,0:T(8,128)(2,1)} %param.8) | copy-start | bytes 1572868
  15.6 24.8 %collective-permute-start.12 = (bf16[768,256]{1,0:T(8,128)(2,1)S(1)}, bf16[768,256]{1,0:T(8,128)(2,1)S(1)}, u32[]{:S(2)}, u32[]{:S(2)}) collective-permute-start(bf16[768,256]{1,0:T(8,128)(2,1)S(1)} %get-tuple-element.67), channel_id=1, source_target_pairs={{16,0},{32,16},{48,32},{64,48},{80,64},{96,80},{112,96},{128,112},... | collective-permute-start | bytes 1179656 | tf_op jit(solution)/shard_map/ppermute | solution.py:370
  23.7 16.7 %copy-start.5 = (bf16[2,2,8,64,256]{4,3,2,1,0:T(8,128)(2,1)S(1)}, bf16[2,2,8,64,256]{4,3,2,1,0:T(8,128)(2,1)}, u32[]{:S(2)}) copy-start(bf16[2,2,8,64,256]{4,3,2,1,0:T(8,128)(2,1)} %param.13) | copy-start | bytes 3145732
  28.5 14.4 %collective-permute-start.11 = (bf16[640,256]{1,0:T(8,128)(2,1)S(1)}, bf16[640,256]{1,0:T(8,128)(2,1)S(1)}, u32[]{:S(2)}, u32[]{:S(2)}) collective-permute-start(bf16[640,256]{1,0:T(8,128)(2,1)S(1)} %get-tuple-element.65), channel_id=1, source_target_pairs={{0,16},{16,32},{32,48},{48,64},{64,80},{80,96},{96,112},{112,128},... | collective-permute-start | bytes 983048 | tf_op jit(solution)/shard_map/ppermute | solution.py:370
  28.6 36.3 %collective-permute-start.10 = (bf16[768,256]{1,0:T(8,128)(2,1)S(1)}, bf16[768,256]{1,0:T(8,128)(2,1)S(1)}, u32[]{:S(2)}, u32[]{:S(2)}) collective-permute-start(bf16[768,256]{1,0:T(8,128)(2,1)S(1)} %get-tuple-element.64), channel_id=1, source_target_pairs={{0,16},{16,32},{32,48},{48,64},{64,80},{80,96},{96,112},{112,128},... | collective-permute-start | bytes 1179656 | tf_op jit(solution)/shard_map/ppermute | solution.py:370
  30.2 40.4 %collective-permute-start.15 = (bf16[640,256]{1,0:T(8,128)(2,1)S(1)}, bf16[640,256]{1,0:T(8,128)(2,1)S(1)}, u32[]{:S(2)}, u32[]{:S(2)}) collective-permute-start(bf16[640,256]{1,0:T(8,128)(2,1)S(1)} %get-tuple-element.71), channel_id=1, source_target_pairs={{16,0},{32,16},{48,32},{64,48},{80,64},{96,80},{112,96},{128,112},... | collective-permute-start | bytes 983048 | tf_op jit(solution)/shard_map/ppermute | solution.py:370
  35.6 34.9 %collective-permute-start.16 = (bf16[640,256]{1,0:T(8,128)(2,1)S(1)}, bf16[640,256]{1,0:T(8,128)(2,1)S(1)}, u32[]{:S(2)}, u32[]{:S(2)}) collective-permute-start(bf16[640,256]{1,0:T(8,128)(2,1)S(1)} %get-tuple-element.72), channel_id=1, source_target_pairs={{16,0},{32,16},{48,32},{64,48},{80,64},{96,80},{112,96},{128,112},... | collective-permute-start | bytes 983048 | tf_op jit(solution)/shard_map/ppermute | solution.py:370
  41.0 29.5 %collective-permute-start.13 = (bf16[384,256]{1,0:T(8,128)(2,1)S(1)}, bf16[384,256]{1,0:T(8,128)(2,1)S(1)}, u32[]{:S(2)}, u32[]{:S(2)}) collective-permute-start(bf16[384,256]{1,0:T(8,128)(2,1)S(1)} %get-tuple-element.69), channel_id=1, source_target_pairs={{1,2},{2,1},{3,4},{4,3},{5,6},{6,5},{7,8},{8,7},{9,10},{10,9},{11,... | collective-permute-start | bytes 589832 | tf_op jit(solution)/shard_map/ppermute | solution.py:362
  43.0 27.6 %collective-permute-start.14 = (bf16[384,256]{1,0:T(8,128)(2,1)S(1)}, bf16[384,256]{1,0:T(8,128)(2,1)S(1)}, u32[]{:S(2)}, u32[]{:S(2)}) collective-permute-start(bf16[384,256]{1,0:T(8,128)(2,1)S(1)} %get-tuple-element.70), channel_id=1, source_target_pairs={{0,1},{1,0},{2,3},{3,2},{4,5},{5,4},{6,7},{7,6},{8,9},{9,8},{10,11... | collective-permute-start | bytes 589832 | tf_op jit(solution)/shard_map/ppermute | solution.py:361
  75.8 56.3 %collective-permute-start.17 = (bf16[4,512,256]{2,1,0:T(8,128)(2,1)}, bf16[4,512,256]{2,1,0:T(8,128)(2,1)S(1)}, u32[]{:S(2)}, u32[]{:S(2)}) collective-permute-start(bf16[4,512,256]{2,1,0:T(8,128)(2,1)} %get-tuple-element.79), channel_id=1, source_target_pairs={{0,240},{16,0},{32,16},{48,32},{64,48},{80,64},{96,80},{112,96},{1... | collective-permute-start | bytes 3145736 | tf_op jit(solution)/shard_map/ppermute | solution.py:370
  78.5 1.7 %copy-start.7 = (bf16[2,2304,256]{2,1,0:T(8,128)(2,1)S(1)}, bf16[2,2304,256]{2,1,0:T(8,128)(2,1)}, u32[]{:S(2)}) copy-start(bf16[2,2304,256]{2,1,0:T(8,128)(2,1)} %copy-done.6) | copy-start | bytes 7077892
  82.5 49.6 %copy-start.9 = (bf16[2,512,256]{2,1,0:T(8,128)(2,1)S(1)}, bf16[2,512,256]{2,1,0:T(8,128)(2,1)}, u32[]{:S(2)}) copy-start(bf16[2,512,256]{2,1,0:T(8,128)(2,1)} %copy-done.8) | copy-start | bytes 1572868
  82.5 2.9 %collective-permute-start = (bf16[2,8,144,256]{3,2,1,0:T(8,128)(2,1)S(1)}, bf16[2,8,144,256]{3,2,1,0:T(8,128)(2,1)S(1)}, u32[]{:S(2)}, u32[]{:S(2)}) collective-permute-start(bf16[2,8,144,256]{3,2,1,0:T(8,128)(2,1)S(1)} %get-tuple-element.11), channel_id=1, source_target_pairs={{0,1},{1,0},{2,3},{3,2},{4,5},{5,4},{6,7},{7,6},{8,9},{9,8},{10,11... | collective-permute-start | bytes 3538952 | tf_op jit(solution)/shard_map/cond/branch_1_fun/ppermute | solution.py:499
  82.6 45.4 %collective-permute-start.5 = (bf16[2,512,256]{2,1,0:T(8,128)(2,1)}, bf16[2,512,256]{2,1,0:T(8,128)(2,1)S(1)}, u32[]{:S(2)}, u32[]{:S(2)}) collective-permute-start(bf16[2,512,256]{2,1,0:T(8,128)(2,1)} %get-tuple-element.18), channel_id=1, source_target_pairs={{0,16},{16,32},{32,48},{48,64},{64,80},{80,96},{96,112},{112,128},... | collective-permute-start | bytes 1572872 | tf_op jit(solution)/shard_map/cond/branch_1_fun/ppermute | solution.py:370
  86.3 11.5 %collective-permute-start.1 = (bf16[2,2,144,256]{3,2,1,0:T(8,128)(2,1)S(1)}, bf16[2,2,144,256]{3,2,1,0:T(8,128)(2,1)S(1)}, u32[]{:S(2)}, u32[]{:S(2)}) collective-permute-start(bf16[2,2,144,256]{3,2,1,0:T(8,128)(2,1)S(1)} %get-tuple-element.13), channel_id=1, source_target_pairs={{0,4},{1,5},{2,6},{3,7},{4,0},{5,1},{6,2},{7,3},{8,12},{9,13},{10,... | collective-permute-start | bytes 884744 | tf_op jit(solution)/shard_map/cond/branch_1_fun/ppermute | solution.py:493
  89.6 14.8 %collective-permute-start.2 = (bf16[2,2,144,256]{3,2,1,0:T(8,128)(2,1)S(1)}, bf16[2,2,144,256]{3,2,1,0:T(8,128)(2,1)S(1)}, u32[]{:S(2)}, u32[]{:S(2)}) collective-permute-start(bf16[2,2,144,256]{3,2,1,0:T(8,128)(2,1)S(1)} %get-tuple-element.14), channel_id=1, source_target_pairs={{0,2},{1,3},{2,4},{3,5},{4,6},{5,7},{6,0},{7,1},{8,10},{9,11},{10,... | collective-permute-start | bytes 884744 | tf_op jit(solution)/shard_map/cond/branch_1_fun/ppermute | solution.py:493
  89.6 14.7 %collective-permute-start.3 = (bf16[2,2,144,256]{3,2,1,0:T(8,128)(2,1)S(1)}, bf16[2,2,144,256]{3,2,1,0:T(8,128)(2,1)S(1)}, u32[]{:S(2)}, u32[]{:S(2)}) collective-permute-start(bf16[2,2,144,256]{3,2,1,0:T(8,128)(2,1)S(1)} %get-tuple-element.15), channel_id=1, source_target_pairs={{0,6},{1,7},{2,0},{3,1},{4,2},{5,3},{6,4},{7,5},{8,14},{9,15},{10,... | collective-permute-start | bytes 884744 | tf_op jit(solution)/shard_map/cond/branch_1_fun/ppermute | solution.py:493
  105.0 27.1 %collective-permute-start.4 = (bf16[2,144,256]{2,1,0:T(8,128)(2,1)S(1)}, bf16[2,144,256]{2,1,0:T(8,128)(2,1)S(1)}, u32[]{:S(2)}, u32[]{:S(2)}) collective-permute-start(bf16[2,144,256]{2,1,0:T(8,128)(2,1)S(1)} %get-tuple-element.17), channel_id=1, source_target_pairs={{0,8},{1,9},{2,10},{3,11},{4,12},{5,13},{6,14},{7,15},{8,0},{9,1},... | collective-permute-start | bytes 442376 | tf_op jit(solution)/shard_map/cond/branch_1_fun/ppermute | solution.py:508
  (5 other events, 6.1 us)

commit v6 on v5

--- a/solution.py
+++ b/solution.py
@@ -166,6 +166,14 @@
         for _ in range(2):
             sides.append(jnp.concatenate([refs.pop(0)[0] for _ in range(count)], 0))
         by_band(at_ref, *sides, *outs[2 * k : 2 * k + 2])
+
+
+def hold(back_ref, ready_ref, out_ref):
+    pass
+
+
+def signal(at_ref, args, outs, own):
+    outs[0][...] = jnp.zeros_like(outs[0])
 
 
 def pick(at_ref, args, outs, own):
@@ -474,12 +482,22 @@
         functools.partial(advance, cols, 0), at, (q, p, w_f, w_g, (fresh, 3), (fresh, 2)),
         (pair, pair), [x_scratch(2)], (token,), True,
     )
-    (w_t,) = kernel(flip, at, (w,), (shape(2, 9 * ch, ch),), after=(token,))
+    w_t, token = kernel(flip, at, (w,), (shape(2, 9 * ch, ch),), after=(token,), token=True)
     back, fields = kernel(
         functools.partial(invert_last, cols), at,
         (*[came_field(k) for k in range(4)], w_f, w_g, (w_t, 0), (w_t, 1), (loss, 1)),
         (shape(4, size, ch), shape(4, size + edge, ch)), [x_scratch(2)],
     )
+    (ready,) = kernel(signal, at, (), (shape(16, 128),), after=(*came_mids, token))
+    ahead_on_z = [
+        (16 * s + b, 16 * s + b + 8 if b < 8 else 16 * (s // 4 * 4 + (s + 1) % 4) + b - 8)
+        for s in range(segments) for b in range(bands)
+    ]
+    ready = lax.ppermute(ready, ("segment", "band"), ahead_on_z)
+    back = pl.pallas_call(
+        hold, out_shape=shape(4, size, ch), in_specs=[ANY, VMEM], out_specs=ANY, input_output_aliases={0: 0},
+        cost_estimate=LITTLE, name="hold",
+    )(back, ready)
     came_back = along(back, back_ring)
     part = 9 * ch // bands
     chunks = (2, 8, part, ch)

time: 134 us -> 134 us (level)
  starting transfers between devices: 66.3 us -> 44 us
  waiting for transfers between devices: 29.2 us -> 47.6 us
  local copies, waits for them, and re-layouts: 3.92 us -> 6.29 us
    ppermute x1, starting transfers between devices: 23.1 us -> 0.12 us  [over_bands(): came = lax.ppermute(send, 'band', [(i, i ^ 8) for i in range(bands)])]
    ppermute x1, waiting for transfers between devices: 1.38 us -> 13.6 us  [over_bands(): came = lax.ppermute(send, 'band', [(i, i ^ 8) for i in range(bands)])]
    ppermute x7, waiting for transfers between devices: 12.4 us -> 17.7 us  [along(): return lax.ppermute(block, 'segment', route)]
    unnamed x20 -> x24, local copies, waits for them, and re-layouts: 3.12 us -> 5.49 us
    pallas_call x11 -> x12, Pallas kernels: 27.4 us -> 27 us  [kernel(): pl.pallas_call(run, out_shape=outs, in_specs=[VMEM] * len(after) + [SMEM]...]
  transfers between devices with their start and end apart: 18 -> 19, of which waited for: 6 -> 7; matrix products, arithmetic and copies ran while one was open for 0% -> 0% of each run, Pallas kernels for 18% -> 22%
where the time goes in v6:
time: 134 us; the launch traced here: 133 us
  waiting for transfers between devices  47.6 us (36%)
  starting transfers between devices  44 us (33%)
  Pallas kernels  33.6 us (25%)
  local copies, waits for them, and re-layouts  6.29 us (5%)
    pallas_call x12, Pallas kernels, kernel(): pl.pallas_call(run, out_shape=outs, in_specs=[VMEM] * len(after) + [SMEM]...  27 us
    ppermute x7, starting transfers between devices, along(): return lax.ppermute(block, 'segment', route)  23.1 us
    ppermute x7, waiting for transfers between devices, along(): return lax.ppermute(block, 'segment', route)  17.7 us
    ppermute x1, waiting for transfers between devices, over_bands(): came = lax.ppermute(send, 'band', [(i, i ^ 8) for i in range(bands)])  13.6 us
    ppermute x3, waiting for transfers between devices, on_x(): lax.ppermute(piece, 'band', [(i, i & 8 | ((i >> 1 & 3) + step) % 4 << 1 |...  13.4 us
    ppermute x3, starting transfers between devices, swap(): lax.ppermute(inner, 'band', [(i, i ^ 1) for i in range(bands)])  8.99 us
    ppermute x3, starting transfers between devices, swap(): lax.ppermute(outer, 'band', [(i, i + 1 if i % 2 else i - 1) for i in rang...  5.89 us
    unnamed x24, local copies, waits for them, and re-layouts  5.49 us
  transfers between devices with their start and end apart: 19, of which 7 were waited for; matrix products, arithmetic and copies ran while one was open for 0% of the time, Pallas kernels for 22%

profile of v6, /device:TPU:18, one launch (start us, length us, event | category | flops | bytes accessed | tf_op | source)
XLA Modules:
  0.0 132.7 jit_solution(9948999241110115591)
XLA Ops:
  0.7 2.5 %pack_edges.1 = (bf16[576,256]{1,0:T(8,128)(2,1)}, bf16[576,256]{1,0:T(8,128)(2,1)}, bf16[448,256]{1,0:T(8,128)(2,1)}, bf16[448,256]{1,0:T(8,128)(2,1)}) custom-call(s32[4]{0:T(128)S(1)} %pad_add_fusion.at_ref.refs_0_.refs_1_.refs_3_, bf16[2,512,256]{2,1,0:T(8,128)(2,1)} %bitcast.24, bf16[2,512,256]{2,1,0:T(8,128)(2,1)} %bitcast.30, ...), custom_call_target="tpu_custom_call" | custom-call | flops 1000 | bytes 1000 | tf_op jit(solution)/shard_map/pack_edges/pallas_call | solution.py:402
  3.2 1.9 %collective-permute-start.8 = (bf16[576,256]{1,0:T(8,128)(2,1)}, bf16[576,256]{1,0:T(8,128)(2,1)S(1)}, u32[]{:S(2)}, u32[]{:S(2)}) collective-permute-start(bf16[576,256]{1,0:T(8,128)(2,1)} %get-tuple-element.58), channel_id=1, source_target_pairs={{1,2},{2,1},{3,4},{4,3},{5,6},{6,5},{7,8},{8,7},{9,10},{10,9},{11,... | collective-permute-start | bytes 884744 | tf_op jit(solution)/shard_map/ppermute | solution.py:370
  6.8 2.1 %collective-permute-start.6 = (bf16[448,256]{1,0:T(8,128)(2,1)}, bf16[448,256]{1,0:T(8,128)(2,1)S(1)}, u32[]{:S(2)}, u32[]{:S(2)}) collective-permute-start(bf16[448,256]{1,0:T(8,128)(2,1)} %get-tuple-element.56), channel_id=1, source_target_pairs={{1,2},{2,1},{3,4},{4,3},{5,6},{6,5},{7,8},{8,7},{9,10},{10,9},{11,... | collective-permute-start | bytes 688136 | tf_op jit(solution)/shard_map/ppermute | solution.py:370
  11.4 4.1 %invert.1 = (bf16[640,256]{1,0:T(8,128)(2,1)S(1)}, bf16[640,256]{1,0:T(8,128)(2,1)S(1)}, bf16[768,256]{1,0:T(8,128)(2,1)S(1)}, bf16[640,256]{1,0:T(8,128)(2,1)S(1)}, bf16[640,256]{1,0:T(8,128)(2,1)S(1)}) custom-call(s32[4]{0:T(128)S(1)} %pad_add_fusion.at_ref.refs_0_.refs_1_.refs_3_, bf16[576,256]{1,0:T(8,128)(2,1)S(1)} %collective-permute-done.8.refs_1_.refs_5_.refs_2_, ...), custom_call_target="tpu_custom_call" | custom-call | flops 1000 | bytes 1000 | tf_op jit(solution)/shard_map/invert/pallas_call | solution.py:83
  15.6 8.1 %collective-permute-start.12 = (bf16[768,256]{1,0:T(8,128)(2,1)S(1)}, bf16[768,256]{1,0:T(8,128)(2,1)S(1)}, u32[]{:S(2)}, u32[]{:S(2)}) collective-permute-start(bf16[768,256]{1,0:T(8,128)(2,1)S(1)} %get-tuple-element.69), channel_id=1, source_target_pairs={{16,0},{32,16},{48,32},{64,48},{80,64},{96,80},{112,96},{128,112},... | collective-permute-start | bytes 1179656 | tf_op jit(solution)/shard_map/ppermute | solution.py:378
  23.7 4.8 %advance.2 = (bf16[2,512,256]{2,1,0:T(8,128)(2,1)S(1)}, bf16[768,256]{1,0:T(8,128)(2,1)S(1)}, bf16[640,256]{1,0:T(8,128)(2,1)S(1)}, bf16[640,256]{1,0:T(8,128)(2...) custom-call(s32[4]{0:T(128)S(1)} %pad_add_fusion.at_ref.refs_0_.refs_1_.refs_3_, ...), custom_call_target="tpu_custom_call" | custom-call | flops 1000 | bytes 1000 | tf_op jit(solution)/shard_map/advance/pallas_call | solution.py:83
  30.2 5.4 %collective-permute-start.15 = (bf16[640,256]{1,0:T(8,128)(2,1)S(1)}, bf16[640,256]{1,0:T(8,128)(2,1)S(1)}, u32[]{:S(2)}, u32[]{:S(2)}) collective-permute-start(bf16[640,256]{1,0:T(8,128)(2,1)S(1)} %get-tuple-element.73), channel_id=1, source_target_pairs={{16,0},{32,16},{48,32},{64,48},{80,64},{96,80},{112,96},{128,112},... | collective-permute-start | bytes 983048 | tf_op jit(solution)/shard_map/ppermute | solution.py:378
  35.6 4.7 %collective-permute-start.16 = (bf16[640,256]{1,0:T(8,128)(2,1)S(1)}, bf16[640,256]{1,0:T(8,128)(2,1)S(1)}, u32[]{:S(2)}, u32[]{:S(2)}) collective-permute-start(bf16[640,256]{1,0:T(8,128)(2,1)S(1)} %get-tuple-element.74), channel_id=1, source_target_pairs={{16,0},{32,16},{48,32},{64,48},{80,64},{96,80},{112,96},{128,112},... | collective-permute-start | bytes 983048 | tf_op jit(solution)/shard_map/ppermute | solution.py:378
  41.0 1.9 %collective-permute-start.13 = (bf16[384,256]{1,0:T(8,128)(2,1)S(1)}, bf16[384,256]{1,0:T(8,128)(2,1)S(1)}, u32[]{:S(2)}, u32[]{:S(2)}) collective-permute-start(bf16[384,256]{1,0:T(8,128)(2,1)S(1)} %get-tuple-element.71), channel_id=1, source_target_pairs={{1,2},{2,1},{3,4},{4,3},{5,6},{6,5},{7,8},{8,7},{9,10},{10,9},{11,... | collective-permute-start | bytes 589832 | tf_op jit(solution)/shard_map/ppermute | solution.py:370
  43.0 6.1 %collective-permute-start.14 = (bf16[384,256]{1,0:T(8,128)(2,1)S(1)}, bf16[384,256]{1,0:T(8,128)(2,1)S(1)}, u32[]{:S(2)}, u32[]{:S(2)}) collective-permute-start(bf16[384,256]{1,0:T(8,128)(2,1)S(1)} %get-tuple-element.72), channel_id=1, source_target_pairs={{0,1},{1,0},{2,3},{3,2},{4,5},{5,4},{6,7},{7,6},{8,9},{9,8},{10,11... | collective-permute-start | bytes 589832 | tf_op jit(solution)/shard_map/ppermute | solution.py:369
  49.0 2.1 %weight_terms.1 = (bf16[2,2304,256]{2,1,0:T(8,128)(2,1)S(1)}, f32[8,128]{1,0:T(8,128)S(1)}) custom-call(f32[8,128]{1,0:T(8,128)S(1)} %get-tuple-element.62.refs_0_, s32[4]{0:T(128)S(1)} %pad_add_fusion.at_ref.refs_0_.refs_1_.refs_3_, bf16[576,256]{1,0:T(8,128)(2,1)S(1)} %collective-permute-done.8.refs_1_.refs_5_.refs_2_, ...), custom_call_target="tpu_custom_call" | custom-call | flops 1000 | bytes 1000 | tf_op jit(solution)/shard_map/weight_terms/pallas_call | solution.py:83
  52.6 12.4 %collective-permute-done.10.refs_2_ = bf16[768,256]{1,0:T(8,128)(2,1)S(1)} collective-permute-done((bf16[768,256]{1,0:T(8,128)(2,1)S(1)}, bf16[768,256]{1,0:T(8,128)(2,1)S(1)}, u32[]{:S(2)}, u32[]{:S(2)}) %collective-permute-start.10) | collective-permute-done | bytes 393248 | tf_op jit(solution)/shard_map/ppermute | solution.py:378
  64.9 4.4 %advance.3 = (bf16[2,512,256]{2,1,0:T(8,128)(2,1)S(1)}, bf16[2,512,256]{2,1,0:T(8,128)(2,1)}, f32[8,128]{1,0:T(8,128)S(1)}) custom-call(f32[8,128]{1,0:T(8,128)S(1)} %get-tuple-element.65.refs_0_, s32[4]{0:T(128)S(1)} %pad_add_fusion.at_ref.refs_0_.refs_1_.refs_3_, bf16[768,256]{1,0:T(8,128)(2,1)S(1)} %collective-permute-done.10.refs_2_, ...), custom_call_target="tpu_custom_call" | custom-call | flops 1000 | bytes 1000 | tf_op jit(solution)/shard_map/advance/pallas_call | solution.py:83
  72.4 4.2 %invert_last.1 = (bf16[4,512,256]{2,1,0:T(8,128)(2,1)S(1)}, bf16[4,640,256]{2,1,0:T(8,128)(2,1)S(1)}) custom-call(s32[4]{0:T(128)S(1)} %pad_add_fusion.at_ref.refs_0_.refs_1_.refs_3_, bf16[384,256]{1,0:T(8,128)(2,1)S(1)} %collective-permute-done.13.refs_1_, bf16[384,256]{1,0:T(8,128)(2,1)S(1)} %collective-permute-done.14.refs_2_, ...), custom_call_target="tpu_custom_call" | custom-call | flops 1000 | bytes 1000 | tf_op jit(solution)/shard_map/invert_last/pallas_call | solution.py:83
  78.9 3.1 %collective-permute-start.18 = (bf16[4,512,256]{2,1,0:T(8,128)(2,1)}, bf16[4,512,256]{2,1,0:T(8,128)(2,1)S(1)}, u32[]{:S(2)}, u32[]{:S(2)}) collective-permute-start(bf16[4,512,256]{2,1,0:T(8,128)(2,1)} %hold.1), channel_id=1, source_target_pairs={{0,240},{16,0},{32,16},{48,32},{64,48},{80,64},{96,80},{112,96},{1... | collective-permute-start | bytes 3145736 | tf_op jit(solution)/shard_map/ppermute | solution.py:378
  83.6 2.3 %weight_sums.1 = (f32[2,8,144,256]{3,2,1,0:T(8,128)S(1)}, bf16[2,8,144,256]{3,2,1,0:T(8,128)(2,1)S(1)}) custom-call(s32[4]{0:T(128)S(1)} %pad_add_fusion.at_ref.refs_0_.refs_1_.refs_3_, bf16[4,640,256]{2,1,0:T(8,128)(2,1)S(1)} %get-tuple-element.77.refs_1_, bf16[2,2304,256]{2,1,0:T(8,128)(2,1)S(1)} %copy-done.7), custom_call_target="tpu_custom_call" | custom-call | flops 1000 | bytes 1000 | tf_op jit(solution)/shard_map/weight_sums/pallas_call | solution.py:83
  86.0 44.9 %conditional.1 = (f32[2,144,256]{2,1,0:T(8,128)S(1)}, bf16[2,512,256]{2,1,0:T(8,128)(2,1)}) conditional(s32[]{:T(128)} %convert_element_type.6, bf16[2,512,256]{2,1,0:T(8,128)(2,1)} %get-tuple-element.68, (bf16[2,8,144,256]{3,2,1,0:T(8,128)(2,1)S(1)}, s32[4]{0:T(128)S(1)}, f32[2,8,144,256]{3,2,1,0:T(8,128)S(1)}, bf16[2,512,256]{2,1,0:T(8,128)(2,1)}) %tuple.16), branch_computations={%region_0.0_spmd, %region_1.0_spmd} | conditional | flops 150456 | bytes 13782228 | solution.py:533
  86.2 2.7 %collective-permute-done.refs_2_ = bf16[2,8,144,256]{3,2,1,0:T(8,128)(2,1)S(1)} collective-permute-done((bf16[2,8,144,256]{3,2,1,0:T(8,128)(2,1)S(1)}, bf16[2,8,144,256]{3,2,1,0:T(8,128)(2,1)S(1)}, u32[]{:S(2)}, u32[]{:S(2)}) %collective-permute-start) | collective-permute-done | bytes 1179680 | tf_op jit(solution)/shard_map/cond/branch_1_fun/ppermute | solution.py:517
  89.7 2.6 %collective-permute-start.1 = (bf16[2,2,144,256]{3,2,1,0:T(8,128)(2,1)S(1)}, bf16[2,2,144,256]{3,2,1,0:T(8,128)(2,1)S(1)}, u32[]{:S(2)}, u32[]{:S(2)}) collective-permute-start(bf16[2,2,144,256]{3,2,1,0:T(8,128)(2,1)S(1)} %get-tuple-element.13), channel_id=1, source_target_pairs={{0,4},{1,5},{2,6},{3,7},{4,0},{5,1},{6,2},{7,3},{8,12},{9,13},{10,... | collective-permute-start | bytes 884744 | tf_op jit(solution)/shard_map/cond/branch_1_fun/ppermute | solution.py:511
  93.1 2.0 %collective-permute-start.3 = (bf16[2,2,144,256]{3,2,1,0:T(8,128)(2,1)S(1)}, bf16[2,2,144,256]{3,2,1,0:T(8,128)(2,1)S(1)}, u32[]{:S(2)}, u32[]{:S(2)}) collective-permute-start(bf16[2,2,144,256]{3,2,1,0:T(8,128)(2,1)S(1)} %get-tuple-element.15), channel_id=1, source_target_pairs={{0,6},{1,7},{2,0},{3,1},{4,2},{5,3},{6,4},{7,5},{8,14},{9,15},{10,... | collective-permute-start | bytes 884744 | tf_op jit(solution)/shard_map/cond/branch_1_fun/ppermute | solution.py:511
  95.1 6.4 %collective-permute-done.1.refs_2_ = bf16[2,2,144,256]{3,2,1,0:T(8,128)(2,1)S(1)} collective-permute-done((bf16[2,2,144,256]{3,2,1,0:T(8,128)(2,1)S(1)}, bf16[2,2,144,256]{3,2,1,0:T(8,128)(2,1)S(1)}, u32[]{:S(2)}, u32[]{:S(2)}) %collective-permute-start.1) | collective-permute-done | bytes 294944 | tf_op jit(solution)/shard_map/cond/branch_1_fun/ppermute | solution.py:511
  101.4 7.0 %collective-permute-done.2.refs_3_ = bf16[2,2,144,256]{3,2,1,0:T(8,128)(2,1)S(1)} collective-permute-done((bf16[2,2,144,256]{3,2,1,0:T(8,128)(2,1)S(1)}, bf16[2,2,144,256]{3,2,1,0:T(8,128)(2,1)S(1)}, u32[]{:S(2)}, u32[]{:S(2)}) %collective-permute-start.2) | collective-permute-done | bytes 294944 | tf_op jit(solution)/shard_map/cond/branch_1_fun/ppermute | solution.py:511
  109.3 5.4 %collective-permute-done.5.ahead_ref = bf16[2,512,256]{2,1,0:T(8,128)(2,1)S(1)} collective-permute-done((bf16[2,512,256]{2,1,0:T(8,128)(2,1)}, bf16[2,512,256]{2,1,0:T(8,128)(2,1)S(1)}, u32[]{:S(2)}, u32[]{:S(2)}) %collective-permute-start.5) | collective-permute-done | bytes 524320 | tf_op jit(solution)/shard_map/cond/branch_1_fun/ppermute | solution.py:378
  117.3 13.6 %collective-permute-done.4 = bf16[2,144,256]{2,1,0:T(8,128)(2,1)S(1)} collective-permute-done((bf16[2,144,256]{2,1,0:T(8,128)(2,1)S(1)}, bf16[2,144,256]{2,1,0:T(8,128)(2,1)S(1)}, u32[]{:S(2)}, u32[]{:S(2)}) %collective-permute-start.4) | collective-permute-done | bytes 147488 | tf_op jit(solution)/shard_map/cond/branch_1_fun/ppermute | solution.py:526
  (60 shorter events, 21.8 us)
Async XLA Ops:
  0.7 9.4 %copy-start = (bf16[1,2,2304,256]{3,2,1,0:T(8,128)(2,1)S(1)}, bf16[1,2,2304,256]{3,2,1,0:T(8,128)(2,1)}, u32[]{:S(2)}) copy-start(bf16[1,2,2304,256]{3,2,1,0:T(8,128)(2,1)} %param.11) | copy-start | bytes 7077892
  3.2 8.2 %collective-permute-start.8 = (bf16[576,256]{1,0:T(8,128)(2,1)}, bf16[576,256]{1,0:T(8,128)(2,1)S(1)}, u32[]{:S(2)}, u32[]{:S(2)}) collective-permute-start(bf16[576,256]{1,0:T(8,128)(2,1)} %get-tuple-element.58), channel_id=1, source_target_pairs={{1,2},{2,1},{3,4},{4,3},{5,6},{6,5},{7,8},{8,7},{9,10},{10,9},{11,... | collective-permute-start | bytes 884744 | tf_op jit(solution)/shard_map/ppermute | solution.py:370
  5.1 6.3 %collective-permute-start.9 = (bf16[576,256]{1,0:T(8,128)(2,1)}, bf16[576,256]{1,0:T(8,128)(2,1)S(1)}, u32[]{:S(2)}, u32[]{:S(2)}) collective-permute-start(bf16[576,256]{1,0:T(8,128)(2,1)} %get-tuple-element.59), channel_id=1, source_target_pairs={{0,1},{1,0},{2,3},{3,2},{4,5},{5,4},{6,7},{7,6},{8,9},{9,8},{10,11... | collective-permute-start | bytes 884744 | tf_op jit(solution)/shard_map/ppermute | solution.py:369
  6.8 16.9 %collective-permute-start.6 = (bf16[448,256]{1,0:T(8,128)(2,1)}, bf16[448,256]{1,0:T(8,128)(2,1)S(1)}, u32[]{:S(2)}, u32[]{:S(2)}) collective-permute-start(bf16[448,256]{1,0:T(8,128)(2,1)} %get-tuple-element.56), channel_id=1, source_target_pairs={{1,2},{2,1},{3,4},{4,3},{5,6},{6,5},{7,8},{8,7},{9,10},{10,9},{11,... | collective-permute-start | bytes 688136 | tf_op jit(solution)/shard_map/ppermute | solution.py:370
  8.8 14.8 %collective-permute-start.7 = (bf16[448,256]{1,0:T(8,128)(2,1)}, bf16[448,256]{1,0:T(8,128)(2,1)S(1)}, u32[]{:S(2)}, u32[]{:S(2)}) collective-permute-start(bf16[448,256]{1,0:T(8,128)(2,1)} %get-tuple-element.57), channel_id=1, source_target_pairs={{0,1},{1,0},{2,3},{3,2},{4,5},{5,4},{6,7},{7,6},{8,9},{9,8},{10,11... | collective-permute-start | bytes 688136 | tf_op jit(solution)/shard_map/ppermute | solution.py:369
  11.3 12.4 %copy-start.1 = (bf16[2,2,8,64,256]{4,3,2,1,0:T(8,128)(2,1)S(1)}, bf16[2,2,8,64,256]{4,3,2,1,0:T(8,128)(2,1)}, u32[]{:S(2)}) copy-start(bf16[2,2,8,64,256]{4,3,2,1,0:T(8,128)(2,1)} %param.12) | copy-start | bytes 3145732
  11.3 12.4 %copy-start.4 = (bf16[1,2,8,64,256]{4,3,2,1,0:T(8,128)(2,1)S(1)}, bf16[1,2,8,64,256]{4,3,2,1,0:T(8,128)(2,1)}, u32[]{:S(2)}) copy-start(bf16[1,2,8,64,256]{4,3,2,1,0:T(8,128)(2,1)} %param.8) | copy-start | bytes 1572868
  15.6 24.8 %collective-permute-start.12 = (bf16[768,256]{1,0:T(8,128)(2,1)S(1)}, bf16[768,256]{1,0:T(8,128)(2,1)S(1)}, u32[]{:S(2)}, u32[]{:S(2)}) collective-permute-start(bf16[768,256]{1,0:T(8,128)(2,1)S(1)} %get-tuple-element.69), channel_id=1, source_target_pairs={{16,0},{32,16},{48,32},{64,48},{80,64},{96,80},{112,96},{128,112},... | collective-permute-start | bytes 1179656 | tf_op jit(solution)/shard_map/ppermute | solution.py:378
  23.7 16.7 %copy-start.5 = (bf16[2,2,8,64,256]{4,3,2,1,0:T(8,128)(2,1)S(1)}, bf16[2,2,8,64,256]{4,3,2,1,0:T(8,128)(2,1)}, u32[]{:S(2)}) copy-start(bf16[2,2,8,64,256]{4,3,2,1,0:T(8,128)(2,1)} %param.13) | copy-start | bytes 3145732
  28.5 14.4 %collective-permute-start.11 = (bf16[640,256]{1,0:T(8,128)(2,1)S(1)}, bf16[640,256]{1,0:T(8,128)(2,1)S(1)}, u32[]{:S(2)}, u32[]{:S(2)}) collective-permute-start(bf16[640,256]{1,0:T(8,128)(2,1)S(1)} %get-tuple-element.67), channel_id=1, source_target_pairs={{0,16},{16,32},{32,48},{48,64},{64,80},{80,96},{96,112},{112,128},... | collective-permute-start | bytes 983048 | tf_op jit(solution)/shard_map/ppermute | solution.py:378
  28.6 36.3 %collective-permute-start.10 = (bf16[768,256]{1,0:T(8,128)(2,1)S(1)}, bf16[768,256]{1,0:T(8,128)(2,1)S(1)}, u32[]{:S(2)}, u32[]{:S(2)}) collective-permute-start(bf16[768,256]{1,0:T(8,128)(2,1)S(1)} %get-tuple-element.66), channel_id=1, source_target_pairs={{0,16},{16,32},{32,48},{48,64},{64,80},{80,96},{96,112},{112,128},... | collective-permute-start | bytes 1179656 | tf_op jit(solution)/shard_map/ppermute | solution.py:378
  30.2 41.1 %collective-permute-start.15 = (bf16[640,256]{1,0:T(8,128)(2,1)S(1)}, bf16[640,256]{1,0:T(8,128)(2,1)S(1)}, u32[]{:S(2)}, u32[]{:S(2)}) collective-permute-start(bf16[640,256]{1,0:T(8,128)(2,1)S(1)} %get-tuple-element.73), channel_id=1, source_target_pairs={{16,0},{32,16},{48,32},{64,48},{80,64},{96,80},{112,96},{128,112},... | collective-permute-start | bytes 983048 | tf_op jit(solution)/shard_map/ppermute | solution.py:378
  35.6 35.7 %collective-permute-start.16 = (bf16[640,256]{1,0:T(8,128)(2,1)S(1)}, bf16[640,256]{1,0:T(8,128)(2,1)S(1)}, u32[]{:S(2)}, u32[]{:S(2)}) collective-permute-start(bf16[640,256]{1,0:T(8,128)(2,1)S(1)} %get-tuple-element.74), channel_id=1, source_target_pairs={{16,0},{32,16},{48,32},{64,48},{80,64},{96,80},{112,96},{128,112},... | collective-permute-start | bytes 983048 | tf_op jit(solution)/shard_map/ppermute | solution.py:378
  41.0 31.4 %collective-permute-start.13 = (bf16[384,256]{1,0:T(8,128)(2,1)S(1)}, bf16[384,256]{1,0:T(8,128)(2,1)S(1)}, u32[]{:S(2)}, u32[]{:S(2)}) collective-permute-start(bf16[384,256]{1,0:T(8,128)(2,1)S(1)} %get-tuple-element.71), channel_id=1, source_target_pairs={{1,2},{2,1},{3,4},{4,3},{5,6},{6,5},{7,8},{8,7},{9,10},{10,9},{11,... | collective-permute-start | bytes 589832 | tf_op jit(solution)/shard_map/ppermute | solution.py:370
  43.0 29.4 %collective-permute-start.14 = (bf16[384,256]{1,0:T(8,128)(2,1)S(1)}, bf16[384,256]{1,0:T(8,128)(2,1)S(1)}, u32[]{:S(2)}, u32[]{:S(2)}) collective-permute-start(bf16[384,256]{1,0:T(8,128)(2,1)S(1)} %get-tuple-element.72), channel_id=1, source_target_pairs={{0,1},{1,0},{2,3},{3,2},{4,5},{5,4},{6,7},{7,6},{8,9},{9,8},{10,11... | collective-permute-start | bytes 589832 | tf_op jit(solution)/shard_map/ppermute | solution.py:369
  71.9 5.7 %collective-permute-start.17 = (bf16[16,128]{1,0:T(8,128)(2,1)S(1)}, bf16[16,128]{1,0:T(8,128)(2,1)S(1)}, u32[]{:S(2)}, u32[]{:S(2)}) collective-permute-start(bf16[16,128]{1,0:T(8,128)(2,1)S(1)} %signal.1), channel_id=1, source_target_pairs={{0,8},{1,9},{2,10},{3,11},{4,12},{5,13},{6,14},{7,15},{8,16},{9,17... | collective-permute-start | bytes 12296 | tf_op jit(solution)/shard_map/ppermute | solution.py:496
  78.9 52.0 %collective-permute-start.18 = (bf16[4,512,256]{2,1,0:T(8,128)(2,1)}, bf16[4,512,256]{2,1,0:T(8,128)(2,1)S(1)}, u32[]{:S(2)}, u32[]{:S(2)}) collective-permute-start(bf16[4,512,256]{2,1,0:T(8,128)(2,1)} %hold.1), channel_id=1, source_target_pairs={{0,240},{16,0},{32,16},{48,32},{64,48},{80,64},{96,80},{112,96},{1... | collective-permute-start | bytes 3145736 | tf_op jit(solution)/shard_map/ppermute | solution.py:378
  86.0 44.9 %copy-start.10 = (bf16[2,512,256]{2,1,0:T(8,128)(2,1)S(1)}, bf16[2,512,256]{2,1,0:T(8,128)(2,1)}, u32[]{:S(2)}) copy-start(bf16[2,512,256]{2,1,0:T(8,128)(2,1)} %copy-done.9) | copy-start | bytes 1572868
  86.0 2.9 %collective-permute-start = (bf16[2,8,144,256]{3,2,1,0:T(8,128)(2,1)S(1)}, bf16[2,8,144,256]{3,2,1,0:T(8,128)(2,1)S(1)}, u32[]{:S(2)}, u32[]{:S(2)}) collective-permute-start(bf16[2,8,144,256]{3,2,1,0:T(8,128)(2,1)S(1)} %get-tuple-element.11), channel_id=1, source_target_pairs={{0,1},{1,0},{2,3},{3,2},{4,5},{5,4},{6,7},{7,6},{8,9},{9,8},{10,11... | collective-permute-start | bytes 3538952 | tf_op jit(solution)/shard_map/cond/branch_1_fun/ppermute | solution.py:517
  86.1 28.5 %collective-permute-start.5 = (bf16[2,512,256]{2,1,0:T(8,128)(2,1)}, bf16[2,512,256]{2,1,0:T(8,128)(2,1)S(1)}, u32[]{:S(2)}, u32[]{:S(2)}) collective-permute-start(bf16[2,512,256]{2,1,0:T(8,128)(2,1)} %get-tuple-element.18), channel_id=1, source_target_pairs={{0,16},{16,32},{32,48},{48,64},{64,80},{80,96},{96,112},{112,128},... | collective-permute-start | bytes 1572872 | tf_op jit(solution)/shard_map/cond/branch_1_fun/ppermute | solution.py:378
  89.7 11.7 %collective-permute-start.1 = (bf16[2,2,144,256]{3,2,1,0:T(8,128)(2,1)S(1)}, bf16[2,2,144,256]{3,2,1,0:T(8,128)(2,1)S(1)}, u32[]{:S(2)}, u32[]{:S(2)}) collective-permute-start(bf16[2,2,144,256]{3,2,1,0:T(8,128)(2,1)S(1)} %get-tuple-element.13), channel_id=1, source_target_pairs={{0,4},{1,5},{2,6},{3,7},{4,0},{5,1},{6,2},{7,3},{8,12},{9,13},{10,... | collective-permute-start | bytes 884744 | tf_op jit(solution)/shard_map/cond/branch_1_fun/ppermute | solution.py:511
  92.3 16.1 %collective-permute-start.2 = (bf16[2,2,144,256]{3,2,1,0:T(8,128)(2,1)S(1)}, bf16[2,2,144,256]{3,2,1,0:T(8,128)(2,1)S(1)}, u32[]{:S(2)}, u32[]{:S(2)}) collective-permute-start(bf16[2,2,144,256]{3,2,1,0:T(8,128)(2,1)S(1)} %get-tuple-element.14), channel_id=1, source_target_pairs={{0,2},{1,3},{2,4},{3,5},{4,6},{5,7},{6,0},{7,1},{8,10},{9,11},{10,... | collective-permute-start | bytes 884744 | tf_op jit(solution)/shard_map/cond/branch_1_fun/ppermute | solution.py:511
  93.1 15.4 %collective-permute-start.3 = (bf16[2,2,144,256]{3,2,1,0:T(8,128)(2,1)S(1)}, bf16[2,2,144,256]{3,2,1,0:T(8,128)(2,1)S(1)}, u32[]{:S(2)}, u32[]{:S(2)}) collective-permute-start(bf16[2,2,144,256]{3,2,1,0:T(8,128)(2,1)S(1)} %get-tuple-element.15), channel_id=1, source_target_pairs={{0,6},{1,7},{2,0},{3,1},{4,2},{5,3},{6,4},{7,5},{8,14},{9,15},{10,... | collective-permute-start | bytes 884744 | tf_op jit(solution)/shard_map/cond/branch_1_fun/ppermute | solution.py:511
  109.1 21.7 %collective-permute-start.4 = (bf16[2,144,256]{2,1,0:T(8,128)(2,1)S(1)}, bf16[2,144,256]{2,1,0:T(8,128)(2,1)S(1)}, u32[]{:S(2)}, u32[]{:S(2)}) collective-permute-start(bf16[2,144,256]{2,1,0:T(8,128)(2,1)S(1)} %get-tuple-element.17), channel_id=1, source_target_pairs={{0,8},{1,9},{2,10},{3,11},{4,12},{5,13},{6,14},{7,15},{8,0},{9,1},... | collective-permute-start | bytes 442376 | tf_op jit(solution)/shard_map/cond/branch_1_fun/ppermute | solution.py:526
  (8 other events, 9.0 us)
